TPU v7x, 512 devices: a whole 4x8x8 slice. The times are simulated.
512 devices in a mesh: row: 64 (over z, y), col: 8 (over x, core).
Axes of the slice: x: 4, y: 8, z: 8, core: 2. Of those that a mesh axis runs over, the one named last changes fastest.
Arguments:
- matrix: float32 [1, 8192, 8, 1024], P(None, 'row', None, 'col'), may hold values from -8 to 8, as said below
Outputs:
- reduced: float32 [1, 8192, 8, 1024], P(None, 'row', None, 'col')
Inputs may be any that keep to these rules, and one draw needn't show every extreme that they name: matrix holds a symmetric matrix.
All inputs are finite; a program needn't handle non-finite values.
Results may differ from a plain program's by a relative error of at most 0.0003.
Values sent between devices are 32-bit elements; how exact they have to be, the bound alone decides.
No kernel may reach another device: no remote copies, remote signals or barrier semaphores. Data moves between devices by JAX's collectives and lax.ppermute only.
A program may use at most 64 MiB of HBM per device.

v0:
```python
import jax
import jax.numpy as jnp
from jax import lax
from jax.sharding import PartitionSpec as P


def from_root(shard, axis, root):
    mine = lax.axis_index(axis) == root
    return lax.psum(jnp.where(mine, shard, jnp.zeros_like(shard)), axis)


def product(left, right, contract):
    return lax.dot_general(
        left,
        right,
        (contract, ((), ())),
        precision=lax.Precision.HIGHEST,
        preferred_element_type=jnp.float32,
    )


def selector(tiles, width):
    identity = jnp.eye(width, dtype=jnp.float32)
    marks = (tiles == 1).astype(jnp.float32)
    return (identity[:, None, :] * marks[None, :, None]).reshape(width, tiles.shape[0] * width)


def per_device(matrix):
    row_count_tiles, width, col_count_tiles, _ = matrix.shape
    row_size = lax.axis_size("row")
    col_size = lax.axis_size("col")
    row_index = lax.axis_index("row")
    col_index = lax.axis_index("col")
    local = matrix.reshape(row_count_tiles * width, col_count_tiles * width)
    row_tiles = jnp.arange(row_count_tiles, dtype=jnp.int32) * row_size + row_index
    col_tiles = jnp.arange(col_count_tiles, dtype=jnp.int32) * col_size + col_index
    identity = jnp.eye(width, dtype=jnp.float32)
    panel = from_root(matrix[:, :, 0, :], "col", 0)
    kept = panel * (row_tiles != 0).astype(jnp.float32)[:, None, None]
    head_part = jnp.sum(panel * (row_tiles == 1).astype(jnp.float32)[:, None, None], axis=0)
    flat = kept.reshape(row_count_tiles * width, width)
    gram_part = product(flat, flat, ((0,), (0,)))
    gram, head = lax.psum((gram_part, head_part), "row")
    lower = jnp.linalg.cholesky(gram)
    basis_rows = jax.scipy.linalg.solve_triangular(lower, flat.T, lower=True)
    top_trans = jax.scipy.linalg.solve_triangular(lower, head.T, lower=True)
    shifted = identity + top_trans
    normal = product(shifted, shifted, ((0,), (0,)))
    coupling = jax.scipy.linalg.cho_solve((jnp.linalg.cholesky(normal), True), shifted.T)
    refl_rows = basis_rows + selector(row_tiles, width)
    head_tiles = from_root(matrix[0], "row", 0).reshape(width, col_count_tiles * width)
    col_mask = jnp.repeat((col_tiles != 0).astype(jnp.float32), width)
    refl_cols = jax.scipy.linalg.solve_triangular(
        lower, head_tiles * col_mask[None, :], lower=True
    ) + selector(col_tiles, width)
    image_rows = lax.psum(product(refl_cols, local, ((1,), (1,))), "col")
    image_cols = lax.psum(product(refl_rows, local, ((1,), (0,))), "row")
    middle = lax.psum(product(refl_rows, image_rows, ((1,), (1,))), "row")
    sandwich = product(coupling, product(middle, coupling, ((1,), (0,))), ((0,), (0,)))
    upd_rows = product(coupling, image_rows, ((0,), (0,))) - 0.5 * product(
        sandwich, refl_rows, ((0,), (0,))
    )
    upd_cols = product(coupling, image_cols, ((0,), (0,))) - 0.5 * product(
        sandwich, refl_cols, ((0,), (0,))
    )
    result = (
        local
        - product(upd_rows, refl_cols, ((0,), (0,)))
        - product(refl_rows, upd_cols, ((0,), (0,)))
    )
    return result.reshape(matrix.shape)


def solution(mesh):
    in_specs = (P(None, "row", None, "col"),)
    out_specs = P(None, "row", None, "col")
    return jax.shard_map(
        per_device, mesh=mesh, in_specs=in_specs, out_specs=out_specs, check_vma=False
    )
```

profile of v0, /device:TPU:1, one launch (start us, length us, event | category | flops | bytes accessed | tf_op | source)
XLA Modules:
  0.0 535.7 jit_solution(2776642212452577276)
XLA Ops:
  6.5 1.7 broadcast_select_fusion
  8.3 0.0 all-reduce.13.cloned.1.call-start
  8.3 1.9 select_bitcast_fusion
  10.2 74.1 %all-reduce.7.cloned.1.call-done = f32[1,128,128]{2,1,0:T(8,128)} async-done(((f32[1,128,128]{2,1,0:T(8,128)}), f32[1,128,128]{2,1,0:T(8,128)}) %all-reduce.7.cloned.1.call-update) | async-done | bytes 65552 | tf_op jit(solution)/shard_map/psum | solution.py:9
  84.3 1.8 fusion.24
  86.1 0.0 all-reduce.13.cloned.1.call-update
  86.1 0.0 all-reduce.9.cloned.1.call-start
  86.2 0.1 broadcast_bitcast_fusion
  86.3 0.7 copy-done.1
  86.9 0.6 multiply_bitcast_fusion
  87.6 155.2 %all-reduce.13.cloned.1.call-done = (f32[128,128]{0,1:T(8,128)}, f32[128,8,128]{2,1,0:T(8,128)}) async-done(((f32[128,128]{0,1:T(8,128)}, f32[128,8,128]{2,1,0:T(8,128)}), (f32[128,128]{0,1:T(8,128)}, f32[128,8,128]{2,1,0:T(8,128)})) %all-reduce.13.cloned.1.call-update) | async-done | bytes 589840 | tf_op jit(solution)/shard_map/psum | solution.py:43
  242.8 1.0 copy.3
  243.8 0.9 fusion.23
  244.6 11.7 %cholesky.44 = f32[128,128]{1,0:T(8,128)S(1)} custom-call(f32[128,128]{1,0:T(8,128)S(1)} %fusion.23), custom_call_target="Cholesky" | custom-call | tf_op jit(solution)/shard_map/jit(cholesky)/cholesky | solution.py:44
  256.4 0.6 compare_reduce_fusion.1
  257.0 0.7 fusion.11
  257.7 9.8 %custom-call.17 = f32[1,128,128]{1,2,0:T(8,128)S(1)} custom-call(f32[1,128,128]{2,1,0:T(8,128)S(1)} %fusion.11), custom_call_target="InvertDiagBlocksLowerTriangular" | custom-call | tf_op jit(solution)/shard_map/jit(_solve_triangular)/triangular_solve/custom-call.0 | solution.py:46
  267.5 0.1 broadcast_multiply_fusion
  267.7 0.7 convolution_add_fusion
  268.4 0.4 copy-done
  268.7 1.2 fusion.7
  269.9 0.2 all-reduce.11.cloned.1.call-start
  270.2 0.3 convolution_add_fusion.1
  270.5 1.5 fusion.5
  271.9 67.9 %all-reduce.9.cloned.1.call-done = f32[128,128]{1,0:T(8,128)} async-done(((f32[128,128]{1,0:T(8,128)}), f32[128,128]{1,0:T(8,128)}) %all-reduce.9.cloned.1.call-update) | async-done | bytes 65552 | tf_op jit(solution)/shard_map/psum | solution.py:56
  339.9 1.7 fusion.36
  341.6 0.0 all-reduce.11.cloned.1.call-update
  341.6 157.3 %all-reduce.11.cloned.1.call-done = (f32[128,128]{0,1:T(8,128)}, f32[128,128]{1,0:T(8,128)}, f32[128,1024]{1,0:T(8,128)}) async-done(((f32[128,128]{0,1:T(8,128)}, f32[128,128]{1,0:T(8,128)}, f32[128,1024]{1,0:T(8,128)}), (f32[128,128]{0,1:T(8,128)}, f32[128,128]{1,0:T(8,128)}, f32[128,1024]{1,0:T(8,128)})) %all-reduce.11.cloned.1.call-update) | async-done | bytes 655376 | tf_op jit(solution)/shard_map/psum | solution.py:43
  498.9 1.1 convolution_add_fusion.2
  500.0 0.3 fusion.34
  500.3 0.1 copy.4
  500.4 11.7 %cholesky.55 = f32[128,128]{1,0:T(8,128)S(1)} custom-call(f32[128,128]{1,0:T(8,128)S(1)} %fusion.19), custom_call_target="Cholesky" | custom-call | tf_op jit(solution)/shard_map/jit(cholesky)/cholesky | solution.py:49
  512.1 0.6 compare_reduce_fusion
  512.8 0.7 fusion.12
  513.5 9.8 %custom-call.13 = f32[1,128,128]{1,2,0:T(8,128)S(1)} custom-call(f32[1,128,128]{2,1,0:T(8,128)S(1)} %fusion.12), custom_call_target="InvertDiagBlocksLowerTriangular" | custom-call | tf_op jit(solution)/shard_map/jit(_cho_solve)/triangular_solve | solution.py:49
  523.3 0.3 fusion.14
  523.6 0.2 fusion.17
  523.8 0.6 fusion.39
  524.4 0.2 copy-done.5
  524.6 0.2 fusion.37
  524.8 0.3 fusion.38
  525.1 0.5 copy-done.4
  525.7 0.3 fusion.35
  526.0 0.3 fusion.2
  526.3 0.6 fusion.1
  526.9 0.7 convolution_subtract_fusion.1
  527.6 0.6 fusion
  528.2 0.9 copy.9
  (17 shorter events, 0.2 us)
Async XLA Ops:
  6.5 77.7 %all-reduce.7.cloned.1.call-start = ((), (), s32[]{:S(2)}) async-start(), calls=%async_computation | async-start | bytes 131072 | tf_op jit(solution)/shard_map/psum | solution.py:9
  8.3 234.5 %all-reduce.13.cloned.1.call-start = ((), (), s32[]{:S(2)}) async-start(), calls=%async_computation.3 | async-start | bytes 1179648 | tf_op jit(solution)/shard_map/psum | solution.py:43
  86.1 0.8 copy-start.1
  86.1 253.7 %all-reduce.9.cloned.1.call-start = ((), (), s32[]{:S(2)}) async-start(), calls=%async_computation.1 | async-start | bytes 131072 | tf_op jit(solution)/shard_map/psum | solution.py:56
  242.8 24.7 %copy-start.3 = (f32[128,8,128]{2,1,0:T(8,128)S(1)}, f32[128,8,128]{2,1,0:T(8,128)}, u32[]{:S(2)}) copy-start(f32[128,8,128]{2,1,0:T(8,128)} %get-tuple-element.11) | copy-start | bytes 1572868
  267.7 1.0 copy-start
  269.9 228.9 %all-reduce.11.cloned.1.call-start = ((), (), s32[]{:S(2)}) async-start(), calls=%async_computation.2 | async-start | bytes 1310720 | tf_op jit(solution)/shard_map/psum | solution.py:43
  500.0 23.8 %copy-start.2 = (f32[128,1024]{1,0:T(8,128)S(1)}, f32[128,1024]{1,0:T(8,128)}, u32[]{:S(2)}) copy-start(f32[128,1024]{1,0:T(8,128)} %get-tuple-element.9) | copy-start | bytes 1572868
  523.8 0.8 copy-start.5
  524.8 0.8 copy-start.4
Sparse Core Ops, SparseCore 0:
  9.6 74.5 all-reduce.6
  87.6 155.1 all-reduce.12
  270.1 69.7 all-reduce.8
  343.3 155.5 all-reduce.10
where the time goes:
time: 540 us; the launch traced here: 536 us
  waiting for transfers between devices  455 us (84%)
  other arithmetic  50.9 us (9%)
  between operations  13.4 us (2%)
  matrix products  12.7 us (2%)
    psum x2, waiting for transfers between devices, per_device(): gram, head = lax.psum((gram_part, head_part), 'row')  312 us
    psum x1, waiting for transfers between devices, from_root(): return lax.psum(jnp.where(mine, shard, jnp.zeros_like(shard)), axis)  74.1 us
    psum x1, waiting for transfers between devices, per_device(): image_rows = lax.psum(product(refl_cols, local, ((1,), (1,))), 'col')  67.9 us
    another operation x3, other arithmetic, per_device(): lower = jnp.linalg.cholesky(gram)  12.4 us
    another operation x3, other arithmetic, per_device(): jnp.linalg.cholesky(normal)  12.4 us
  transfers between devices with their start and end apart: 4, of which 4 were waited for; matrix products, arithmetic and copies ran while one was open for 1% of the time, Pallas kernels for 0%

commit v1 on v0

v1 whole, which is shorter than its diff:
```python
import jax
import jax.numpy as jnp
from jax import lax
from jax.sharding import Mesh, PartitionSpec as P

COL = ("x", "k")
PLANE = ("y", "x", "k")


def product(left, right, contract):
    return lax.dot_general(
        left,
        right,
        (contract, ((), ())),
        precision=lax.Precision.HIGHEST,
        preferred_element_type=jnp.float32,
    )


def spread(block, axis, count):
    whole = jnp.broadcast_to(block[None], (count,) + block.shape)
    return lax.all_to_all(whole, axis, 0, 0, tiled=True)


def per_device(matrix):
    _, width, count, _ = matrix.shape
    side = lax.axis_size("y")
    row = lax.axis_index("z") * side + lax.axis_index("y")
    col = lax.axis_index(COL)
    swap = [(a * side + b, b * side + a) for a in range(side) for b in range(side)]
    piece = width // side
    identity = jnp.eye(width, dtype=jnp.float32)
    local = matrix[0]

    first = spread(local[:, 0, :], COL, side)
    panel_row = first[0] * (row != 0).astype(jnp.float32)
    next_row = first[1]
    panel_own = lax.ppermute(panel_row, PLANE, swap)
    next_own = lax.ppermute(next_row, PLANE, swap)
    panel = spread(panel_own, "z", count)

    part = product(local, panel, ((1, 2), (0, 1)))
    gram_part = product(panel, panel, ((0, 1), (0, 1)))
    both = jnp.concatenate([part, gram_part], axis=0)
    slots = jnp.concatenate(
        [
            jnp.broadcast_to(both[None], (side, 2 * width, width)),
            panel[0].reshape(side, piece, width),
        ],
        axis=1,
    )
    came = lax.all_to_all(slots, COL, 0, 0, tiled=True)
    head_slice = came[1, 2 * width :]
    total = jnp.sum(came[:, : 2 * width], axis=0)
    mixed_row, gram = total[:width], total[width:]
    mixed_own = lax.ppermute(mixed_row, PLANE, swap)

    lower = jnp.linalg.cholesky(gram)
    inverse = jax.scipy.linalg.solve_triangular(lower, identity, lower=True)
    image_own = product(mixed_own, inverse, ((1,), (1,))) + next_own
    image = spread(image_own, "z", count)

    at_col = ((jnp.arange(count) == 0) & (col == 1)).astype(jnp.float32)
    refl_row = product(panel_row, inverse, ((1,), (1,))) + identity * (row == 1)
    image_row = product(mixed_row, inverse, ((1,), (1,))) + next_row
    refl = product(panel, inverse, ((2,), (1,))) + identity[None] * at_col[:, None, None]

    middle_part = product(refl, image, ((0, 1), (0, 1)))
    came = spread(jnp.concatenate([middle_part, head_slice], axis=0), COL, side)
    middle = jnp.sum(came[:, :width], axis=0)
    head = came[:, width:].reshape(width, width)

    shifted = identity + product(inverse, head, ((1,), (1,)))
    normal = product(shifted, shifted, ((0,), (0,)))
    coupling = jax.scipy.linalg.cho_solve(
        (jnp.linalg.cholesky(normal), True), shifted.T
    )
    sandwich = product(coupling, product(middle, coupling, ((1,), (0,))), ((0,), (0,)))
    upd_row = product(image_row, coupling, ((1,), (0,))) - 0.5 * product(
        refl_row, sandwich, ((1,), (0,))
    )
    upd = product(image, coupling, ((2,), (0,))) - 0.5 * product(
        refl, sandwich, ((2,), (0,))
    )
    left = jnp.concatenate([upd_row, refl_row], axis=1)
    right = jnp.concatenate([refl, upd], axis=2)
    result = local - product(left, right, ((1,), (2,)))
    return result[None]


def solution(mesh):
    grid = Mesh(mesh.devices.reshape(8, 8, 4, 2), ("z", "y", "x", "k"))
    spec = P(None, ("z", "y"), None, COL)
    return jax.shard_map(
        per_device, mesh=grid, in_specs=(spec,), out_specs=spec, check_vma=False
    )
```

time: 540 us -> 184 us (0.34)
  waiting for transfers between devices: 455 us -> 50.1 us
  starting transfers between devices: 0.31 us -> 50.6 us
  blocking collectives: 0 us -> 20.2 us
  between operations: 13.4 us -> 0.37 us
    psum x4 -> x0, waiting for transfers between devices: 454 us -> none  [the longest x2 312 us: per_device(): gram, head = lax.psum((gram_part, head_part), 'row')]
    all_to_all x0 -> x4, waiting for transfers between devices: none -> 44.8 us  [the longest x3 31.8 us: spread(): return lax.all_to_all(whole, axis, 0, 0, tiled=True)]
    all_to_all x0 -> x4, starting transfers between devices: none -> 42.3 us  [the longest x3 30.2 us: spread(): return lax.all_to_all(whole, axis, 0, 0, tiled=True)]
    all_to_all x0 -> x1, blocking collectives: none -> 20.2 us  [spread(): return lax.all_to_all(whole, axis, 0, 0, tiled=True)]
    ppermute x0 -> x3, starting transfers between devices: none -> 8.29 us  [the longest x1 3.74 us: per_device(): mixed_own = lax.ppermute(mixed_row, PLANE, swap)]
  transfers between devices with their start and end apart: 4 -> 7, of which waited for: 4 -> 6; matrix products, arithmetic and copies ran while one was open for 1% -> 14% of each run, Pallas kernels for 0% -> 0%
where the time goes in v1:
time: 184 us; the launch traced here: 183 us
  starting transfers between devices  50.6 us (28%)
  waiting for transfers between devices  50.1 us (27%)
  other arithmetic  46.9 us (25%)
  blocking collectives  20.2 us (11%)
  matrix products  8.84 us (5%)
  local copies, waits for them, and re-layouts  5.9 us (3%)
    all_to_all x3, waiting for transfers between devices, spread(): return lax.all_to_all(whole, axis, 0, 0, tiled=True)  31.8 us
    all_to_all x3, starting transfers between devices, spread(): return lax.all_to_all(whole, axis, 0, 0, tiled=True)  30.2 us
    all_to_all x1, blocking collectives, spread(): return lax.all_to_all(whole, axis, 0, 0, tiled=True)  20.2 us
    all_to_all x1, waiting for transfers between devices, per_device(): came = lax.all_to_all(slots, COL, 0, 0, tiled=True)  13 us
    another operation x3, other arithmetic, per_device(): lower = jnp.linalg.cholesky(gram)  12.4 us
    another operation x3, other arithmetic, per_device(): jnp.linalg.cholesky(normal)  12.4 us
    all_to_all x1, starting transfers between devices, per_device(): came = lax.all_to_all(slots, COL, 0, 0, tiled=True)  12.1 us
    another operation x2, other arithmetic, per_device(): jax.scipy.linalg.cho_solve((jnp.linalg.cholesky(normal), True), shifted.T)  10.5 us
  transfers between devices with their start and end apart: 7, of which 6 were waited for; matrix products, arithmetic and copies ran while one was open for 14% of the time, Pallas kernels for 0%

profile of v1, /device:TPU:1, one launch (start us, length us, event | category | flops | bytes accessed | tf_op | source)
XLA Modules:
  0.0 183.0 jit_solution(5293331838943757057)
XLA Ops:
  0.0 1.1 copy.48
  1.2 0.8 broadcast_in_dim.16
  2.0 10.2 %all-to-all-start = ((f32[8,128,128]{2,1,0:T(8,128)}), f32[8,128,128]{2,1,0:T(8,128)S(1)}, u32[]{:S(2)}, u32[]{:S(2)}) async-start(f32[8,128,128]{2,1,0:T(8,128)} %broadcast_in_dim.16), calls=%async_computation | async-start | bytes 1048576 | tf_op jit(solution)/shard_map/all_to_all | solution.py:22
  12.2 9.4 %all-to-all-done = f32[8,128,128]{2,1,0:T(8,128)S(1)} async-done(((f32[8,128,128]{2,1,0:T(8,128)}), f32[8,128,128]{2,1,0:T(8,128)S(1)}, u32[]{:S(2)}, u32[]{:S(2)}) %all-to-all-start) | async-done | bytes 524320 | tf_op jit(solution)/shard_map/all_to_all | solution.py:22
  21.6 1.9 %collective-permute-start = (f32[128,128]{1,0:T(8,128)S(1)}, f32[128,128]{1,0:T(8,128)S(1)}, u32[]{:S(2)}, u32[]{:S(2)}) collective-permute-start(f32[128,128]{1,0:T(8,128)S(1)} %get-tuple-element.8), channel_id=1, source_target_pairs={{0,0},{1,8},{2,16},{3,24},{4,32},{5,40},{6,48},{7,56},{8,1},{9,9},... | collective-permute-start | bytes 196616 | tf_op jit(solution)/shard_map/ppermute | solution.py:38
  23.5 3.7 %collective-permute-done = f32[128,128]{1,0:T(8,128)S(1)} collective-permute-done((f32[128,128]{1,0:T(8,128)S(1)}, f32[128,128]{1,0:T(8,128)S(1)}, u32[]{:S(2)}, u32[]{:S(2)}) %collective-permute-start) | collective-permute-done | bytes 65568 | tf_op jit(solution)/shard_map/ppermute | solution.py:38
  27.3 20.2 %all_to_all.25 = f32[8,128,128]{2,1,0:T(8,128)S(1)} all-to-all(f32[8,128,128]{2,1,0:T(8,128)S(1)} %broadcast_in_dim.17), channel_id=1, replica_groups=mesh['z'=8,'y'=8,'x'=4,'k'=2] {'z'}, dimensions={0} | all-to-all | bytes 1048576 | tf_op jit(solution)/shard_map/all_to_all | solution.py:22
  47.4 1.0 convolution_bitcast_fusion.1
  48.4 0.7 convolution_bitcast_fusion.2
  49.3 0.8 slice-done
  50.0 1.1 pad_maximum_fusion
  51.1 12.1 %all-to-all-start.2 = ((f32[8,272,128]{2,1,0:T(8,128)}), f32[8,272,128]{2,1,0:T(8,128)S(1)}, u32[]{:S(2)}, u32[]{:S(2)}) async-start(f32[8,272,128]{2,1,0:T(8,128)} %pad_maximum_fusion), calls=%async_computation.2 | async-start | bytes 2228224 | tf_op jit(solution)/shard_map/all_to_all | solution.py:52
  63.2 2.6 %collective-permute-start.2 = (f32[128,128]{1,0:T(8,128)S(1)}, f32[128,128]{1,0:T(8,128)S(1)}, u32[]{:S(2)}, u32[]{:S(2)}) collective-permute-start(f32[128,128]{1,0:T(8,128)S(1)} %get-tuple-element.6), channel_id=1, source_target_pairs={{0,0},{1,8},{2,16},{3,24},{4,32},{5,40},{6,48},{7,56},{8,1},{9,9},... | collective-permute-start | bytes 196616 | tf_op jit(solution)/shard_map/ppermute | solution.py:39
  65.8 13.0 %all-to-all-done.2 = f32[8,272,128]{2,1,0:T(8,128)S(1)} async-done(((f32[8,272,128]{2,1,0:T(8,128)}), f32[8,272,128]{2,1,0:T(8,128)S(1)}, u32[]{:S(2)}, u32[]{:S(2)}) %all-to-all-start.2) | async-done | bytes 1114144 | tf_op jit(solution)/shard_map/all_to_all | solution.py:52
  79.1 11.7 %cholesky.44 = f32[128,128]{1,0:T(8,128)S(1)} custom-call(f32[128,128]{1,0:T(8,128)S(1)} %get-tuple-element.10), custom_call_target="Cholesky" | custom-call | tf_op jit(solution)/shard_map/jit(cholesky)/cholesky | solution.py:58
  90.8 0.7 compare_reduce_fusion.1
  91.5 0.6 fusion.7
  92.1 9.8 %custom-call.11 = f32[1,128,128]{1,2,0:T(8,128)S(1)} custom-call(f32[1,128,128]{2,1,0:T(8,128)S(1)} %fusion.7), custom_call_target="InvertDiagBlocksLowerTriangular" | custom-call | tf_op jit(solution)/shard_map/jit(_solve_triangular)/triangular_solve/custom-call.0 | solution.py:59
  102.0 3.7 %collective-permute-start.1 = (f32[128,128]{1,0:T(8,128)S(1)}, f32[128,128]{1,0:T(8,128)S(1)}, u32[]{:S(2)}, u32[]{:S(2)}) collective-permute-start(f32[128,128]{1,0:T(8,128)S(1)} %get-tuple-element.9), channel_id=1, source_target_pairs={{0,0},{1,8},{2,16},{3,24},{4,32},{5,40},{6,48},{7,56},{8,1},{9,9},... | collective-permute-start | bytes 196616 | tf_op jit(solution)/shard_map/ppermute | solution.py:56
  105.7 0.3 fusion.18
  106.0 1.7 collective-permute-done.1
  107.7 0.3 convolution_add_fusion.2
  107.9 0.8 broadcast_in_dim.19
  108.8 3.5 %all-to-all-start.3 = ((f32[8,128,128]{2,1,0:T(8,128)}), f32[8,128,128]{2,1,0:T(8,128)S(1)}, u32[]{:S(2)}, u32[]{:S(2)}) async-start(f32[8,128,128]{2,1,0:T(8,128)} %broadcast_in_dim.19), calls=%async_computation.3 | async-start | bytes 1048576 | tf_op jit(solution)/shard_map/all_to_all | solution.py:22
  112.4 0.6 convolution_add_fusion
  113.0 13.7 %all-to-all-done.3 = f32[8,128,128]{2,1,0:T(8,128)S(1)} async-done(((f32[8,128,128]{2,1,0:T(8,128)}), f32[8,128,128]{2,1,0:T(8,128)S(1)}, u32[]{:S(2)}, u32[]{:S(2)}) %all-to-all-start.3) | async-done | bytes 524320 | tf_op jit(solution)/shard_map/all_to_all | solution.py:22
  126.8 0.6 convolution_bitcast_fusion
  127.4 0.8 broadcast_in_dim.20
  128.3 16.5 %all-to-all-start.4 = ((f32[8,144,128]{2,1,0:T(8,128)}), f32[8,144,128]{2,1,0:T(8,128)S(1)}, u32[]{:S(2)}, u32[]{:S(2)}) async-start(f32[8,144,128]{2,1,0:T(8,128)} %broadcast_in_dim.20), calls=%async_computation.4 | async-start | bytes 1179648 | tf_op jit(solution)/shard_map/all_to_all | solution.py:22
  144.7 0.3 convolution_add_fusion.1
  145.0 1.1 convolution_add_fusion.3
  146.1 8.7 %all-to-all-done.4 = f32[8,144,128]{2,1,0:T(8,128)S(1)} async-done(((f32[8,144,128]{2,1,0:T(8,128)}), f32[8,144,128]{2,1,0:T(8,128)S(1)}, u32[]{:S(2)}, u32[]{:S(2)}) %all-to-all-start.4) | async-done | bytes 589856 | tf_op jit(solution)/shard_map/all_to_all | solution.py:22
  154.8 0.3 fusion.31
  155.1 0.3 fusion.24
  155.5 11.7 %cholesky.55 = f32[128,128]{1,0:T(8,128)S(1)} custom-call(f32[128,128]{1,0:T(8,128)S(1)} %fusion.16), custom_call_target="Cholesky" | custom-call | tf_op jit(solution)/shard_map/jit(cholesky)/cholesky | solution.py:76
  167.2 0.6 compare_reduce_fusion
  167.9 0.7 fusion.8
  168.5 9.8 %custom-call.9 = f32[1,128,128]{1,2,0:T(8,128)S(1)} custom-call(f32[1,128,128]{2,1,0:T(8,128)S(1)} %fusion.8), custom_call_target="InvertDiagBlocksLowerTriangular" | custom-call | tf_op jit(solution)/shard_map/jit(_cho_solve)/triangular_solve | solution.py:75
  178.3 0.3 fusion.12
  178.6 0.2 fusion.14
  178.9 0.2 fusion.32
  179.1 0.2 fusion.33
  179.3 0.3 fusion.34
  179.6 0.6 convolution_multiply_fusion
  180.2 0.2 fusion.1
  180.4 0.6 convolution_subtract_fusion.1
  181.1 0.8 fusion
  181.9 1.1 copy.32
  (30 shorter events, 0.6 us)
Async XLA Ops:
  2.0 19.6 %all-to-all-start = ((f32[8,128,128]{2,1,0:T(8,128)}), f32[8,128,128]{2,1,0:T(8,128)S(1)}, u32[]{:S(2)}, u32[]{:S(2)}) async-start(f32[8,128,128]{2,1,0:T(8,128)} %broadcast_in_dim.16), calls=%async_computation | async-start | bytes 1048576 | tf_op jit(solution)/shard_map/all_to_all | solution.py:22
  21.6 5.6 %copy-start.3 = (f32[8,128,128]{2,1,0:T(8,128)}, f32[8,128,128]{2,1,0:T(8,128)S(1)}, u32[]{:S(2)}) copy-start(f32[8,128,128]{2,1,0:T(8,128)S(1)} %all-to-all-done) | copy-start | bytes 1572868
  21.6 5.6 %collective-permute-start = (f32[128,128]{1,0:T(8,128)S(1)}, f32[128,128]{1,0:T(8,128)S(1)}, u32[]{:S(2)}, u32[]{:S(2)}) collective-permute-start(f32[128,128]{1,0:T(8,128)S(1)} %get-tuple-element.8), channel_id=1, source_target_pairs={{0,0},{1,8},{2,16},{3,24},{4,32},{5,40},{6,48},{7,56},{8,1},{9,9},... | collective-permute-start | bytes 196616 | tf_op jit(solution)/shard_map/ppermute | solution.py:38
  27.2 21.2 %copy-start.2 = (f32[1,128,8,128]{3,2,1,0:T(8,128)S(1)}, f32[1,128,8,128]{3,2,1,0:T(8,128)}, u32[]{:S(2)}) copy-start(f32[1,128,8,128]{3,2,1,0:T(8,128)} %param.4) | copy-start | bytes 1572868
  47.4 1.7 copy-start
  49.2 0.8 slice-start
  51.1 27.8 %all-to-all-start.2 = ((f32[8,272,128]{2,1,0:T(8,128)}), f32[8,272,128]{2,1,0:T(8,128)S(1)}, u32[]{:S(2)}, u32[]{:S(2)}) async-start(f32[8,272,128]{2,1,0:T(8,128)} %pad_maximum_fusion), calls=%async_computation.2 | async-start | bytes 2228224 | tf_op jit(solution)/shard_map/all_to_all | solution.py:52
  63.2 42.8 %collective-permute-start.2 = (f32[128,128]{1,0:T(8,128)S(1)}, f32[128,128]{1,0:T(8,128)S(1)}, u32[]{:S(2)}, u32[]{:S(2)}) collective-permute-start(f32[128,128]{1,0:T(8,128)S(1)} %get-tuple-element.6), channel_id=1, source_target_pairs={{0,0},{1,8},{2,16},{3,24},{4,32},{5,40},{6,48},{7,56},{8,1},{9,9},... | collective-permute-start | bytes 196616 | tf_op jit(solution)/shard_map/ppermute | solution.py:39
  101.9 10.5 %copy-start.1 = (f32[8,128,128]{2,1,0:T(8,128)S(1)}, f32[8,128,128]{2,1,0:T(8,128)}, u32[]{:S(2)}) copy-start(f32[8,128,128]{2,1,0:T(8,128)} %copy-done) | copy-start | bytes 1572868
  102.0 5.7 %collective-permute-start.1 = (f32[128,128]{1,0:T(8,128)S(1)}, f32[128,128]{1,0:T(8,128)S(1)}, u32[]{:S(2)}, u32[]{:S(2)}) collective-permute-start(f32[128,128]{1,0:T(8,128)S(1)} %get-tuple-element.9), channel_id=1, source_target_pairs={{0,0},{1,8},{2,16},{3,24},{4,32},{5,40},{6,48},{7,56},{8,1},{9,9},... | collective-permute-start | bytes 196616 | tf_op jit(solution)/shard_map/ppermute | solution.py:56
  108.8 18.0 %all-to-all-start.3 = ((f32[8,128,128]{2,1,0:T(8,128)}), f32[8,128,128]{2,1,0:T(8,128)S(1)}, u32[]{:S(2)}, u32[]{:S(2)}) async-start(f32[8,128,128]{2,1,0:T(8,128)} %broadcast_in_dim.19), calls=%async_computation.3 | async-start | bytes 1048576 | tf_op jit(solution)/shard_map/all_to_all | solution.py:22
  128.3 26.5 %all-to-all-start.4 = ((f32[8,144,128]{2,1,0:T(8,128)}), f32[8,144,128]{2,1,0:T(8,128)S(1)}, u32[]{:S(2)}, u32[]{:S(2)}) async-start(f32[8,144,128]{2,1,0:T(8,128)} %broadcast_in_dim.20), calls=%async_computation.4 | async-start | bytes 1179648 | tf_op jit(solution)/shard_map/all_to_all | solution.py:22

commit v2 on v1

v2 whole, which is shorter than its diff:
```python
import jax
import jax.numpy as jnp
from jax import lax
from jax.experimental import pallas as pl
from jax.experimental.pallas import tpu as pltpu
from jax.sharding import Mesh, PartitionSpec as P

COL = ("x", "k")
PLANE = ("y", "x", "k")
BLOCK = 8


def product(left, right, contract):
    return lax.dot_general(
        left,
        right,
        (contract, ((), ())),
        precision=lax.Precision.HIGHEST,
        preferred_element_type=jnp.float32,
    )


def spread(block, axis, count):
    whole = jnp.broadcast_to(block[None], (count,) + block.shape)
    return lax.all_to_all(whole, axis, 0, 0, tiled=True)


def unit(width):
    rows = lax.broadcasted_iota(jnp.int32, (width, width), 0)
    lanes = lax.broadcasted_iota(jnp.int32, (width, width), 1)
    return (rows == lanes).astype(jnp.float32)


def cholesky_kernel(upper_ref, corner_ref, out_ref, work):
    width = out_ref.shape[0]
    half, quarter = width // 2, width // 4
    work[:half, :width] = upper_ref[...]
    work[half : half + quarter, half:width] = corner_ref[:, :half]
    work[half + quarter :, half:width] = corner_ref[:, half:]
    work[half:, :half] = jnp.zeros((half, half), jnp.float32)
    work[:, width:] = unit(width)
    place = lax.broadcasted_iota(jnp.int32, (BLOCK, 1), 0)
    for low in range(0, width, BLOCK):
        rows = work[low : low + BLOCK, :]
        wide = (BLOCK, width)
        cols = [
            jnp.broadcast_to(rows[:, low + b : low + b + 1], wide) for b in range(BLOCK)
        ]
        for j in range(BLOCK):
            scale = lax.rsqrt(jnp.broadcast_to(cols[j][j : j + 1, :], wide))
            factor = jnp.where(place > j, cols[j] * scale, 0.0)
            for b in range(j + 1, BLOCK):
                pivot = jnp.broadcast_to(cols[b][j : j + 1, :], wide) * scale
                cols[b] = cols[b] - factor * pivot
            pivot = jnp.broadcast_to(rows[j : j + 1, :], rows.shape)
            pivot = pivot * jnp.concatenate([scale, scale], axis=1)
            factor = jnp.concatenate([factor, factor], axis=1)
            rows = jnp.where(place == j, pivot, rows - factor * pivot)
        out_ref[low : low + BLOCK, :] = rows[:, width:]
        if low + BLOCK < width:
            below = rows[:, low + BLOCK : width]
            work[low + BLOCK :, :] = work[low + BLOCK :, :] - product(
                below, rows, ((0,), (0,))
            )


def inverse_kernel(matrix_ref, out_ref, work):
    width = out_ref.shape[0]
    work[:, :width] = matrix_ref[...]
    work[:, width:] = unit(width)
    place = lax.broadcasted_iota(jnp.int32, (BLOCK, 1), 0)
    for low in range(0, width, BLOCK):
        rows = work[low : low + BLOCK, :]
        wide = (BLOCK, width)
        cols = [
            jnp.broadcast_to(rows[:, low + b : low + b + 1], wide) for b in range(BLOCK)
        ]
        for j in range(BLOCK):
            scale = 1.0 / jnp.broadcast_to(cols[j][j : j + 1, :], wide)
            factor = jnp.where(place != j, cols[j], 0.0)
            for b in range(j + 1, BLOCK):
                pivot = jnp.broadcast_to(cols[b][j : j + 1, :], wide) * scale
                cols[b] = jnp.where(place == j, pivot, cols[b] - factor * pivot)
            pivot = jnp.broadcast_to(rows[j : j + 1, :], rows.shape)
            pivot = pivot * jnp.concatenate([scale, scale], axis=1)
            factor = jnp.concatenate([factor, factor], axis=1)
            rows = jnp.where(place == j, pivot, rows - factor * pivot)
        own = unit(width)[:, low : low + BLOCK]
        work[...] = work[...] - product(
            work[:, low : low + BLOCK] - own, rows, ((1,), (0,))
        )
    out_ref[...] = work[:, width:]


def factor_call(kernel, *operands):
    width = operands[0].shape[1]
    return pl.pallas_call(
        kernel,
        out_shape=jax.ShapeDtypeStruct((width, width), jnp.float32),
        scratch_shapes=[pltpu.VMEM((width, 2 * width), jnp.float32)],
        cost_estimate=pl.CostEstimate(
            flops=0, bytes_accessed=30_000_000, transcendentals=0
        ),
        compiler_params=pltpu.CompilerParams(vmem_limit_bytes=4 << 20),
    )(*operands)


def per_device(matrix):
    _, width, count, _ = matrix.shape
    side = lax.axis_size("y")
    row = lax.axis_index("z") * side + lax.axis_index("y")
    col = lax.axis_index(COL)
    swap = [(a * side + b, b * side + a) for a in range(side) for b in range(side)]
    piece, half, quarter = width // side, width // 2, width // 4
    identity = jnp.eye(width, dtype=jnp.float32)
    local = matrix[0]

    first = spread(local[:, 0, :], COL, side)
    panel_row = first[0] * (row != 0).astype(jnp.float32)
    next_row = first[1]
    panel_own = lax.ppermute(panel_row, PLANE, swap)
    panel_own, next_row = lax.optimization_barrier((panel_own, next_row))
    next_own = lax.ppermute(next_row, PLANE, swap)
    panel = spread(panel_own, "z", count)

    part = product(local, panel, ((1, 2), (0, 1)))
    gram_part = product(panel, panel, ((0, 1), (0, 1)))
    shared = jnp.concatenate(
        [
            part,
            gram_part[:half],
            jnp.concatenate(
                [
                    gram_part[half : half + quarter, half:],
                    gram_part[half + quarter :, half:],
                ],
                axis=1,
            ),
        ],
        axis=0,
    )
    tall = shared.shape[0]
    slots = jnp.concatenate(
        [
            jnp.broadcast_to(shared[None], (side, tall, width)),
            panel[0].reshape(side, piece, width),
        ],
        axis=1,
    )
    came = lax.all_to_all(slots, COL, 0, 0, tiled=True)
    total = jnp.sum(came[:, :tall], axis=0)
    mixed_row = total[:width]
    mixed_own = lax.ppermute(mixed_row, PLANE, swap)
    head = spread(came[1, tall:], COL, side).reshape(width, width)
    inverse = factor_call(
        cholesky_kernel, total[width : width + half], total[width + half :]
    )

    image_own = product(mixed_own, inverse, ((1,), (1,))) + next_own
    image = spread(image_own, "z", count)

    coupling = factor_call(
        inverse_kernel, identity + product(inverse, head, ((1,), (1,)))
    )
    at_col = ((jnp.arange(count) == 0) & (col == 1)).astype(jnp.float32)
    refl_row = product(panel_row, inverse, ((1,), (1,))) + identity * (row == 1)
    image_row = product(mixed_row, inverse, ((1,), (1,))) + next_row
    refl = product(panel, inverse, ((2,), (1,))) + identity[None] * at_col[:, None, None]
    half_row = product(image_row, coupling, ((1,), (0,)))
    turned_row = product(refl_row, coupling, ((1,), (1,)))
    turned = product(refl, coupling, ((2,), (1,)))

    middle_part = product(refl, image, ((0, 1), (0, 1)))
    came = spread(middle_part, COL, side)
    half_col = product(image, coupling, ((2,), (0,)))
    left = jnp.concatenate([half_row, refl_row], axis=1)
    right = jnp.concatenate([refl, half_col], axis=2)
    partial = lax.optimization_barrier(local - product(left, right, ((1,), (2,))))

    middle = jnp.sum(came, axis=0)
    turned_row = product(turned_row, middle, ((1,), (0,)))
    result = partial + product(turned_row, turned, ((1,), (2,)))
    return result[None]


def solution(mesh):
    grid = Mesh(mesh.devices.reshape(8, 8, 4, 2), ("z", "y", "x", "k"))
    spec = P(None, ("z", "y"), None, COL)

    return jax.shard_map(
        per_device, mesh=grid, in_specs=(spec,), out_specs=spec, check_vma=False
    )
```

time: 184 us -> 142 us (0.77)
  other arithmetic: 46.9 us -> 1.19 us
  Pallas kernels: 0 us -> 15.9 us
  waiting for transfers between devices: 50.1 us -> 38.9 us
    another operation x10 -> x0, other arithmetic: 45.7 us -> none  [the longest x3 12.4 us: per_device(): lower = jnp.linalg.cholesky(gram)]
    pallas_call x0 -> x2, Pallas kernels: none -> 15.9 us  [factor_call(): pl.pallas_call(kernel, out_shape=jax.ShapeDtypeStruct((width, width), jnp...]
    all_to_all x3 -> x4, waiting for transfers between devices: 31.8 us -> 23.8 us  [spread(): return lax.all_to_all(whole, axis, 0, 0, tiled=True)]
    all_to_all x3 -> x4, starting transfers between devices: 30.2 us -> 31.3 us  [spread(): return lax.all_to_all(whole, axis, 0, 0, tiled=True)]
    dot_general x16 -> x15, matrix products: 8.07 us -> 7.67 us  [product(): lax.dot_general(left, right, (contract, ((), ())), precision=lax.Precisio...]
  transfers between devices with their start and end apart: 7 -> 8, of which waited for: 6 -> 5; matrix products, arithmetic and copies ran while one was open for 14% -> 4% of each run, Pallas kernels for 0% -> 11%
where the time goes in v2:
time: 142 us
  starting transfers between devices  50.7 us (36%)
  waiting for transfers between devices  38.9 us (27%)
  blocking collectives  19.9 us (14%)
  Pallas kernels  15.9 us (11%)
  matrix products  7.67 us (5%)
  local copies, waits for them, and re-layouts  7.12 us (5%)
    all_to_all x4, starting transfers between devices, spread(): return lax.all_to_all(whole, axis, 0, 0, tiled=True)  31.3 us
    all_to_all x4, waiting for transfers between devices, spread(): return lax.all_to_all(whole, axis, 0, 0, tiled=True)  23.8 us
    all_to_all x1, blocking collectives, spread(): return lax.all_to_all(whole, axis, 0, 0, tiled=True)  19.9 us
    pallas_call x2, Pallas kernels, factor_call(): pl.pallas_call(kernel, out_shape=jax.ShapeDtypeStruct((width, width), jnp...  15.9 us
    all_to_all x1, starting transfers between devices, per_device(): came = lax.all_to_all(slots, COL, 0, 0, tiled=True)  12.2 us
    all_to_all x1, waiting for transfers between devices, per_device(): came = lax.all_to_all(slots, COL, 0, 0, tiled=True)  11.5 us
    dot_general x15, matrix products, product(): lax.dot_general(left, right, (contract, ((), ())), precision=lax.Precisio...  7.67 us
    ppermute x1, waiting for transfers between devices, per_device(): panel_own = lax.ppermute(panel_row, PLANE, swap)  3.66 us
  transfers between devices with their start and end apart: 8, of which 5 were waited for; matrix products, arithmetic and copies ran while one was open for 4% of the time, Pallas kernels for 11%

profile of v2, /device:TPU:1, one launch (start us, length us, event | category | flops | bytes accessed | tf_op | source)
XLA Modules:
  0.0 141.7 jit_solution(16502169506012535660)
XLA Ops:
  0.0 1.1 copy.21
  1.2 0.8 broadcast_in_dim.19
  2.0 10.2 %all-to-all-start = ((f32[8,128,128]{2,1,0:T(8,128)}), f32[8,128,128]{2,1,0:T(8,128)S(1)}, u32[]{:S(2)}, u32[]{:S(2)}) async-start(f32[8,128,128]{2,1,0:T(8,128)} %broadcast_in_dim.19), calls=%async_computation | async-start | bytes 1048576 | tf_op jit(solution)/shard_map/all_to_all | solution.py:25
  12.2 9.4 %all-to-all-done = f32[8,128,128]{2,1,0:T(8,128)S(1)} async-done(((f32[8,128,128]{2,1,0:T(8,128)}), f32[8,128,128]{2,1,0:T(8,128)S(1)}, u32[]{:S(2)}, u32[]{:S(2)}) %all-to-all-start) | async-done | bytes 524320 | tf_op jit(solution)/shard_map/all_to_all | solution.py:25
  21.6 1.9 %collective-permute-start = (f32[128,128]{1,0:T(8,128)S(1)}, f32[128,128]{1,0:T(8,128)S(1)}, u32[]{:S(2)}, u32[]{:S(2)}) collective-permute-start(f32[128,128]{1,0:T(8,128)S(1)} %get-tuple-element.10), channel_id=1, source_target_pairs={{0,0},{1,8},{2,16},{3,24},{4,32},{5,40},{6,48},{7,56},{8,1},{9,9},... | collective-permute-start | bytes 196616 | tf_op jit(solution)/shard_map/ppermute | solution.py:121
  23.5 3.7 %collective-permute-done = f32[128,128]{1,0:T(8,128)S(1)} collective-permute-done((f32[128,128]{1,0:T(8,128)S(1)}, f32[128,128]{1,0:T(8,128)S(1)}, u32[]{:S(2)}, u32[]{:S(2)}) %collective-permute-start) | collective-permute-done | bytes 65568 | tf_op jit(solution)/shard_map/ppermute | solution.py:121
  27.2 19.9 %all_to_all.30 = f32[8,128,128]{2,1,0:T(8,128)S(1)} all-to-all(f32[8,128,128]{2,1,0:T(8,128)S(1)} %broadcast_in_dim.20), channel_id=1, replica_groups=mesh['z'=8,'y'=8,'x'=4,'k'=2] {'z'}, dimensions={0} | all-to-all | bytes 1048576 | tf_op jit(solution)/shard_map/all_to_all | solution.py:25
  47.2 1.0 convolution_bitcast_fusion.2
  48.2 0.6 copy-done.3
  48.8 0.1 fusion.15
  48.9 0.7 convolution_bitcast_fusion.3
  49.6 0.1 slice-done.1
  49.7 0.1 maximum_maximum_fusion
  49.7 0.1 broadcast_in_dim.21
  49.8 0.8 slice-done
  50.6 1.0 pad_maximum_fusion
  51.6 12.2 %all-to-all-start.2 = ((f32[8,240,128]{2,1,0:T(8,128)}), f32[8,240,128]{2,1,0:T(8,128)S(1)}, u32[]{:S(2)}, u32[]{:S(2)}) async-start(f32[8,240,128]{2,1,0:T(8,128)} %pad_maximum_fusion), calls=%async_computation.2 | async-start | bytes 1966080 | tf_op jit(solution)/shard_map/all_to_all | solution.py:150
  63.8 0.1 copy.11
  63.9 2.6 %collective-permute-start.2 = (f32[128,128]{1,0:T(8,128)S(1)}, f32[128,128]{1,0:T(8,128)S(1)}, u32[]{:S(2)}, u32[]{:S(2)}) collective-permute-start(f32[128,128]{1,0:T(8,128)S(1)} %get-tuple-element.8), channel_id=1, source_target_pairs={{0,0},{1,8},{2,16},{3,24},{4,32},{5,40},{6,48},{7,56},{8,1},{9,9},... | collective-permute-start | bytes 196616 | tf_op jit(solution)/shard_map/ppermute | solution.py:123
  66.6 11.5 %all-to-all-done.2 = f32[8,240,128]{2,1,0:T(8,128)S(1)} async-done(((f32[8,240,128]{2,1,0:T(8,128)}), f32[8,240,128]{2,1,0:T(8,128)S(1)}, u32[]{:S(2)}, u32[]{:S(2)}) %all-to-all-start.2) | async-done | bytes 983072 | tf_op jit(solution)/shard_map/all_to_all | solution.py:150
  78.1 0.0 copy-start.1
  78.2 0.6 broadcast_in_dim.23
  78.8 5.4 %all-to-all-start.3 = ((f32[8,16,128]{2,1,0:T(8,128)}), f32[8,16,128]{2,1,0:T(8,128)S(1)}, u32[]{:S(2)}, u32[]{:S(2)}) async-start(f32[8,16,128]{2,1,0:T(8,128)} %broadcast_in_dim.23), calls=%async_computation.3 | async-start | bytes 131072 | tf_op jit(solution)/shard_map/all_to_all | solution.py:25
  84.3 2.6 %collective-permute-start.1 = (f32[128,128]{1,0:T(8,128)S(1)}, f32[128,128]{1,0:T(8,128)S(1)}, u32[]{:S(2)}, u32[]{:S(2)}) collective-permute-start(f32[128,128]{1,0:T(8,128)S(1)} %slice.56), channel_id=1, source_target_pairs={{0,0},{1,8},{2,16},{3,24},{4,32},{5,40},{6,48},{7,56},{8,1},{9,9},... | collective-permute-start | bytes 196616 | tf_op jit(solution)/shard_map/ppermute | solution.py:153
  86.9 8.1 %shard_map.17 = f32[128,128]{1,0:T(8,128)S(1)} custom-call(f32[64,128]{1,0:T(8,128)S(1)} %slice.57.upper_ref, f32[32,128]{1,0:T(8,128)S(1)} %slice.58.corner_ref), custom_call_target="tpu_custom_call" | custom-call | bytes 30000000 | tf_op jit(solution)/shard_map/pallas_call | solution.py:97
  95.0 0.3 convolution_add_fusion.3
  95.3 0.6 convolution_add_fusion.1
  95.9 0.3 convolution_add_fusion.5
  96.2 0.0 collective-permute-done.2
  96.2 0.3 convolution_add_fusion.2
  96.4 0.0 all-to-all-done.3
  96.5 0.8 broadcast_in_dim.24
  97.3 3.7 %all-to-all-start.4 = ((f32[8,128,128]{2,1,0:T(8,128)}), f32[8,128,128]{2,1,0:T(8,128)S(1)}, u32[]{:S(2)}, u32[]{:S(2)}) async-start(f32[8,128,128]{2,1,0:T(8,128)} %broadcast_in_dim.24), calls=%async_computation.4 | async-start | bytes 1048576 | tf_op jit(solution)/shard_map/all_to_all | solution.py:25
  101.0 0.3 convolution_add_fusion.4.matrix_ref
  101.2 7.8 %shard_map.18 = f32[128,128]{1,0:T(8,128)S(1)} custom-call(f32[128,128]{1,0:T(8,128)S(1)} %convolution_add_fusion.4.matrix_ref), custom_call_target="tpu_custom_call" | custom-call | bytes 30000000 | tf_op jit(solution)/shard_map/pallas_call | solution.py:97
  109.1 0.2 fusion.16
  109.3 0.3 fusion.17
  109.5 1.0 fusion.7
  110.5 6.4 %all-to-all-done.4 = f32[8,128,128]{2,1,0:T(8,128)S(1)} async-done(((f32[8,128,128]{2,1,0:T(8,128)}), f32[8,128,128]{2,1,0:T(8,128)S(1)}, u32[]{:S(2)}, u32[]{:S(2)}) %all-to-all-start.4) | async-done | bytes 524320 | tf_op jit(solution)/shard_map/all_to_all | solution.py:25
  116.9 0.6 convolution_bitcast_fusion.1
  117.6 0.8 broadcast_in_dim.50
  118.4 12.0 %all-to-all-start.5 = ((f32[8,128,128]{2,1,0:T(8,128)}), f32[8,128,128]{2,1,0:T(8,128)S(1)}, u32[]{:S(2)}, u32[]{:S(2)}) async-start(f32[8,128,128]{2,1,0:T(8,128)} %broadcast_in_dim.50), calls=%async_computation.5 | async-start | bytes 1048576 | tf_op jit(solution)/shard_map/all_to_all | solution.py:25
  130.4 0.6 fusion.9
  131.0 0.8 convolution_subtract_fusion
  131.8 8.0 %all-to-all-done.5 = f32[8,128,128]{2,1,0:T(8,128)S(1)} async-done(((f32[8,128,128]{2,1,0:T(8,128)}), f32[8,128,128]{2,1,0:T(8,128)S(1)}, u32[]{:S(2)}, u32[]{:S(2)}) %all-to-all-start.5) | async-done | bytes 524320 | tf_op jit(solution)/shard_map/all_to_all | solution.py:25
  139.8 0.2 convolution_bitcast_fusion
  140.0 0.6 fusion
  140.6 1.1 copy.13
  (20 shorter events, 0.2 us)
Async XLA Ops:
  2.0 19.6 %all-to-all-start = ((f32[8,128,128]{2,1,0:T(8,128)}), f32[8,128,128]{2,1,0:T(8,128)S(1)}, u32[]{:S(2)}, u32[]{:S(2)}) async-start(f32[8,128,128]{2,1,0:T(8,128)} %broadcast_in_dim.19), calls=%async_computation | async-start | bytes 1048576 | tf_op jit(solution)/shard_map/all_to_all | solution.py:25
  21.6 5.6 %collective-permute-start = (f32[128,128]{1,0:T(8,128)S(1)}, f32[128,128]{1,0:T(8,128)S(1)}, u32[]{:S(2)}, u32[]{:S(2)}) collective-permute-start(f32[128,128]{1,0:T(8,128)S(1)} %get-tuple-element.10), channel_id=1, source_target_pairs={{0,0},{1,8},{2,16},{3,24},{4,32},{5,40},{6,48},{7,56},{8,1},{9,9},... | collective-permute-start | bytes 196616 | tf_op jit(solution)/shard_map/ppermute | solution.py:121
  47.2 2.6 %copy-start = (f32[8,128,128]{2,1,0:T(8,128)}, f32[8,128,128]{2,1,0:T(8,128)S(1)}, u32[]{:S(2)}) copy-start(f32[8,128,128]{2,1,0:T(8,128)S(1)} %all_to_all.30) | copy-start | bytes 1572868
  47.2 1.7 %copy-start.2 = (f32[1,128,8,128]{3,2,1,0:T(8,128)S(1)}, f32[1,128,8,128]{3,2,1,0:T(8,128)}, u32[]{:S(2)}) copy-start(f32[1,128,8,128]{3,2,1,0:T(8,128)} %param.1) | copy-start | bytes 1572868
  48.2 0.6 copy-start.3
  48.9 0.8 slice-start.1
  49.7 0.8 slice-start
  51.6 26.5 %all-to-all-start.2 = ((f32[8,240,128]{2,1,0:T(8,128)}), f32[8,240,128]{2,1,0:T(8,128)S(1)}, u32[]{:S(2)}, u32[]{:S(2)}) async-start(f32[8,240,128]{2,1,0:T(8,128)} %pad_maximum_fusion), calls=%async_computation.2 | async-start | bytes 1966080 | tf_op jit(solution)/shard_map/all_to_all | solution.py:150
  63.9 32.2 %collective-permute-start.2 = (f32[128,128]{1,0:T(8,128)S(1)}, f32[128,128]{1,0:T(8,128)S(1)}, u32[]{:S(2)}, u32[]{:S(2)}) collective-permute-start(f32[128,128]{1,0:T(8,128)S(1)} %get-tuple-element.8), channel_id=1, source_target_pairs={{0,0},{1,8},{2,16},{3,24},{4,32},{5,40},{6,48},{7,56},{8,1},{9,9},... | collective-permute-start | bytes 196616 | tf_op jit(solution)/shard_map/ppermute | solution.py:123
  78.1 17.1 %copy-start.1 = (f32[8,128,128]{2,1,0:T(8,128)S(1)}, f32[8,128,128]{2,1,0:T(8,128)}, u32[]{:S(2)}) copy-start(f32[8,128,128]{2,1,0:T(8,128)} %copy-done) | copy-start | bytes 1572868
  78.8 17.6 %all-to-all-start.3 = ((f32[8,16,128]{2,1,0:T(8,128)}), f32[8,16,128]{2,1,0:T(8,128)S(1)}, u32[]{:S(2)}, u32[]{:S(2)}) async-start(f32[8,16,128]{2,1,0:T(8,128)} %broadcast_in_dim.23), calls=%async_computation.3 | async-start | bytes 131072 | tf_op jit(solution)/shard_map/all_to_all | solution.py:25
  84.3 11.9 %collective-permute-start.1 = (f32[128,128]{1,0:T(8,128)S(1)}, f32[128,128]{1,0:T(8,128)S(1)}, u32[]{:S(2)}, u32[]{:S(2)}) collective-permute-start(f32[128,128]{1,0:T(8,128)S(1)} %slice.56), channel_id=1, source_target_pairs={{0,0},{1,8},{2,16},{3,24},{4,32},{5,40},{6,48},{7,56},{8,1},{9,9},... | collective-permute-start | bytes 196616 | tf_op jit(solution)/shard_map/ppermute | solution.py:153
  97.3 19.7 %all-to-all-start.4 = ((f32[8,128,128]{2,1,0:T(8,128)}), f32[8,128,128]{2,1,0:T(8,128)S(1)}, u32[]{:S(2)}, u32[]{:S(2)}) async-start(f32[8,128,128]{2,1,0:T(8,128)} %broadcast_in_dim.24), calls=%async_computation.4 | async-start | bytes 1048576 | tf_op jit(solution)/shard_map/all_to_all | solution.py:25
  118.4 21.3 %all-to-all-start.5 = ((f32[8,128,128]{2,1,0:T(8,128)}), f32[8,128,128]{2,1,0:T(8,128)S(1)}, u32[]{:S(2)}, u32[]{:S(2)}) async-start(f32[8,128,128]{2,1,0:T(8,128)} %broadcast_in_dim.50), calls=%async_computation.5 | async-start | bytes 1048576 | tf_op jit(solution)/shard_map/all_to_all | solution.py:25

commit v3 on v2

--- a/solution.py
+++ b/solution.py
@@ -108,20 +108,22 @@
 def per_device(matrix):
     _, width, count, _ = matrix.shape
     side = lax.axis_size("y")
-    row = lax.axis_index("z") * side + lax.axis_index("y")
+    depth = lax.axis_index("z")
+    row = depth * side + lax.axis_index("y")
     col = lax.axis_index(COL)
     swap = [(a * side + b, b * side + a) for a in range(side) for b in range(side)]
     piece, half, quarter = width // side, width // 2, width // 4
-    identity = jnp.eye(width, dtype=jnp.float32)
     local = matrix[0]
+
+    on_row = lax.optimization_barrier(unit(width) * (row == 1))
+    identity = unit(width)
 
     first = spread(local[:, 0, :], COL, side)
     panel_row = first[0] * (row != 0).astype(jnp.float32)
     next_row = first[1]
     panel_own = lax.ppermute(panel_row, PLANE, swap)
-    panel_own, next_row = lax.optimization_barrier((panel_own, next_row))
+    panel = spread(panel_own, "z", count)
     next_own = lax.ppermute(next_row, PLANE, swap)
-    panel = spread(panel_own, "z", count)
 
     part = product(local, panel, ((1, 2), (0, 1)))
     gram_part = product(panel, panel, ((0, 1), (0, 1)))
@@ -136,50 +138,45 @@
                 ],
                 axis=1,
             ),
+            lax.dynamic_slice_in_dim(panel[0], depth * piece, piece, 0),
         ],
         axis=0,
     )
-    tall = shared.shape[0]
-    slots = jnp.concatenate(
-        [
-            jnp.broadcast_to(shared[None], (side, tall, width)),
-            panel[0].reshape(side, piece, width),
-        ],
-        axis=1,
-    )
-    came = lax.all_to_all(slots, COL, 0, 0, tiled=True)
+    came = spread(shared, COL, side)
+    tall = shared.shape[0] - piece
     total = jnp.sum(came[:, :tall], axis=0)
+    head_slice = came[1, tall:]
     mixed_row = total[:width]
     mixed_own = lax.ppermute(mixed_row, PLANE, swap)
-    head = spread(came[1, tall:], COL, side).reshape(width, width)
     inverse = factor_call(
         cholesky_kernel, total[width : width + half], total[width + half :]
     )
 
     image_own = product(mixed_own, inverse, ((1,), (1,))) + next_own
-    image = spread(image_own, "z", count)
+    came = spread(jnp.concatenate([image_own, head_slice], axis=0), "z", count)
+    image = came[:, :width]
+    head = came[:, width:].reshape(width, width)
+
+    at_col = ((jnp.arange(count) == 0) & (col == 1)).astype(jnp.float32)
+    refl_row = product(panel_row, inverse, ((1,), (1,))) + on_row
+    image_row = product(mixed_row, inverse, ((1,), (1,))) + next_row
+    refl = product(panel, inverse, ((2,), (1,))) + identity[None] * at_col[:, None, None]
+
+    middle_part = product(refl, image, ((0, 1), (0, 1)))
+    came = spread(middle_part, COL, side)
 
     coupling = factor_call(
         inverse_kernel, identity + product(inverse, head, ((1,), (1,)))
     )
-    at_col = ((jnp.arange(count) == 0) & (col == 1)).astype(jnp.float32)
-    refl_row = product(panel_row, inverse, ((1,), (1,))) + identity * (row == 1)
-    image_row = product(mixed_row, inverse, ((1,), (1,))) + next_row
-    refl = product(panel, inverse, ((2,), (1,))) + identity[None] * at_col[:, None, None]
+    turned_row = product(refl_row, coupling, ((1,), (1,)))
     half_row = product(image_row, coupling, ((1,), (0,)))
-    turned_row = product(refl_row, coupling, ((1,), (1,)))
-    turned = product(refl, coupling, ((2,), (1,)))
-
-    middle_part = product(refl, image, ((0, 1), (0, 1)))
-    came = spread(middle_part, COL, side)
-    half_col = product(image, coupling, ((2,), (0,)))
-    left = jnp.concatenate([half_row, refl_row], axis=1)
-    right = jnp.concatenate([refl, half_col], axis=2)
-    partial = lax.optimization_barrier(local - product(left, right, ((1,), (2,))))
+    partial = lax.optimization_barrier(local - product(turned_row, image, ((1,), (2,))))
 
     middle = jnp.sum(came, axis=0)
-    turned_row = product(turned_row, middle, ((1,), (0,)))
-    result = partial + product(turned_row, turned, ((1,), (2,)))
+    sandwich_row = product(
+        product(turned_row, middle, ((1,), (0,))), coupling, ((1,), (0,))
+    )
+    result = partial - product(half_row - sandwich_row, refl, ((1,), (2,)))
     return result[None]
 
 

time: 142 us -> 140 us (0.986)
  blocking collectives: 19.9 us -> 0 us
  waiting for transfers between devices: 38.9 us -> 55.3 us
  starting transfers between devices: 50.7 us -> 54.3 us
    all_to_all x4 -> x5, waiting for transfers between devices: 23.8 us -> 51.7 us  [spread(): return lax.all_to_all(whole, axis, 0, 0, tiled=True)]
    all_to_all x1 -> x0, blocking collectives: 19.9 us -> none  [spread(): return lax.all_to_all(whole, axis, 0, 0, tiled=True)]
    all_to_all x4 -> x5, starting transfers between devices: 31.3 us -> 46.1 us  [spread(): return lax.all_to_all(whole, axis, 0, 0, tiled=True)]
    all_to_all x1 -> x0, starting transfers between devices: 12.2 us -> none  [per_device(): came = lax.all_to_all(slots, COL, 0, 0, tiled=True)]
    all_to_all x1 -> x0, waiting for transfers between devices: 11.5 us -> none  [per_device(): came = lax.all_to_all(slots, COL, 0, 0, tiled=True)]
    dot_general x15 -> x14, matrix products: 7.67 us -> 6.47 us  [product(): lax.dot_general(left, right, (contract, ((), ())), precision=lax.Precisio...]
    broadcast_in_dim x7 -> x6, local copies, waits for them, and re-layouts: 3.16 us -> 4.35 us  [spread(): whole = jnp.broadcast_to(block[None], (count,) + block.shape)]
  transfers between devices with their start and end apart: 8 -> 8, of which waited for: 5 -> 6; matrix products, arithmetic and copies ran while one was open for 4% -> 2% of each run, Pallas kernels for 11% -> 11%
where the time goes in v3:
time: 140 us
  waiting for transfers between devices  55.3 us (40%)
  starting transfers between devices  54.3 us (39%)
  Pallas kernels  15.9 us (11%)
  local copies, waits for them, and re-layouts  7.3 us (5%)
  matrix products  6.47 us (5%)
    all_to_all x5, waiting for transfers between devices, spread(): return lax.all_to_all(whole, axis, 0, 0, tiled=True)  51.7 us
    all_to_all x5, starting transfers between devices, spread(): return lax.all_to_all(whole, axis, 0, 0, tiled=True)  46.1 us
    pallas_call x2, Pallas kernels, factor_call(): pl.pallas_call(kernel, out_shape=jax.ShapeDtypeStruct((width, width), jnp...  15.9 us
    dot_general x14, matrix products, product(): lax.dot_general(left, right, (contract, ((), ())), precision=lax.Precisio...  6.47 us
    broadcast_in_dim x6, local copies, waits for them, and re-layouts, spread(): whole = jnp.broadcast_to(block[None], (count,) + block.shape)  4.35 us
    ppermute x1, waiting for transfers between devices, per_device(): panel_own = lax.ppermute(panel_row, PLANE, swap)  3.66 us
    ppermute x1, starting transfers between devices, per_device(): mixed_own = lax.ppermute(mixed_row, PLANE, swap)  3.61 us
  transfers between devices with their start and end apart: 8, of which 6 were waited for; matrix products, arithmetic and copies ran while one was open for 2% of the time, Pallas kernels for 11%

profile of v3, /device:TPU:1, one launch (start us, length us, event | category | flops | bytes accessed | tf_op | source)
XLA Modules:
  0.0 139.7 jit_solution(1349011497440832113)
XLA Ops:
  0.0 1.1 copy.13
  1.2 0.8 broadcast_in_dim.15
  2.0 10.2 %all-to-all-start = ((f32[8,128,128]{2,1,0:T(8,128)}), f32[8,128,128]{2,1,0:T(8,128)S(1)}, u32[]{:S(2)}, u32[]{:S(2)}) async-start(f32[8,128,128]{2,1,0:T(8,128)} %broadcast_in_dim.15), calls=%async_computation | async-start | bytes 1048576 | tf_op jit(solution)/shard_map/all_to_all | solution.py:25
  12.2 9.4 %all-to-all-done = f32[8,128,128]{2,1,0:T(8,128)S(1)} async-done(((f32[8,128,128]{2,1,0:T(8,128)}), f32[8,128,128]{2,1,0:T(8,128)S(1)}, u32[]{:S(2)}, u32[]{:S(2)}) %all-to-all-start) | async-done | bytes 524320 | tf_op jit(solution)/shard_map/all_to_all | solution.py:25
  21.6 1.9 %collective-permute-start = (f32[128,128]{1,0:T(8,128)S(1)}, f32[128,128]{1,0:T(8,128)S(1)}, u32[]{:S(2)}, u32[]{:S(2)}) collective-permute-start(f32[128,128]{1,0:T(8,128)S(1)} %get-tuple-element.6), channel_id=1, source_target_pairs={{0,0},{1,8},{2,16},{3,24},{4,32},{5,40},{6,48},{7,56},{8,1},{9,9},... | collective-permute-start | bytes 196616 | tf_op jit(solution)/shard_map/ppermute | solution.py:124
  23.5 3.7 %collective-permute-done = f32[128,128]{1,0:T(8,128)S(1)} collective-permute-done((f32[128,128]{1,0:T(8,128)S(1)}, f32[128,128]{1,0:T(8,128)S(1)}, u32[]{:S(2)}, u32[]{:S(2)}) %collective-permute-start) | collective-permute-done | bytes 65568 | tf_op jit(solution)/shard_map/ppermute | solution.py:124
  27.2 0.8 broadcast_in_dim.16
  28.0 6.0 %all-to-all-start.1 = ((f32[8,128,128]{2,1,0:T(8,128)}), f32[8,128,128]{2,1,0:T(8,128)S(1)}, u32[]{:S(2)}, u32[]{:S(2)}) async-start(f32[8,128,128]{2,1,0:T(8,128)} %broadcast_in_dim.16), calls=%async_computation.1 | async-start | bytes 1048576 | tf_op jit(solution)/shard_map/all_to_all | solution.py:25
  34.0 0.0 copy-start
  34.0 14.1 %all-to-all-done.1 = f32[8,128,128]{2,1,0:T(8,128)S(1)} async-done(((f32[8,128,128]{2,1,0:T(8,128)}), f32[8,128,128]{2,1,0:T(8,128)S(1)}, u32[]{:S(2)}, u32[]{:S(2)}) %all-to-all-start.1) | async-done | bytes 524320 | tf_op jit(solution)/shard_map/all_to_all | solution.py:25
  48.2 1.0 convolution_bitcast_fusion.1
  49.2 0.0 copy-start.1
  49.2 0.1 fusion.10
  49.3 0.5 copy-done.1
  49.8 0.0 copy-done
  49.8 0.0 slice-start
  49.8 0.7 convolution_bitcast_fusion.2
  50.5 0.0 slice-done
  50.6 0.1 pad_maximum_fusion
  50.7 1.0 broadcast_in_dim.17
  51.7 12.2 %all-to-all-start.2 = ((f32[8,240,128]{2,1,0:T(8,128)}), f32[8,240,128]{2,1,0:T(8,128)S(1)}, u32[]{:S(2)}, u32[]{:S(2)}) async-start(f32[8,240,128]{2,1,0:T(8,128)} %broadcast_in_dim.17), calls=%async_computation.2 | async-start | bytes 1966080 | tf_op jit(solution)/shard_map/all_to_all | solution.py:25
  63.9 2.6 %collective-permute-start.2 = (f32[128,128]{1,0:T(8,128)S(1)}, f32[128,128]{1,0:T(8,128)S(1)}, u32[]{:S(2)}, u32[]{:S(2)}) collective-permute-start(f32[128,128]{1,0:T(8,128)S(1)} %get-tuple-element.5), channel_id=1, source_target_pairs={{0,0},{1,8},{2,16},{3,24},{4,32},{5,40},{6,48},{7,56},{8,1},{9,9},... | collective-permute-start | bytes 196616 | tf_op jit(solution)/shard_map/ppermute | solution.py:126
  66.5 11.6 %all-to-all-done.2 = f32[8,240,128]{2,1,0:T(8,128)S(1)} async-done(((f32[8,240,128]{2,1,0:T(8,128)}), f32[8,240,128]{2,1,0:T(8,128)S(1)}, u32[]{:S(2)}, u32[]{:S(2)}) %all-to-all-start.2) | async-done | bytes 983072 | tf_op jit(solution)/shard_map/all_to_all | solution.py:25
  78.2 3.6 %collective-permute-start.1 = (f32[128,128]{1,0:T(8,128)S(1)}, f32[128,128]{1,0:T(8,128)S(1)}, u32[]{:S(2)}, u32[]{:S(2)}) collective-permute-start(f32[128,128]{1,0:T(8,128)S(1)} %slice.65), channel_id=1, source_target_pairs={{0,0},{1,8},{2,16},{3,24},{4,32},{5,40},{6,48},{7,56},{8,1},{9,9},... | collective-permute-start | bytes 196616 | tf_op jit(solution)/shard_map/ppermute | solution.py:150
  81.9 8.1 %shard_map.17 = f32[128,128]{1,0:T(8,128)S(1)} custom-call(f32[64,128]{1,0:T(8,128)S(1)} %slice.63.upper_ref, f32[32,128]{1,0:T(8,128)S(1)} %slice.64.corner_ref), custom_call_target="tpu_custom_call" | custom-call | bytes 30000000 | tf_op jit(solution)/shard_map/pallas_call | solution.py:97
  89.9 0.0 collective-permute-done.2
  90.0 0.0 collective-permute-done.1
  90.0 0.3 convolution_add_fusion.3
  90.2 0.9 broadcast_in_dim.18
  91.1 3.5 %all-to-all-start.3 = ((f32[8,144,128]{2,1,0:T(8,128)}), f32[8,144,128]{2,1,0:T(8,128)S(1)}, u32[]{:S(2)}, u32[]{:S(2)}) async-start(f32[8,144,128]{2,1,0:T(8,128)} %broadcast_in_dim.18), calls=%async_computation.3 | async-start | bytes 1179648 | tf_op jit(solution)/shard_map/all_to_all | solution.py:25
  94.7 0.3 convolution_add_fusion.4
  95.0 0.3 convolution_add_fusion.1
  95.2 0.6 convolution_add_fusion
  95.8 16.4 %all-to-all-done.3 = f32[8,144,128]{2,1,0:T(8,128)S(1)} async-done(((f32[8,144,128]{2,1,0:T(8,128)}), f32[8,144,128]{2,1,0:T(8,128)S(1)}, u32[]{:S(2)}, u32[]{:S(2)}) %all-to-all-start.3) | async-done | bytes 589856 | tf_op jit(solution)/shard_map/all_to_all | solution.py:25
  112.2 1.0 convolution_bitcast_fusion
  113.2 0.8 broadcast_in_dim.19
  114.0 14.1 %all-to-all-start.4 = ((f32[8,128,128]{2,1,0:T(8,128)}), f32[8,128,128]{2,1,0:T(8,128)S(1)}, u32[]{:S(2)}, u32[]{:S(2)}) async-start(f32[8,128,128]{2,1,0:T(8,128)} %broadcast_in_dim.19), calls=%async_computation.4 | async-start | bytes 1048576 | tf_op jit(solution)/shard_map/all_to_all | solution.py:25
  128.2 0.3 convolution_add_fusion.2.matrix_ref
  128.5 7.8 %shard_map.18 = f32[128,128]{1,0:T(8,128)S(1)} custom-call(f32[128,128]{1,0:T(8,128)S(1)} %convolution_add_fusion.2.matrix_ref), custom_call_target="tpu_custom_call" | custom-call | bytes 30000000 | tf_op jit(solution)/shard_map/pallas_call | solution.py:97
  136.3 0.3 fusion.11
  136.5 0.6 convolution_subtract_fusion.1
  137.2 0.2 fusion.12
  137.4 0.1 all-to-all-done.4
  137.6 0.2 fusion.13
  137.8 0.2 fusion.1
  138.0 0.6 fusion
  138.6 1.1 copy.7
  (15 shorter events, 0.2 us)
Async XLA Ops:
  2.0 19.6 %all-to-all-start = ((f32[8,128,128]{2,1,0:T(8,128)}), f32[8,128,128]{2,1,0:T(8,128)S(1)}, u32[]{:S(2)}, u32[]{:S(2)}) async-start(f32[8,128,128]{2,1,0:T(8,128)} %broadcast_in_dim.15), calls=%async_computation | async-start | bytes 1048576 | tf_op jit(solution)/shard_map/all_to_all | solution.py:25
  21.6 5.6 %collective-permute-start = (f32[128,128]{1,0:T(8,128)S(1)}, f32[128,128]{1,0:T(8,128)S(1)}, u32[]{:S(2)}, u32[]{:S(2)}) collective-permute-start(f32[128,128]{1,0:T(8,128)S(1)} %get-tuple-element.6), channel_id=1, source_target_pairs={{0,0},{1,8},{2,16},{3,24},{4,32},{5,40},{6,48},{7,56},{8,1},{9,9},... | collective-permute-start | bytes 196616 | tf_op jit(solution)/shard_map/ppermute | solution.py:124
  28.0 20.1 %all-to-all-start.1 = ((f32[8,128,128]{2,1,0:T(8,128)}), f32[8,128,128]{2,1,0:T(8,128)S(1)}, u32[]{:S(2)}, u32[]{:S(2)}) async-start(f32[8,128,128]{2,1,0:T(8,128)} %broadcast_in_dim.16), calls=%async_computation.1 | async-start | bytes 1048576 | tf_op jit(solution)/shard_map/all_to_all | solution.py:25
  34.0 15.8 %copy-start = (f32[1,128,8,128]{3,2,1,0:T(8,128)S(1)}, f32[1,128,8,128]{3,2,1,0:T(8,128)}, u32[]{:S(2)}) copy-start(f32[1,128,8,128]{3,2,1,0:T(8,128)} %param.1) | copy-start | bytes 1572868
  49.2 0.6 copy-start.1
  49.8 0.8 slice-start
  51.7 26.5 %all-to-all-start.2 = ((f32[8,240,128]{2,1,0:T(8,128)}), f32[8,240,128]{2,1,0:T(8,128)S(1)}, u32[]{:S(2)}, u32[]{:S(2)}) async-start(f32[8,240,128]{2,1,0:T(8,128)} %broadcast_in_dim.17), calls=%async_computation.2 | async-start | bytes 1966080 | tf_op jit(solution)/shard_map/all_to_all | solution.py:25
  63.9 26.1 %collective-permute-start.2 = (f32[128,128]{1,0:T(8,128)S(1)}, f32[128,128]{1,0:T(8,128)S(1)}, u32[]{:S(2)}, u32[]{:S(2)}) collective-permute-start(f32[128,128]{1,0:T(8,128)S(1)} %get-tuple-element.5), channel_id=1, source_target_pairs={{0,0},{1,8},{2,16},{3,24},{4,32},{5,40},{6,48},{7,56},{8,1},{9,9},... | collective-permute-start | bytes 196616 | tf_op jit(solution)/shard_map/ppermute | solution.py:126
  78.2 11.7 %collective-permute-start.1 = (f32[128,128]{1,0:T(8,128)S(1)}, f32[128,128]{1,0:T(8,128)S(1)}, u32[]{:S(2)}, u32[]{:S(2)}) collective-permute-start(f32[128,128]{1,0:T(8,128)S(1)} %slice.65), channel_id=1, source_target_pairs={{0,0},{1,8},{2,16},{3,24},{4,32},{5,40},{6,48},{7,56},{8,1},{9,9},... | collective-permute-start | bytes 196616 | tf_op jit(solution)/shard_map/ppermute | solution.py:150
  91.1 21.1 %all-to-all-start.3 = ((f32[8,144,128]{2,1,0:T(8,128)}), f32[8,144,128]{2,1,0:T(8,128)S(1)}, u32[]{:S(2)}, u32[]{:S(2)}) async-start(f32[8,144,128]{2,1,0:T(8,128)} %broadcast_in_dim.18), calls=%async_computation.3 | async-start | bytes 1179648 | tf_op jit(solution)/shard_map/all_to_all | solution.py:25
  114.0 23.5 %all-to-all-start.4 = ((f32[8,128,128]{2,1,0:T(8,128)}), f32[8,128,128]{2,1,0:T(8,128)S(1)}, u32[]{:S(2)}, u32[]{:S(2)}) async-start(f32[8,128,128]{2,1,0:T(8,128)} %broadcast_in_dim.19), calls=%async_computation.4 | async-start | bytes 1048576 | tf_op jit(solution)/shard_map/all_to_all | solution.py:25

commit v4 on v3

v4 whole, which is shorter than its diff:
```python
import jax
import jax.numpy as jnp
from jax import lax
from jax.experimental import pallas as pl
from jax.experimental.pallas import tpu as pltpu
from jax.sharding import Mesh, PartitionSpec as P

COL = ("x", "k")
PLANE = ("y", "x", "k")
BLOCK = 8
GROUP = 32


def product(left, right, contract):
    return lax.dot_general(
        left,
        right,
        (contract, ((), ())),
        precision=lax.Precision.HIGHEST,
        preferred_element_type=jnp.float32,
    )


def spread(block, axis, count):
    whole = jnp.broadcast_to(block[None], (count,) + block.shape)
    return lax.all_to_all(whole, axis, 0, 0, tiled=True)


def packed(square):
    half = square.shape[0] // 2
    corner = square[half:, half:]
    corner = jnp.concatenate([corner[: half // 2], corner[half // 2 :]], axis=1)
    return jnp.concatenate([square[:half], corner], axis=0)


def unit(width):
    rows = lax.broadcasted_iota(jnp.int32, (width, width), 0)
    lanes = lax.broadcasted_iota(jnp.int32, (width, width), 1)
    return (rows == lanes).astype(jnp.float32)


def columns_of(rows, low, width):
    return [
        jnp.broadcast_to(rows[:, low + b : low + b + 1], (BLOCK, width))
        for b in range(BLOCK)
    ]


def row_of(rows, j):
    return jnp.broadcast_to(rows[j : j + 1, :], rows.shape)


def cholesky_kernel(upper_ref, corner_ref, out_ref):
    width = out_ref.shape[0]
    half = width // 2
    upper, corner = upper_ref[...], corner_ref[...]
    lower = jnp.concatenate(
        [jnp.zeros((half, half), jnp.float32)]
        + [jnp.concatenate([corner[:, :half], corner[:, half:]], axis=0)],
        axis=1,
    )
    gram = jnp.concatenate([upper, lower], axis=0)
    lanes = lax.broadcasted_iota(jnp.int32, (1, width), 1)
    place = lax.broadcasted_iota(jnp.int32, (BLOCK, 1), 0)
    turned = gram.T
    rows = []
    for low in range(0, width, BLOCK):
        own = gram[low : low + BLOCK, :]
        if low >= half:
            own = jnp.where(lanes < half, turned[low : low + BLOCK, :], own)
        rows.append(own)
    count = width // BLOCK
    for i in range(count):
        low = BLOCK * i
        live = range(i, count)
        cols = {v: columns_of(rows[v], low, width) for v in live}
        inside = (lanes >= low) & (lanes < low + BLOCK)
        for v in live:
            fill = (lanes == low + place).astype(jnp.float32) if v == i else 0.0
            rows[v] = jnp.where(inside, fill, rows[v])
        for j in range(BLOCK):
            scale = lax.rsqrt(row_of(cols[i][j], j))
            pivots = [
                row_of(cols[i][b], j) * scale if b > j else None for b in range(BLOCK)
            ]
            pivot = row_of(rows[i], j) * scale
            for v in live:
                factor = cols[v][j] * scale
                if v == i:
                    factor = jnp.where(place > j, factor, 0.0)
                for b in range(j + 1, BLOCK):
                    cols[v][b] = cols[v][b] - factor * pivots[b]
                after = rows[v] - factor * pivot
                rows[v] = jnp.where(place == j, pivot, after) if v == i else after
        out_ref[low : low + BLOCK, :] = jnp.where(lanes < low + BLOCK, rows[i], 0.0)


def inverse_kernel(matrix_ref, out_ref, work):
    width = out_ref.shape[0]
    work[...] = matrix_ref[...]
    lanes = lax.broadcasted_iota(jnp.int32, (1, width), 1)
    place = lax.broadcasted_iota(jnp.int32, (BLOCK, 1), 0)
    count = GROUP // BLOCK
    for top in range(0, width, GROUP):
        rows = [work[top + BLOCK * v : top + BLOCK * (v + 1), :] for v in range(count)]
        for i in range(count):
            low = top + BLOCK * i
            cols = [columns_of(rows[v], low, width) for v in range(count)]
            inside = (lanes >= low) & (lanes < low + BLOCK)
            for v in range(count):
                fill = (lanes == low + place).astype(jnp.float32) if v == i else 0.0
                rows[v] = jnp.where(inside, fill, rows[v])
            for j in range(BLOCK):
                scale = 1.0 / row_of(cols[i][j], j)
                pivots = [
                    row_of(cols[i][b], j) * scale if b > j else None
                    for b in range(BLOCK)
                ]
                pivot = row_of(rows[i], j) * scale
                for v in range(count):
                    factor = cols[v][j]
                    for b in range(j + 1, BLOCK):
                        after = cols[v][b] - factor * pivots[b]
                        if v == i:
                            after = jnp.where(place == j, pivots[b], after)
                        cols[v][b] = after
                    after = rows[v] - factor * pivot
                    rows[v] = jnp.where(place == j, pivot, after) if v == i else after
        group = jnp.concatenate(rows, axis=0)
        inside = (lanes >= top) & (lanes < top + GROUP)
        for start, stop in ((0, top), (top + GROUP, width)):
            if stop > start:
                old = work[start:stop, :]
                work[start:stop, :] = jnp.where(inside, 0.0, old) - product(
                    old[:, top : top + GROUP], group, ((1,), (0,))
                )
        work[top : top + GROUP, :] = group
    out_ref[...] = work[...]


def transposition(side):
    def ring(a, b, size):
        return min((a - b) % size, (b - a) % size)

    pairs = []
    for c in range(side):
        targets = sorted(range(side), key=lambda y: -ring(y, c, side))
        sources = sorted(range(side), key=lambda d: ring(d // 2, c // 2, side // 2))
        pairs += [(c * side + d, y * side + c) for d, y in zip(sources, targets)]
    return pairs


def factor_call(kernel, scratch, *operands):
    width = operands[0].shape[1]
    return pl.pallas_call(
        kernel,
        out_shape=jax.ShapeDtypeStruct((width, width), jnp.float32),
        scratch_shapes=[pltpu.VMEM((width, width), jnp.float32)] * scratch,
        cost_estimate=pl.CostEstimate(
            flops=0, bytes_accessed=30_000_000, transcendentals=0
        ),
        compiler_params=pltpu.CompilerParams(vmem_limit_bytes=4 << 20),
    )(*operands)


def per_device(matrix):
    _, width, count, _ = matrix.shape
    side = lax.axis_size("y")
    depth = lax.axis_index("z")
    row = depth * side + lax.axis_index("y")
    col = lax.axis_index(COL)
    swap = transposition(side)
    piece, half = width // side, width // 2
    local = matrix[0]

    on_row = lax.optimization_barrier(unit(width) * (row == 1))
    identity = unit(width)

    first = spread(local[:, 0, :], COL, side)
    panel_row = first[0] * (row != 0).astype(jnp.float32)
    next_row = first[1]
    panel_own = lax.ppermute(panel_row, PLANE, swap)
    panel = spread(panel_own, "z", count)
    next_own = lax.ppermute(next_row, PLANE, swap)

    part = product(local, panel, ((1, 2), (0, 1)))
    gram_part = product(panel, panel, ((0, 1), (0, 1)))
    shared = jnp.concatenate(
        [
            part,
            packed(gram_part),
            lax.dynamic_slice_in_dim(panel[0], depth * piece, piece, 0),
        ],
        axis=0,
    )
    came = spread(shared, COL, side)
    tall = shared.shape[0] - piece
    total = jnp.sum(came[:, :tall], axis=0)
    head_slice = came[1, tall:]
    mixed_row = total[:width]
    mixed_own = lax.ppermute(mixed_row, PLANE, swap)
    inverse = factor_call(
        cholesky_kernel, 0, total[width : width + half], total[width + half :]
    )

    image_own = product(mixed_own, inverse, ((1,), (1,))) + next_own
    came = spread(jnp.concatenate([image_own, head_slice], axis=0), "z", count)
    image = came[:, :width]
    head = came[:, width:].reshape(width, width)

    at_col = ((jnp.arange(count) == 0) & (col == 1)).astype(jnp.float32)
    refl_row = product(panel_row, inverse, ((1,), (1,))) + on_row
    image_row = product(mixed_row, inverse, ((1,), (1,))) + next_row
    refl = product(panel, inverse, ((2,), (1,))) + identity[None] * at_col[:, None, None]

    middle_part = packed(product(refl, image, ((0, 1), (0, 1))))
    came = spread(middle_part, COL, side)

    coupling = factor_call(
        inverse_kernel, 1, identity + product(inverse, head, ((1,), (1,)))
    )
    turned_row = product(refl_row, coupling, ((1,), (1,)))
    half_row = product(image_row, coupling, ((1,), (0,)))
    partial = lax.optimization_barrier(local - product(turned_row, image, ((1,), (2,))))

    upper = jnp.sum(came[:, :half], axis=0)
    corner = came[:, half:]
    corner = jnp.concatenate([corner[:, :, :half], corner[:, :, half:]], axis=1)
    corner = jnp.sum(corner, axis=0)
    far = turned_row[:, half:]
    sandwich_row = product(turned_row[:, :half], upper, ((1,), (0,)))
    sandwich_row += jnp.concatenate(
        [
            product(far, upper[:, half:], ((1,), (1,))),
            product(far, corner, ((1,), (0,))),
        ],
        axis=1,
    )
    sandwich_row = product(sandwich_row, coupling, ((1,), (0,)))
    result = partial - product(half_row - sandwich_row, refl, ((1,), (2,)))
    return result[None]


def solution(mesh):
    grid = Mesh(mesh.devices.reshape(8, 8, 4, 2), ("z", "y", "x", "k"))
    spec = P(None, ("z", "y"), None, COL)

    return jax.shard_map(
        per_device, mesh=grid, in_specs=(spec,), out_specs=spec, check_vma=False
    )
```

time: 140 us -> 130 us (0.929)
  the two profiles are of different devices: /device:TPU:1 before, /device:TPU:40 now
where the time goes in v4:
time: 130 us; the launch traced here: 129 us
  waiting for transfers between devices  72.2 us (56%)
  starting transfers between devices  33.8 us (26%)
  Pallas kernels  8.05 us (6%)
  local copies, waits for them, and re-layouts  7.44 us (6%)
  matrix products  7.22 us (6%)
    all_to_all x5, waiting for transfers between devices, spread(): return lax.all_to_all(whole, axis, 0, 0, tiled=True)  59.4 us
    all_to_all x5, starting transfers between devices, spread(): return lax.all_to_all(whole, axis, 0, 0, tiled=True)  25.3 us
    ppermute x1, waiting for transfers between devices, per_device(): panel_own = lax.ppermute(panel_row, PLANE, swap)  8.77 us
    pallas_call x2, Pallas kernels, factor_call(): pl.pallas_call(kernel, out_shape=jax.ShapeDtypeStruct((width, width), jnp...  8.05 us
    dot_general x16, matrix products, product(): lax.dot_general(left, right, (contract, ((), ())), precision=lax.Precisio...  7.22 us
    ppermute x1, starting transfers between devices, per_device(): next_own = lax.ppermute(next_row, PLANE, swap)  4.59 us
    broadcast_in_dim x6, local copies, waits for them, and re-layouts, spread(): whole = jnp.broadcast_to(block[None], (count,) + block.shape)  4.32 us
    ppermute x1, waiting for transfers between devices, per_device(): mixed_own = lax.ppermute(mixed_row, PLANE, swap)  4.11 us
  transfers between devices with their start and end apart: 8, of which 7 were waited for; matrix products, arithmetic and copies ran while one was open for 2% of the time, Pallas kernels for 6%

profile of v4, /device:TPU:40, one launch (start us, length us, event | category | flops | bytes accessed | tf_op | source)
XLA Modules:
  0.0 129.3 jit_solution(16945007062887442528)
XLA Ops:
  0.0 1.1 copy.20
  1.2 0.8 broadcast_in_dim.15
  2.0 4.3 %all-to-all-start = ((f32[8,128,128]{2,1,0:T(8,128)}), f32[8,128,128]{2,1,0:T(8,128)S(1)}, u32[]{:S(2)}, u32[]{:S(2)}) async-start(f32[8,128,128]{2,1,0:T(8,128)} %broadcast_in_dim.15), calls=%async_computation | async-start | bytes 1048576 | tf_op jit(solution)/shard_map/all_to_all | solution.py:26
  6.3 10.3 %all-to-all-done = f32[8,128,128]{2,1,0:T(8,128)S(1)} async-done(((f32[8,128,128]{2,1,0:T(8,128)}), f32[8,128,128]{2,1,0:T(8,128)S(1)}, u32[]{:S(2)}, u32[]{:S(2)}) %all-to-all-start) | async-done | bytes 524320 | tf_op jit(solution)/shard_map/all_to_all | solution.py:26
  16.6 1.9 %collective-permute-start = (f32[128,128]{1,0:T(8,128)S(1)}, f32[128,128]{1,0:T(8,128)S(1)}, u32[]{:S(2)}, u32[]{:S(2)}) collective-permute-start(f32[128,128]{1,0:T(8,128)S(1)} %get-tuple-element.6), channel_id=1, source_target_pairs={{0,32},{1,24},{2,40},{3,16},{6,48},{7,8},{4,56},{5,0},{8,41},{9,33... | collective-permute-start | bytes 196616 | tf_op jit(solution)/shard_map/ppermute | solution.py:182
  18.6 8.8 %collective-permute-done = f32[128,128]{1,0:T(8,128)S(1)} collective-permute-done((f32[128,128]{1,0:T(8,128)S(1)}, f32[128,128]{1,0:T(8,128)S(1)}, u32[]{:S(2)}, u32[]{:S(2)}) %collective-permute-start) | collective-permute-done | bytes 65568 | tf_op jit(solution)/shard_map/ppermute | solution.py:182
  27.3 0.8 broadcast_in_dim.16
  28.2 10.3 %all-to-all-start.1 = ((f32[8,128,128]{2,1,0:T(8,128)}), f32[8,128,128]{2,1,0:T(8,128)S(1)}, u32[]{:S(2)}, u32[]{:S(2)}) async-start(f32[8,128,128]{2,1,0:T(8,128)} %broadcast_in_dim.16), calls=%async_computation.1 | async-start | bytes 1048576 | tf_op jit(solution)/shard_map/all_to_all | solution.py:26
  38.5 17.0 %all-to-all-done.1 = f32[8,128,128]{2,1,0:T(8,128)S(1)} async-done(((f32[8,128,128]{2,1,0:T(8,128)}), f32[8,128,128]{2,1,0:T(8,128)S(1)}, u32[]{:S(2)}, u32[]{:S(2)}) %all-to-all-start.1) | async-done | bytes 524320 | tf_op jit(solution)/shard_map/all_to_all | solution.py:26
  55.5 1.0 convolution_bitcast_fusion.1
  56.5 0.1 fusion.18
  56.6 0.5 copy-done.1
  57.1 0.0 slice-start
  57.1 0.7 convolution_bitcast_fusion.2
  57.8 0.0 slice-done
  57.9 0.1 pad_maximum_fusion
  57.9 1.0 broadcast_in_dim.17
  59.0 3.6 %all-to-all-start.2 = ((f32[8,240,128]{2,1,0:T(8,128)}), f32[8,240,128]{2,1,0:T(8,128)S(1)}, u32[]{:S(2)}, u32[]{:S(2)}) async-start(f32[8,240,128]{2,1,0:T(8,128)} %broadcast_in_dim.17), calls=%async_computation.2 | async-start | bytes 1966080 | tf_op jit(solution)/shard_map/all_to_all | solution.py:26
  62.5 4.6 %collective-permute-start.2 = (f32[128,128]{1,0:T(8,128)S(1)}, f32[128,128]{1,0:T(8,128)S(1)}, u32[]{:S(2)}, u32[]{:S(2)}) collective-permute-start(f32[128,128]{1,0:T(8,128)S(1)} %get-tuple-element.5), channel_id=1, source_target_pairs={{0,32},{1,24},{2,40},{3,16},{6,48},{7,8},{4,56},{5,0},{8,41},{9,33... | collective-permute-start | bytes 196616 | tf_op jit(solution)/shard_map/ppermute | solution.py:184
  67.1 11.9 %all-to-all-done.2 = f32[8,240,128]{2,1,0:T(8,128)S(1)} async-done(((f32[8,240,128]{2,1,0:T(8,128)}), f32[8,240,128]{2,1,0:T(8,128)S(1)}, u32[]{:S(2)}, u32[]{:S(2)}) %all-to-all-start.2) | async-done | bytes 983072 | tf_op jit(solution)/shard_map/all_to_all | solution.py:26
  79.1 1.9 %collective-permute-start.1 = (f32[128,128]{1,0:T(8,128)S(1)}, f32[128,128]{1,0:T(8,128)S(1)}, u32[]{:S(2)}, u32[]{:S(2)}) collective-permute-start(f32[128,128]{1,0:T(8,128)S(1)} %slice.110), channel_id=1, source_target_pairs={{0,32},{1,24},{2,40},{3,16},{6,48},{7,8},{4,56},{5,0},{8,41},{9,33... | collective-permute-start | bytes 196616 | tf_op jit(solution)/shard_map/ppermute | solution.py:201
  81.1 4.0 %shard_map.17 = f32[128,128]{1,0:T(8,128)S(1)} custom-call(f32[64,128]{1,0:T(8,128)S(1)} %slice.108.upper_ref, f32[32,128]{1,0:T(8,128)S(1)} %slice.109.corner_ref), custom_call_target="tpu_custom_call" | custom-call | bytes 30000000 | tf_op jit(solution)/shard_map/pallas_call | solution.py:155
  85.1 4.1 %collective-permute-done.1 = f32[128,128]{1,0:T(8,128)S(1)} collective-permute-done((f32[128,128]{1,0:T(8,128)S(1)}, f32[128,128]{1,0:T(8,128)S(1)}, u32[]{:S(2)}, u32[]{:S(2)}) %collective-permute-start.1) | collective-permute-done | bytes 65568 | tf_op jit(solution)/shard_map/ppermute | solution.py:201
  89.2 0.3 convolution_add_fusion.4
  89.5 0.9 broadcast_in_dim.18
  90.4 3.5 %all-to-all-start.3 = ((f32[8,144,128]{2,1,0:T(8,128)}), f32[8,144,128]{2,1,0:T(8,128)S(1)}, u32[]{:S(2)}, u32[]{:S(2)}) async-start(f32[8,144,128]{2,1,0:T(8,128)} %broadcast_in_dim.18), calls=%async_computation.3 | async-start | bytes 1179648 | tf_op jit(solution)/shard_map/all_to_all | solution.py:26
  94.0 0.3 convolution_add_fusion.5
  94.2 0.3 convolution_add_fusion.2
  94.5 0.6 convolution_add_fusion
  95.1 17.0 %all-to-all-done.3 = f32[8,144,128]{2,1,0:T(8,128)S(1)} async-done(((f32[8,144,128]{2,1,0:T(8,128)}), f32[8,144,128]{2,1,0:T(8,128)S(1)}, u32[]{:S(2)}, u32[]{:S(2)}) %all-to-all-start.3) | async-done | bytes 589856 | tf_op jit(solution)/shard_map/all_to_all | solution.py:26
  112.1 1.0 convolution_bitcast_fusion
  113.1 0.1 fusion.17
  113.2 0.1 maximum_maximum_fusion
  113.3 0.8 broadcast_in_dim.19
  114.1 3.6 %all-to-all-start.4 = ((f32[8,96,128]{2,1,0:T(8,128)}), f32[8,96,128]{2,1,0:T(8,128)S(1)}, u32[]{:S(2)}, u32[]{:S(2)}) async-start(f32[8,96,128]{2,1,0:T(8,128)} %broadcast_in_dim.19), calls=%async_computation.4 | async-start | bytes 786432 | tf_op jit(solution)/shard_map/all_to_all | solution.py:26
  117.7 0.3 convolution_add_fusion.3.matrix_ref
  118.0 4.1 %shard_map.18 = f32[128,128]{1,0:T(8,128)S(1)} custom-call(f32[128,128]{1,0:T(8,128)S(1)} %convolution_add_fusion.3.matrix_ref), custom_call_target="tpu_custom_call" | custom-call | bytes 30000000 | tf_op jit(solution)/shard_map/pallas_call | solution.py:155
  122.1 0.3 fusion.19
  122.3 0.7 convolution_subtract_fusion.1
  123.1 0.2 fusion.20
  123.3 3.1 %all-to-all-done.4 = f32[8,96,128]{2,1,0:T(8,128)S(1)} async-done(((f32[8,96,128]{2,1,0:T(8,128)}), f32[8,96,128]{2,1,0:T(8,128)S(1)}, u32[]{:S(2)}, u32[]{:S(2)}) %all-to-all-start.4) | async-done | bytes 393248 | tf_op jit(solution)/shard_map/all_to_all | solution.py:26
  126.4 0.3 fusion.9
  126.7 0.1 fusion.16
  126.8 0.3 fusion.12
  127.1 0.3 convolution_add_fusion.1
  127.4 0.2 fusion.1
  127.6 0.6 fusion
  128.2 1.1 copy.11
  (21 shorter events, 0.2 us)
Async XLA Ops:
  2.0 14.6 %all-to-all-start = ((f32[8,128,128]{2,1,0:T(8,128)}), f32[8,128,128]{2,1,0:T(8,128)S(1)}, u32[]{:S(2)}, u32[]{:S(2)}) async-start(f32[8,128,128]{2,1,0:T(8,128)} %broadcast_in_dim.15), calls=%async_computation | async-start | bytes 1048576 | tf_op jit(solution)/shard_map/all_to_all | solution.py:26
  16.6 10.7 %collective-permute-start = (f32[128,128]{1,0:T(8,128)S(1)}, f32[128,128]{1,0:T(8,128)S(1)}, u32[]{:S(2)}, u32[]{:S(2)}) collective-permute-start(f32[128,128]{1,0:T(8,128)S(1)} %get-tuple-element.6), channel_id=1, source_target_pairs={{0,32},{1,24},{2,40},{3,16},{6,48},{7,8},{4,56},{5,0},{8,41},{9,33... | collective-permute-start | bytes 196616 | tf_op jit(solution)/shard_map/ppermute | solution.py:182
  28.2 27.3 %all-to-all-start.1 = ((f32[8,128,128]{2,1,0:T(8,128)}), f32[8,128,128]{2,1,0:T(8,128)S(1)}, u32[]{:S(2)}, u32[]{:S(2)}) async-start(f32[8,128,128]{2,1,0:T(8,128)} %broadcast_in_dim.16), calls=%async_computation.1 | async-start | bytes 1048576 | tf_op jit(solution)/shard_map/all_to_all | solution.py:26
  38.5 18.6 %copy-start = (f32[1,128,8,128]{3,2,1,0:T(8,128)S(1)}, f32[1,128,8,128]{3,2,1,0:T(8,128)}, u32[]{:S(2)}) copy-start(f32[1,128,8,128]{3,2,1,0:T(8,128)} %param.1) | copy-start | bytes 1572868
  56.5 0.6 copy-start.1
  57.1 0.8 slice-start
  59.0 20.1 %all-to-all-start.2 = ((f32[8,240,128]{2,1,0:T(8,128)}), f32[8,240,128]{2,1,0:T(8,128)S(1)}, u32[]{:S(2)}, u32[]{:S(2)}) async-start(f32[8,240,128]{2,1,0:T(8,128)} %broadcast_in_dim.17), calls=%async_computation.2 | async-start | bytes 1966080 | tf_op jit(solution)/shard_map/all_to_all | solution.py:26
  62.5 22.6 %collective-permute-start.2 = (f32[128,128]{1,0:T(8,128)S(1)}, f32[128,128]{1,0:T(8,128)S(1)}, u32[]{:S(2)}, u32[]{:S(2)}) collective-permute-start(f32[128,128]{1,0:T(8,128)S(1)} %get-tuple-element.5), channel_id=1, source_target_pairs={{0,32},{1,24},{2,40},{3,16},{6,48},{7,8},{4,56},{5,0},{8,41},{9,33... | collective-permute-start | bytes 196616 | tf_op jit(solution)/shard_map/ppermute | solution.py:184
  79.1 10.1 %collective-permute-start.1 = (f32[128,128]{1,0:T(8,128)S(1)}, f32[128,128]{1,0:T(8,128)S(1)}, u32[]{:S(2)}, u32[]{:S(2)}) collective-permute-start(f32[128,128]{1,0:T(8,128)S(1)} %slice.110), channel_id=1, source_target_pairs={{0,32},{1,24},{2,40},{3,16},{6,48},{7,8},{4,56},{5,0},{8,41},{9,33... | collective-permute-start | bytes 196616 | tf_op jit(solution)/shard_map/ppermute | solution.py:201
  90.4 21.8 %all-to-all-start.3 = ((f32[8,144,128]{2,1,0:T(8,128)}), f32[8,144,128]{2,1,0:T(8,128)S(1)}, u32[]{:S(2)}, u32[]{:S(2)}) async-start(f32[8,144,128]{2,1,0:T(8,128)} %broadcast_in_dim.18), calls=%async_computation.3 | async-start | bytes 1179648 | tf_op jit(solution)/shard_map/all_to_all | solution.py:26
  114.1 12.3 %all-to-all-start.4 = ((f32[8,96,128]{2,1,0:T(8,128)}), f32[8,96,128]{2,1,0:T(8,128)S(1)}, u32[]{:S(2)}, u32[]{:S(2)}) async-start(f32[8,96,128]{2,1,0:T(8,128)} %broadcast_in_dim.19), calls=%async_computation.4 | async-start | bytes 786432 | tf_op jit(solution)/shard_map/all_to_all | solution.py:26

commit v5 on v4

--- a/solution.py
+++ b/solution.py
@@ -6,6 +6,7 @@
 from jax.sharding import Mesh, PartitionSpec as P
 
 COL = ("x", "k")
+ROW = ("z", "y")
 PLANE = ("y", "x", "k")
 BLOCK = 8
 GROUP = 32
@@ -138,18 +139,6 @@
     out_ref[...] = work[...]
 
 
-def transposition(side):
-    def ring(a, b, size):
-        return min((a - b) % size, (b - a) % size)
-
-    pairs = []
-    for c in range(side):
-        targets = sorted(range(side), key=lambda y: -ring(y, c, side))
-        sources = sorted(range(side), key=lambda d: ring(d // 2, c // 2, side // 2))
-        pairs += [(c * side + d, y * side + c) for d, y in zip(sources, targets)]
-    return pairs
-
-
 def factor_call(kernel, scratch, *operands):
     width = operands[0].shape[1]
     return pl.pallas_call(
@@ -169,62 +158,64 @@
     depth = lax.axis_index("z")
     row = depth * side + lax.axis_index("y")
     col = lax.axis_index(COL)
-    swap = transposition(side)
+    swap = [(a * side + b, b * side + a) for a in range(side) for b in range(side)]
     piece, half = width // side, width // 2
+    identity = unit(width)
     local = matrix[0]
 
-    on_row = lax.optimization_barrier(unit(width) * (row == 1))
-    identity = unit(width)
-
-    first = spread(local[:, 0, :], COL, side)
-    panel_row = first[0] * (row != 0).astype(jnp.float32)
-    next_row = first[1]
-    panel_own = lax.ppermute(panel_row, PLANE, swap)
-    panel = spread(panel_own, "z", count)
-    next_own = lax.ppermute(next_row, PLANE, swap)
+    start = local[:, 0, :].reshape(side, piece, width)
+    turned = lax.all_to_all(start, "y", 0, 0, tiled=True)
+    slots = jnp.concatenate([turned, start], axis=1)
+    came = lax.all_to_all(slots, COL, 0, 0, tiled=True)
+    panel_piece = came[0, :piece] * (depth * side + col != 0)
+    next_piece = came[1, :piece]
+    panel_slice = came[0, piece:] * (row != 0)
+    next_slice = came[1, piece:]
+    panel = spread(panel_piece, ROW, side * count).reshape(count, width, width)
 
     part = product(local, panel, ((1, 2), (0, 1)))
     gram_part = product(panel, panel, ((0, 1), (0, 1)))
-    shared = jnp.concatenate(
+    shared = jnp.concatenate([packed(gram_part), panel[0]], axis=0)
+    slots = jnp.concatenate(
         [
-            part,
-            packed(gram_part),
-            lax.dynamic_slice_in_dim(panel[0], depth * piece, piece, 0),
+            part.reshape(side, piece, width),
+            jnp.broadcast_to(shared[None], (side,) + shared.shape),
         ],
-        axis=0,
-    )
-    came = spread(shared, COL, side)
-    tall = shared.shape[0] - piece
-    total = jnp.sum(came[:, :tall], axis=0)
-    head_slice = came[1, tall:]
-    mixed_row = total[:width]
-    mixed_own = lax.ppermute(mixed_row, PLANE, swap)
-    inverse = factor_call(
-        cholesky_kernel, 0, total[width : width + half], total[width + half :]
-    )
-
-    image_own = product(mixed_own, inverse, ((1,), (1,))) + next_own
-    came = spread(jnp.concatenate([image_own, head_slice], axis=0), "z", count)
-    image = came[:, :width]
-    head = came[:, width:].reshape(width, width)
-
-    at_col = ((jnp.arange(count) == 0) & (col == 1)).astype(jnp.float32)
-    refl_row = product(panel_row, inverse, ((1,), (1,))) + on_row
-    image_row = product(mixed_row, inverse, ((1,), (1,))) + next_row
-    refl = product(panel, inverse, ((2,), (1,))) + identity[None] * at_col[:, None, None]
-
-    middle_part = packed(product(refl, image, ((0, 1), (0, 1))))
-    came = spread(middle_part, COL, side)
+        axis=1,
+    )
+    came = lax.all_to_all(slots, COL, 0, 0, tiled=True)
+    tall = piece + half + half // 2
+    head = came[1, tall:]
+    mixed_slice = jnp.sum(came[:, :piece], axis=0)
+    total = jnp.sum(came[:, piece:tall], axis=0)
+    mixed_piece = lax.ppermute(mixed_slice, PLANE, swap)
+    inverse = factor_call(cholesky_kernel, 0, total[:half], total[half:])
+
+    image_piece = product(mixed_piece, inverse, ((1,), (1,))) + next_piece
+    image = spread(image_piece, ROW, side * count).reshape(count, width, width)
 
     coupling = factor_call(
         inverse_kernel, 1, identity + product(inverse, head, ((1,), (1,)))
     )
-    turned_row = product(refl_row, coupling, ((1,), (1,)))
-    half_row = product(image_row, coupling, ((1,), (0,)))
-    partial = lax.optimization_barrier(local - product(turned_row, image, ((1,), (2,))))
-
+    at_col = ((jnp.arange(count) == 0) & (col == 1)).astype(jnp.float32)
+    refl = product(panel, inverse, ((2,), (1,))) + identity[None] * at_col[:, None, None]
+    rows = lax.broadcasted_iota(jnp.int32, (piece, width), 0) + col * piece
+    lanes = lax.broadcasted_iota(jnp.int32, (piece, width), 1)
+    on_row = ((rows == lanes) & (row == 1)).astype(jnp.float32)
+    refl_slice = product(panel_slice, inverse, ((1,), (1,))) + on_row
+    image_slice = product(mixed_slice, inverse, ((1,), (1,))) + next_slice
+    turned_slice = product(refl_slice, coupling, ((1,), (1,)))
+    half_slice = product(image_slice, coupling, ((1,), (0,)))
+
+    middle_part = packed(product(refl, image, ((0, 1), (0, 1))))
+    came = spread(
+        jnp.concatenate([middle_part, turned_slice, half_slice], axis=0), COL, side
+    )
+    tall = half + half // 2
+    turned_row = came[:, tall : tall + piece].reshape(width, width)
+    half_row = came[:, tall + piece :].reshape(width, width)
     upper = jnp.sum(came[:, :half], axis=0)
-    corner = came[:, half:]
+    corner = came[:, half:tall]
     corner = jnp.concatenate([corner[:, :, :half], corner[:, :, half:]], axis=1)
     corner = jnp.sum(corner, axis=0)
     far = turned_row[:, half:]
@@ -237,7 +228,9 @@
         axis=1,
     )
     sandwich_row = product(sandwich_row, coupling, ((1,), (0,)))
-    result = partial - product(half_row - sandwich_row, refl, ((1,), (2,)))
+    left = jnp.concatenate([half_row - sandwich_row, turned_row], axis=1)
+    right = jnp.concatenate([refl, image], axis=2)
+    result = local - product(left, right, ((1,), (2,)))
     return result[None]
 
 

time: 130 us -> 138 us (1.062)
  the two profiles are of different devices: /device:TPU:40 before, /device:TPU:1 now
where the time goes in v5:
time: 138 us; the launch traced here: 137 us
  blocking collectives  42.8 us (31%)
  waiting for transfers between devices  38.5 us (28%)
  starting transfers between devices  33.2 us (24%)
  Pallas kernels  8.1 us (6%)
  local copies, waits for them, and re-layouts  6.17 us (4%)
  matrix products  5.99 us (4%)
  other arithmetic  1.95 us (1%)
    all_to_all x1, blocking collectives, spread(): return lax.all_to_all(whole, axis, 0, 0, tiled=True)  28 us
    all_to_all x2, waiting for transfers between devices, per_device(): came = lax.all_to_all(slots, COL, 0, 0, tiled=True)  19.4 us
    all_to_all x2, waiting for transfers between devices, spread(): return lax.all_to_all(whole, axis, 0, 0, tiled=True)  19.1 us
    all_to_all x2, starting transfers between devices, spread(): return lax.all_to_all(whole, axis, 0, 0, tiled=True)  16.3 us
    all_to_all x1, blocking collectives, per_device(): turned = lax.all_to_all(start, 'y', 0, 0, tiled=True)  14.8 us
    all_to_all x2, starting transfers between devices, per_device(): came = lax.all_to_all(slots, COL, 0, 0, tiled=True)  13.1 us
    pallas_call x2, Pallas kernels, factor_call(): pl.pallas_call(kernel, out_shape=jax.ShapeDtypeStruct((width, width), jnp...  8.1 us
    dot_general x15, matrix products, product(): lax.dot_general(left, right, (contract, ((), ())), precision=lax.Precisio...  5.99 us
  transfers between devices with their start and end apart: 5, of which 4 were waited for; matrix products, arithmetic and copies ran while one was open for 1% of the time, Pallas kernels for 6%

profile of v5, /device:TPU:1, one launch (start us, length us, event | category | flops | bytes accessed | tf_op | source)
XLA Modules:
  0.0 137.0 jit_solution(12539526458542661893)
XLA Ops:
  0.0 1.1 copy.55
  1.2 14.8 %all_to_all.30 = f32[8,16,128]{2,1,0:T(8,128)S(1)} all-to-all(f32[8,16,128]{2,1,0:T(8,128)S(1)} %bitcast.74), channel_id=1, replica_groups=mesh['z'=8,'y'=8,'x'=4,'k'=2] {'y'}, dimensions={0} | all-to-all | bytes 131072 | tf_op jit(solution)/shard_map/all_to_all | solution.py:167
  15.9 0.7 pad_maximum_fusion.1
  16.6 6.3 %all-to-all-start.1 = ((f32[8,32,128]{2,1,0:T(8,128)}), f32[8,32,128]{2,1,0:T(8,128)S(1)}, u32[]{:S(2)}, u32[]{:S(2)}) async-start(f32[8,32,128]{2,1,0:T(8,128)} %pad_maximum_fusion.1), calls=%async_computation.1 | async-start | bytes 262144 | tf_op jit(solution)/shard_map/all_to_all | solution.py:169
  22.9 5.2 %all-to-all-done.1 = f32[8,32,128]{2,1,0:T(8,128)S(1)} async-done(((f32[8,32,128]{2,1,0:T(8,128)}), f32[8,32,128]{2,1,0:T(8,128)S(1)}, u32[]{:S(2)}, u32[]{:S(2)}) %all-to-all-start.1) | async-done | bytes 131104 | tf_op jit(solution)/shard_map/all_to_all | solution.py:169
  28.2 28.0 %all_to_all.31 = f32[64,16,128]{2,1,0:T(8,128)S(1)} all-to-all(f32[64,16,128]{2,1,0:T(8,128)S(1)} %broadcast_in_dim.13), channel_id=1, replica_groups=mesh['z'=8,'y'=8,'x'=4,'k'=2] {'z','y'}, dimensions={0} | all-to-all | bytes 1048576 | tf_op jit(solution)/shard_map/all_to_all | solution.py:27
  56.2 1.0 convolution_bitcast_fusion.1
  57.2 0.0 copy-start.1
  57.3 0.6 copy-done.1
  57.9 0.1 fusion.24
  57.9 0.7 fusion.20
  58.6 0.0 slice-start
  58.7 0.7 slice-done
  59.4 0.1 pad_maximum_fusion.2
  59.5 0.1 broadcast_in_dim.14
  59.6 1.0 pad_maximum_fusion
  60.6 6.8 %all-to-all-start.3 = ((f32[8,240,128]{2,1,0:T(8,128)}), f32[8,240,128]{2,1,0:T(8,128)S(1)}, u32[]{:S(2)}, u32[]{:S(2)}) async-start(f32[8,240,128]{2,1,0:T(8,128)} %pad_maximum_fusion), calls=%async_computation.3 | async-start | bytes 1966080 | tf_op jit(solution)/shard_map/all_to_all | solution.py:186
  67.4 0.1 copy.37
  67.5 14.2 %all-to-all-done.3 = f32[8,240,128]{2,1,0:T(8,128)S(1)} async-done(((f32[8,240,128]{2,1,0:T(8,128)}), f32[8,240,128]{2,1,0:T(8,128)S(1)}, u32[]{:S(2)}, u32[]{:S(2)}) %all-to-all-start.3) | async-done | bytes 983072 | tf_op jit(solution)/shard_map/all_to_all | solution.py:186
  81.7 3.8 %collective-permute-start = (f32[16,128]{1,0:T(8,128)S(1)}, f32[16,128]{1,0:T(8,128)S(1)}, u32[]{:S(2)}, u32[]{:S(2)}) collective-permute-start(f32[16,128]{1,0:T(8,128)S(1)} %slice_reduce_fusion.2), channel_id=1, source_target_pairs={{0,0},{1,8},{2,16},{3,24},{4,32},{5,40},{6,48},{7,56},{8,1},{9,9},... | collective-permute-start | bytes 24584 | tf_op jit(solution)/shard_map/ppermute | solution.py:191
  85.6 4.0 %shard_map.17 = f32[128,128]{1,0:T(8,128)S(1)} custom-call(f32[64,128]{1,0:T(8,128)S(1)} %slice.117.upper_ref, f32[32,128]{1,0:T(8,128)S(1)} %slice.118.corner_ref), custom_call_target="tpu_custom_call" | custom-call | bytes 30000000 | tf_op jit(solution)/shard_map/pallas_call | solution.py:144
  89.6 0.3 convolution_add_fusion.2.matrix_ref
  89.8 0.2 convolution_add_fusion.5
  90.0 0.9 broadcast_in_dim.15
  90.9 7.8 %all-to-all-start.4 = ((f32[64,16,128]{2,1,0:T(8,128)}), f32[64,16,128]{2,1,0:T(8,128)S(1)}, u32[]{:S(2)}, u32[]{:S(2)}) async-start(f32[64,16,128]{2,1,0:T(8,128)} %broadcast_in_dim.15), calls=%async_computation.4 | async-start | bytes 1048576 | tf_op jit(solution)/shard_map/all_to_all | solution.py:27
  98.8 0.2 convolution_add_fusion.3
  98.9 4.1 %shard_map.18 = f32[128,128]{1,0:T(8,128)S(1)} custom-call(f32[128,128]{1,0:T(8,128)S(1)} %convolution_add_fusion.2.matrix_ref), custom_call_target="tpu_custom_call" | custom-call | bytes 30000000 | tf_op jit(solution)/shard_map/pallas_call | solution.py:144
  103.1 0.2 fusion.26
  103.2 0.2 convolution_add_fusion.4
  103.4 0.2 fusion.25
  103.6 0.7 convolution_add_fusion
  104.3 9.9 %all-to-all-done.4 = f32[64,16,128]{2,1,0:T(8,128)S(1)} async-done(((f32[64,16,128]{2,1,0:T(8,128)}), f32[64,16,128]{2,1,0:T(8,128)S(1)}, u32[]{:S(2)}, u32[]{:S(2)}) %all-to-all-start.4) | async-done | bytes 524320 | tf_op jit(solution)/shard_map/all_to_all | solution.py:27
  114.2 0.6 convolution_bitcast_fusion
  114.9 0.1 fusion.23
  115.0 0.1 pad_maximum_fusion.3
  115.0 0.8 broadcast_in_dim.16
  115.9 8.4 %all-to-all-start.5 = ((f32[8,128,128]{2,1,0:T(8,128)}), f32[8,128,128]{2,1,0:T(8,128)S(1)}, u32[]{:S(2)}, u32[]{:S(2)}) async-start(f32[8,128,128]{2,1,0:T(8,128)} %broadcast_in_dim.16), calls=%async_computation.5 | async-start | bytes 1048576 | tf_op jit(solution)/shard_map/all_to_all | solution.py:27
  124.3 0.2 copy.42
  124.5 9.2 %all-to-all-done.5 = f32[8,128,128]{2,1,0:T(8,128)S(1)} async-done(((f32[8,128,128]{2,1,0:T(8,128)}), f32[8,128,128]{2,1,0:T(8,128)S(1)}, u32[]{:S(2)}, u32[]{:S(2)}) %all-to-all-start.5) | async-done | bytes 524320 | tf_op jit(solution)/shard_map/all_to_all | solution.py:27
  133.7 0.1 copy.40
  133.8 0.1 copy.41
  133.9 0.1 fusion.21
  134.1 0.3 fusion.9
  134.3 0.3 fusion.11
  134.6 0.2 convolution_add_fusion.1
  134.8 0.3 convolution_subtract_fusion.1
  135.1 0.8 fusion
  135.9 1.1 copy.45
  (18 shorter events, 0.2 us)
Async XLA Ops:
  16.6 11.5 %all-to-all-start.1 = ((f32[8,32,128]{2,1,0:T(8,128)}), f32[8,32,128]{2,1,0:T(8,128)S(1)}, u32[]{:S(2)}, u32[]{:S(2)}) async-start(f32[8,32,128]{2,1,0:T(8,128)} %pad_maximum_fusion.1), calls=%async_computation.1 | async-start | bytes 262144 | tf_op jit(solution)/shard_map/all_to_all | solution.py:169
  56.2 1.7 %copy-start = (f32[1,128,8,128]{3,2,1,0:T(8,128)S(1)}, f32[1,128,8,128]{3,2,1,0:T(8,128)}, u32[]{:S(2)}) copy-start(f32[1,128,8,128]{3,2,1,0:T(8,128)} %param.1) | copy-start | bytes 1572868
  57.2 0.6 copy-start.1
  58.6 0.8 slice-start
  60.6 21.1 %all-to-all-start.3 = ((f32[8,240,128]{2,1,0:T(8,128)}), f32[8,240,128]{2,1,0:T(8,128)S(1)}, u32[]{:S(2)}, u32[]{:S(2)}) async-start(f32[8,240,128]{2,1,0:T(8,128)} %pad_maximum_fusion), calls=%async_computation.3 | async-start | bytes 1966080 | tf_op jit(solution)/shard_map/all_to_all | solution.py:186
  81.7 8.1 %collective-permute-start = (f32[16,128]{1,0:T(8,128)S(1)}, f32[16,128]{1,0:T(8,128)S(1)}, u32[]{:S(2)}, u32[]{:S(2)}) collective-permute-start(f32[16,128]{1,0:T(8,128)S(1)} %slice_reduce_fusion.2), channel_id=1, source_target_pairs={{0,0},{1,8},{2,16},{3,24},{4,32},{5,40},{6,48},{7,56},{8,1},{9,9},... | collective-permute-start | bytes 24584 | tf_op jit(solution)/shard_map/ppermute | solution.py:191
  90.9 23.3 %all-to-all-start.4 = ((f32[64,16,128]{2,1,0:T(8,128)}), f32[64,16,128]{2,1,0:T(8,128)S(1)}, u32[]{:S(2)}, u32[]{:S(2)}) async-start(f32[64,16,128]{2,1,0:T(8,128)} %broadcast_in_dim.15), calls=%async_computation.4 | async-start | bytes 1048576 | tf_op jit(solution)/shard_map/all_to_all | solution.py:27
  115.9 17.8 %all-to-all-start.5 = ((f32[8,128,128]{2,1,0:T(8,128)}), f32[8,128,128]{2,1,0:T(8,128)S(1)}, u32[]{:S(2)}, u32[]{:S(2)}) async-start(f32[8,128,128]{2,1,0:T(8,128)} %broadcast_in_dim.16), calls=%async_computation.5 | async-start | bytes 1048576 | tf_op jit(solution)/shard_map/all_to_all | solution.py:27

commit v6 on v4

--- a/solution.py
+++ b/solution.py
@@ -7,16 +7,17 @@
 
 COL = ("x", "k")
 PLANE = ("y", "x", "k")
+FAST = lax.Precision.HIGH
 BLOCK = 8
 GROUP = 32
 
 
-def product(left, right, contract):
+def product(left, right, contract, precision=lax.Precision.HIGHEST):
     return lax.dot_general(
         left,
         right,
         (contract, ((), ())),
-        precision=lax.Precision.HIGHEST,
+        precision=precision,
         preferred_element_type=jnp.float32,
     )
 
@@ -37,6 +38,57 @@
     rows = lax.broadcasted_iota(jnp.int32, (width, width), 0)
     lanes = lax.broadcasted_iota(jnp.int32, (width, width), 1)
     return (rows == lanes).astype(jnp.float32)
+
+
+def first_kernel(matrix_ref, out_ref, tile, sems):
+    tile[...] = matrix_ref[0, :, 0, :]
+    copies = [
+        pltpu.make_async_copy(tile, out_ref.at[i], sems.at[i])
+        for i in range(out_ref.shape[0])
+    ]
+    for copy in copies:
+        copy.start()
+    for copy in copies:
+        copy.wait()
+
+
+def first_call(matrix, count):
+    width = matrix.shape[-1]
+    return pl.pallas_call(
+        first_kernel,
+        out_shape=jax.ShapeDtypeStruct((count, width, width), jnp.float32),
+        in_specs=[pl.BlockSpec(memory_space=pltpu.VMEM)],
+        out_specs=pl.BlockSpec(memory_space=pl.ANY),
+        scratch_shapes=[
+            pltpu.VMEM((width, width), jnp.float32),
+            pltpu.SemaphoreType.DMA((count,)),
+        ],
+        compiler_params=pltpu.CompilerParams(vmem_limit_bytes=2 << 20),
+        name="first_tile",
+    )(matrix)
+
+
+def shared_kernel(part_ref, gram_ref, head_ref, out_ref):
+    width = part_ref.shape[1]
+    half, quarter = width // 2, width // 4
+    gram = gram_ref[...]
+    out_ref[:width, :] = part_ref[...]
+    out_ref[width : width + half, :] = gram[:half]
+    corner = [gram[half : half + quarter, half:], gram[half + quarter :, half:]]
+    low = width + half
+    out_ref[low : low + quarter, :] = jnp.concatenate(corner, axis=1)
+    out_ref[low + quarter :, :] = head_ref[...]
+
+
+def shared_call(part, gram, head):
+    width = part.shape[1]
+    tall = width + width // 2 + width // 4 + head.shape[0]
+    return pl.pallas_call(
+        shared_kernel,
+        out_shape=jax.ShapeDtypeStruct((tall, width), jnp.float32),
+        compiler_params=pltpu.CompilerParams(vmem_limit_bytes=2 << 20),
+        name="shared",
+    )(part, gram, head)
 
 
 def columns_of(rows, low, width):
@@ -176,7 +228,7 @@
     on_row = lax.optimization_barrier(unit(width) * (row == 1))
     identity = unit(width)
 
-    first = spread(local[:, 0, :], COL, side)
+    first = lax.all_to_all(first_call(matrix, side), COL, 0, 0, tiled=True)
     panel_row = first[0] * (row != 0).astype(jnp.float32)
     next_row = first[1]
     panel_own = lax.ppermute(panel_row, PLANE, swap)
@@ -185,14 +237,8 @@
 
     part = product(local, panel, ((1, 2), (0, 1)))
     gram_part = product(panel, panel, ((0, 1), (0, 1)))
-    shared = jnp.concatenate(
-        [
-            part,
-            packed(gram_part),
-            lax.dynamic_slice_in_dim(panel[0], depth * piece, piece, 0),
-        ],
-        axis=0,
-    )
+    head_slice = lax.dynamic_slice_in_dim(panel[0], depth * piece, piece, 0)
+    shared = shared_call(part, gram_part, head_slice)
     came = spread(shared, COL, side)
     tall = shared.shape[0] - piece
     total = jnp.sum(came[:, :tall], axis=0)
@@ -213,7 +259,7 @@
     image_row = product(mixed_row, inverse, ((1,), (1,))) + next_row
     refl = product(panel, inverse, ((2,), (1,))) + identity[None] * at_col[:, None, None]
 
-    middle_part = packed(product(refl, image, ((0, 1), (0, 1))))
+    middle_part = packed(product(refl, image, ((0, 1), (0, 1)), FAST))
     came = spread(middle_part, COL, side)
 
     coupling = factor_call(
@@ -221,7 +267,7 @@
     )
     turned_row = product(refl_row, coupling, ((1,), (1,)))
     half_row = product(image_row, coupling, ((1,), (0,)))
-    partial = lax.optimization_barrier(local - product(turned_row, image, ((1,), (2,))))
+    partial = lax.optimization_barrier(local - product(turned_row, image, ((1,), (2,)), FAST))
 
     upper = jnp.sum(came[:, :half], axis=0)
     corner = came[:, half:]
@@ -237,7 +283,7 @@
         axis=1,
     )
     sandwich_row = product(sandwich_row, coupling, ((1,), (0,)))
-    result = partial - product(half_row - sandwich_row, refl, ((1,), (2,)))
+    result = partial - product(half_row - sandwich_row, refl, ((1,), (2,)), FAST)
     return result[None]
 
 

time: 130 us -> 129 us (level)
    all_to_all x5 -> x4, waiting for transfers between devices: 59.4 us -> 48.9 us  [spread(): return lax.all_to_all(whole, axis, 0, 0, tiled=True)]
    all_to_all x0 -> x1, waiting for transfers between devices: none -> 10.3 us  [per_device(): first = lax.all_to_all(first_call(matrix, side), COL, 0, 0, tiled=True)]
    all_to_all x0 -> x1, starting transfers between devices: none -> 4.31 us  [per_device(): first = lax.all_to_all(first_call(matrix, side), COL, 0, 0, tiled=True)]
    all_to_all x5 -> x4, starting transfers between devices: 25.3 us -> 21 us  [spread(): return lax.all_to_all(whole, axis, 0, 0, tiled=True)]
    broadcast_in_dim x6 -> x4, local copies, waits for them, and re-layouts: 4.32 us -> 3.48 us  [spread(): whole = jnp.broadcast_to(block[None], (count,) + block.shape)]
where the time goes in v6:
time: 129 us; the launch traced here: 128 us
  waiting for transfers between devices  72.1 us (56%)
  starting transfers between devices  33.8 us (26%)
  Pallas kernels  9.02 us (7%)
  local copies, waits for them, and re-layouts  6.5 us (5%)
  matrix products  6.3 us (5%)
    all_to_all x4, waiting for transfers between devices, spread(): return lax.all_to_all(whole, axis, 0, 0, tiled=True)  48.9 us
    all_to_all x4, starting transfers between devices, spread(): return lax.all_to_all(whole, axis, 0, 0, tiled=True)  21 us
    all_to_all x1, waiting for transfers between devices, per_device(): first = lax.all_to_all(first_call(matrix, side), COL, 0, 0, tiled=True)  10.3 us
    ppermute x1, waiting for transfers between devices, per_device(): panel_own = lax.ppermute(panel_row, PLANE, swap)  8.77 us
    pallas_call x2, Pallas kernels, factor_call(): pl.pallas_call(kernel, out_shape=jax.ShapeDtypeStruct((width, width), jnp...  8.05 us
    dot_general x16, matrix products, product(): lax.dot_general(left, right, (contract, ((), ())), precision=precision, p...  6.3 us
    ppermute x1, starting transfers between devices, per_device(): next_own = lax.ppermute(next_row, PLANE, swap)  4.59 us
    all_to_all x1, starting transfers between devices, per_device(): first = lax.all_to_all(first_call(matrix, side), COL, 0, 0, tiled=True)  4.31 us
  transfers between devices with their start and end apart: 8, of which 7 were waited for; matrix products, arithmetic and copies ran while one was open for 2% of the time, Pallas kernels for 6%

profile of v6, /device:TPU:40, one launch (start us, length us, event | category | flops | bytes accessed | tf_op | source)
XLA Modules:
  0.0 128.2 jit_solution(817017605259869905)
XLA Ops:
  0.0 1.0 copy-done
  1.0 0.9 first_tile.1
  1.9 4.3 %all-to-all-start = ((f32[8,128,128]{2,1,0:T(8,128)}), f32[8,128,128]{2,1,0:T(8,128)S(1)}, u32[]{:S(2)}, u32[]{:S(2)}) async-start(f32[8,128,128]{2,1,0:T(8,128)} %first_tile.1), calls=%async_computation | async-start | bytes 1048576 | tf_op jit(solution)/shard_map/all_to_all | solution.py:231
  6.2 10.3 %all-to-all-done = f32[8,128,128]{2,1,0:T(8,128)S(1)} async-done(((f32[8,128,128]{2,1,0:T(8,128)}), f32[8,128,128]{2,1,0:T(8,128)S(1)}, u32[]{:S(2)}, u32[]{:S(2)}) %all-to-all-start) | async-done | bytes 524320 | tf_op jit(solution)/shard_map/all_to_all | solution.py:231
  16.6 1.9 %collective-permute-start = (f32[128,128]{1,0:T(8,128)S(1)}, f32[128,128]{1,0:T(8,128)S(1)}, u32[]{:S(2)}, u32[]{:S(2)}) collective-permute-start(f32[128,128]{1,0:T(8,128)S(1)} %get-tuple-element.6), channel_id=1, source_target_pairs={{0,32},{1,24},{2,40},{3,16},{6,48},{7,8},{4,56},{5,0},{8,41},{9,33... | collective-permute-start | bytes 196616 | tf_op jit(solution)/shard_map/ppermute | solution.py:234
  18.5 8.8 %collective-permute-done = f32[128,128]{1,0:T(8,128)S(1)} collective-permute-done((f32[128,128]{1,0:T(8,128)S(1)}, f32[128,128]{1,0:T(8,128)S(1)}, u32[]{:S(2)}, u32[]{:S(2)}) %collective-permute-start) | collective-permute-done | bytes 65568 | tf_op jit(solution)/shard_map/ppermute | solution.py:234
  27.3 0.1 copy.12
  27.4 0.8 broadcast_in_dim.10
  28.2 10.3 %all-to-all-start.1 = ((f32[8,128,128]{1,2,0:T(8,128)}), f32[8,128,128]{1,2,0:T(8,128)S(1)}, u32[]{:S(2)}, u32[]{:S(2)}) async-start(f32[8,128,128]{1,2,0:T(8,128)} %broadcast_in_dim.10), calls=%async_computation.1 | async-start | bytes 1048576 | tf_op jit(solution)/shard_map/all_to_all | solution.py:27
  38.6 17.0 %all-to-all-done.1 = f32[8,128,128]{1,2,0:T(8,128)S(1)} async-done(((f32[8,128,128]{1,2,0:T(8,128)}), f32[8,128,128]{1,2,0:T(8,128)S(1)}, u32[]{:S(2)}, u32[]{:S(2)}) %all-to-all-start.1) | async-done | bytes 524320 | tf_op jit(solution)/shard_map/all_to_all | solution.py:27
  55.5 0.1 constant_dynamic-slice_fusion
  55.6 0.1 copy.15
  55.7 0.6 convolution_bitcast_fusion.1.gram_ref
  56.3 0.5 copy-done.1
  56.7 0.6 convolution_bitcast_fusion.2.part_ref
  57.3 0.1 shared.1
  57.4 1.0 broadcast_in_dim.11
  58.4 3.6 %all-to-all-start.2 = ((f32[8,240,128]{2,1,0:T(8,128)}), f32[8,240,128]{2,1,0:T(8,128)S(1)}, u32[]{:S(2)}, u32[]{:S(2)}) async-start(f32[8,240,128]{2,1,0:T(8,128)} %broadcast_in_dim.11), calls=%async_computation.2 | async-start | bytes 1966080 | tf_op jit(solution)/shard_map/all_to_all | solution.py:27
  62.0 4.6 %collective-permute-start.2 = (f32[128,128]{1,0:T(8,128)S(1)}, f32[128,128]{1,0:T(8,128)S(1)}, u32[]{:S(2)}, u32[]{:S(2)}) collective-permute-start(f32[128,128]{1,0:T(8,128)S(1)} %get-tuple-element.5), channel_id=1, source_target_pairs={{0,32},{1,24},{2,40},{3,16},{6,48},{7,8},{4,56},{5,0},{8,41},{9,33... | collective-permute-start | bytes 196616 | tf_op jit(solution)/shard_map/ppermute | solution.py:236
  66.6 11.9 %all-to-all-done.2 = f32[8,240,128]{2,1,0:T(8,128)S(1)} async-done(((f32[8,240,128]{2,1,0:T(8,128)}), f32[8,240,128]{2,1,0:T(8,128)S(1)}, u32[]{:S(2)}, u32[]{:S(2)}) %all-to-all-start.2) | async-done | bytes 983072 | tf_op jit(solution)/shard_map/all_to_all | solution.py:27
  78.6 1.9 %collective-permute-start.1 = (f32[128,128]{1,0:T(8,128)S(1)}, f32[128,128]{1,0:T(8,128)S(1)}, u32[]{:S(2)}, u32[]{:S(2)}) collective-permute-start(f32[128,128]{1,0:T(8,128)S(1)} %slice.87), channel_id=1, source_target_pairs={{0,32},{1,24},{2,40},{3,16},{6,48},{7,8},{4,56},{5,0},{8,41},{9,33... | collective-permute-start | bytes 196616 | tf_op jit(solution)/shard_map/ppermute | solution.py:247
  80.6 4.0 %shard_map.17 = f32[128,128]{1,0:T(8,128)S(1)} custom-call(f32[64,128]{1,0:T(8,128)S(1)} %slice.85.upper_ref, f32[32,128]{1,0:T(8,128)S(1)} %slice.86.corner_ref), custom_call_target="tpu_custom_call" | custom-call | bytes 30000000 | tf_op jit(solution)/shard_map/pallas_call | solution.py:207
  84.6 4.1 %collective-permute-done.1 = f32[128,128]{1,0:T(8,128)S(1)} collective-permute-done((f32[128,128]{1,0:T(8,128)S(1)}, f32[128,128]{1,0:T(8,128)S(1)}, u32[]{:S(2)}, u32[]{:S(2)}) %collective-permute-start.1) | collective-permute-done | bytes 65568 | tf_op jit(solution)/shard_map/ppermute | solution.py:247
  88.7 0.3 convolution_add_fusion.4
  89.0 0.9 broadcast_in_dim.12
  89.8 3.5 %all-to-all-start.3 = ((f32[8,144,128]{2,1,0:T(8,128)}), f32[8,144,128]{2,1,0:T(8,128)S(1)}, u32[]{:S(2)}, u32[]{:S(2)}) async-start(f32[8,144,128]{2,1,0:T(8,128)} %broadcast_in_dim.12), calls=%async_computation.3 | async-start | bytes 1179648 | tf_op jit(solution)/shard_map/all_to_all | solution.py:27
  93.4 0.3 convolution_add_fusion.5
  93.7 0.3 convolution_add_fusion.2
  94.0 1.0 convolution_add_fusion
  95.0 16.6 %all-to-all-done.3 = f32[8,144,128]{2,1,0:T(8,128)S(1)} async-done(((f32[8,144,128]{2,1,0:T(8,128)}), f32[8,144,128]{2,1,0:T(8,128)S(1)}, u32[]{:S(2)}, u32[]{:S(2)}) %all-to-all-start.3) | async-done | bytes 589856 | tf_op jit(solution)/shard_map/all_to_all | solution.py:27
  111.6 0.6 convolution_bitcast_fusion
  112.2 0.1 fusion.19
  112.3 0.1 maximum_maximum_fusion
  112.3 0.8 broadcast_in_dim.13
  113.1 3.6 %all-to-all-start.4 = ((f32[8,96,128]{2,1,0:T(8,128)}), f32[8,96,128]{2,1,0:T(8,128)S(1)}, u32[]{:S(2)}, u32[]{:S(2)}) async-start(f32[8,96,128]{2,1,0:T(8,128)} %broadcast_in_dim.13), calls=%async_computation.4 | async-start | bytes 786432 | tf_op jit(solution)/shard_map/all_to_all | solution.py:27
  116.8 0.3 convolution_add_fusion.3.matrix_ref
  117.0 4.1 %shard_map.18 = f32[128,128]{1,0:T(8,128)S(1)} custom-call(f32[128,128]{1,0:T(8,128)S(1)} %convolution_add_fusion.3.matrix_ref), custom_call_target="tpu_custom_call" | custom-call | bytes 30000000 | tf_op jit(solution)/shard_map/pallas_call | solution.py:207
  121.1 0.3 fusion.20
  121.4 0.5 convolution_subtract_fusion.1
  121.9 0.2 fusion.21
  122.1 3.3 %all-to-all-done.4 = f32[8,96,128]{2,1,0:T(8,128)S(1)} async-done(((f32[8,96,128]{2,1,0:T(8,128)}), f32[8,96,128]{2,1,0:T(8,128)S(1)}, u32[]{:S(2)}, u32[]{:S(2)}) %all-to-all-start.4) | async-done | bytes 393248 | tf_op jit(solution)/shard_map/all_to_all | solution.py:27
  125.4 0.3 fusion.11
  125.8 0.1 fusion.18
  125.9 0.3 fusion.14
  126.2 0.3 convolution_add_fusion.1
  126.5 0.2 fusion.1
  126.7 0.4 fusion
  127.1 1.1 copy.19
  (18 shorter events, 0.2 us)
Async XLA Ops:
  0.0 1.0 copy-start
  1.9 14.6 %all-to-all-start = ((f32[8,128,128]{2,1,0:T(8,128)}), f32[8,128,128]{2,1,0:T(8,128)S(1)}, u32[]{:S(2)}, u32[]{:S(2)}) async-start(f32[8,128,128]{2,1,0:T(8,128)} %first_tile.1), calls=%async_computation | async-start | bytes 1048576 | tf_op jit(solution)/shard_map/all_to_all | solution.py:231
  16.6 10.7 %collective-permute-start = (f32[128,128]{1,0:T(8,128)S(1)}, f32[128,128]{1,0:T(8,128)S(1)}, u32[]{:S(2)}, u32[]{:S(2)}) collective-permute-start(f32[128,128]{1,0:T(8,128)S(1)} %get-tuple-element.6), channel_id=1, source_target_pairs={{0,32},{1,24},{2,40},{3,16},{6,48},{7,8},{4,56},{5,0},{8,41},{9,33... | collective-permute-start | bytes 196616 | tf_op jit(solution)/shard_map/ppermute | solution.py:234
  28.2 27.3 %all-to-all-start.1 = ((f32[8,128,128]{1,2,0:T(8,128)}), f32[8,128,128]{1,2,0:T(8,128)S(1)}, u32[]{:S(2)}, u32[]{:S(2)}) async-start(f32[8,128,128]{1,2,0:T(8,128)} %broadcast_in_dim.10), calls=%async_computation.1 | async-start | bytes 1048576 | tf_op jit(solution)/shard_map/all_to_all | solution.py:27
  55.7 1.1 copy-start.1
  58.4 20.1 %all-to-all-start.2 = ((f32[8,240,128]{2,1,0:T(8,128)}), f32[8,240,128]{2,1,0:T(8,128)S(1)}, u32[]{:S(2)}, u32[]{:S(2)}) async-start(f32[8,240,128]{2,1,0:T(8,128)} %broadcast_in_dim.11), calls=%async_computation.2 | async-start | bytes 1966080 | tf_op jit(solution)/shard_map/all_to_all | solution.py:27
  62.0 22.6 %collective-permute-start.2 = (f32[128,128]{1,0:T(8,128)S(1)}, f32[128,128]{1,0:T(8,128)S(1)}, u32[]{:S(2)}, u32[]{:S(2)}) collective-permute-start(f32[128,128]{1,0:T(8,128)S(1)} %get-tuple-element.5), channel_id=1, source_target_pairs={{0,32},{1,24},{2,40},{3,16},{6,48},{7,8},{4,56},{5,0},{8,41},{9,33... | collective-permute-start | bytes 196616 | tf_op jit(solution)/shard_map/ppermute | solution.py:236
  78.6 10.1 %collective-permute-start.1 = (f32[128,128]{1,0:T(8,128)S(1)}, f32[128,128]{1,0:T(8,128)S(1)}, u32[]{:S(2)}, u32[]{:S(2)}) collective-permute-start(f32[128,128]{1,0:T(8,128)S(1)} %slice.87), channel_id=1, source_target_pairs={{0,32},{1,24},{2,40},{3,16},{6,48},{7,8},{4,56},{5,0},{8,41},{9,33... | collective-permute-start | bytes 196616 | tf_op jit(solution)/shard_map/ppermute | solution.py:247
  89.8 21.8 %all-to-all-start.3 = ((f32[8,144,128]{2,1,0:T(8,128)}), f32[8,144,128]{2,1,0:T(8,128)S(1)}, u32[]{:S(2)}, u32[]{:S(2)}) async-start(f32[8,144,128]{2,1,0:T(8,128)} %broadcast_in_dim.12), calls=%async_computation.3 | async-start | bytes 1179648 | tf_op jit(solution)/shard_map/all_to_all | solution.py:27
  113.1 12.3 %all-to-all-start.4 = ((f32[8,96,128]{2,1,0:T(8,128)}), f32[8,96,128]{2,1,0:T(8,128)S(1)}, u32[]{:S(2)}, u32[]{:S(2)}) async-start(f32[8,96,128]{2,1,0:T(8,128)} %broadcast_in_dim.13), calls=%async_computation.4 | async-start | bytes 786432 | tf_op jit(solution)/shard_map/all_to_all | solution.py:27

commit v7 on v6

--- a/solution.py
+++ b/solution.py
@@ -40,8 +40,10 @@
     return (rows == lanes).astype(jnp.float32)
 
 
-def first_kernel(matrix_ref, out_ref, tile, sems):
-    tile[...] = matrix_ref[0, :, 0, :]
+def first_kernel(matrix_ref, out_ref, tile, sem, sems):
+    take = pltpu.make_async_copy(matrix_ref.at[0, :, 0, :], tile, sem)
+    take.start()
+    take.wait()
     copies = [
         pltpu.make_async_copy(tile, out_ref.at[i], sems.at[i])
         for i in range(out_ref.shape[0])
@@ -57,15 +59,16 @@
     return pl.pallas_call(
         first_kernel,
         out_shape=jax.ShapeDtypeStruct((count, width, width), jnp.float32),
-        in_specs=[pl.BlockSpec(memory_space=pltpu.VMEM)],
+        in_specs=[pl.BlockSpec(memory_space=pltpu.HBM)],
         out_specs=pl.BlockSpec(memory_space=pl.ANY),
         scratch_shapes=[
             pltpu.VMEM((width, width), jnp.float32),
+            pltpu.SemaphoreType.DMA,
             pltpu.SemaphoreType.DMA((count,)),
         ],
         compiler_params=pltpu.CompilerParams(vmem_limit_bytes=2 << 20),
         name="first_tile",
-    )(matrix)
+    )(pltpu.with_memory_space_constraint(matrix, pltpu.HBM))
 
 
 def shared_kernel(part_ref, gram_ref, head_ref, out_ref):
@@ -232,10 +235,11 @@
     panel_row = first[0] * (row != 0).astype(jnp.float32)
     next_row = first[1]
     panel_own = lax.ppermute(panel_row, PLANE, swap)
+    near = lax.optimization_barrier(jnp.transpose(local, (1, 0, 2)))
     panel = spread(panel_own, "z", count)
     next_own = lax.ppermute(next_row, PLANE, swap)
 
-    part = product(local, panel, ((1, 2), (0, 1)))
+    part = product(near, panel, ((0, 2), (0, 1)))
     gram_part = product(panel, panel, ((0, 1), (0, 1)))
     head_slice = lax.dynamic_slice_in_dim(panel[0], depth * piece, piece, 0)
     shared = shared_call(part, gram_part, head_slice)
@@ -267,7 +271,7 @@
     )
     turned_row = product(refl_row, coupling, ((1,), (1,)))
     half_row = product(image_row, coupling, ((1,), (0,)))
-    partial = lax.optimization_barrier(local - product(turned_row, image, ((1,), (2,)), FAST))
+    partial = lax.optimization_barrier(near.transpose(1, 0, 2) - product(turned_row, image, ((1,), (2,)), FAST))
 
     upper = jnp.sum(came[:, :half], axis=0)
     corner = came[:, half:]

time: 129 us -> 128 us (level)
  local copies, waits for them, and re-layouts: 6.5 us -> 5.1 us
    unnamed x4 -> x3, local copies, waits for them, and re-layouts: 1.5 us -> 0.11 us
where the time goes in v7:
time: 128 us
  waiting for transfers between devices  72 us (56%)
  starting transfers between devices  33.9 us (26%)
  Pallas kernels  9.83 us (8%)
  matrix products  6.2 us (5%)
  local copies, waits for them, and re-layouts  5.1 us (4%)
    all_to_all x4, waiting for transfers between devices, spread(): return lax.all_to_all(whole, axis, 0, 0, tiled=True)  48.8 us
    all_to_all x4, starting transfers between devices, spread(): return lax.all_to_all(whole, axis, 0, 0, tiled=True)  21.2 us
    all_to_all x1, waiting for transfers between devices, per_device(): first = lax.all_to_all(first_call(matrix, side), COL, 0, 0, tiled=True)  10.3 us
    ppermute x1, waiting for transfers between devices, per_device(): panel_own = lax.ppermute(panel_row, PLANE, swap)  8.77 us
    pallas_call x2, Pallas kernels, factor_call(): pl.pallas_call(kernel, out_shape=jax.ShapeDtypeStruct((width, width), jnp...  8.05 us
    dot_general x16, matrix products, product(): lax.dot_general(left, right, (contract, ((), ())), precision=precision, p...  6.2 us
    ppermute x1, starting transfers between devices, per_device(): next_own = lax.ppermute(next_row, PLANE, swap)  4.59 us
    all_to_all x1, starting transfers between devices, per_device(): first = lax.all_to_all(first_call(matrix, side), COL, 0, 0, tiled=True)  4.31 us
  transfers between devices with their start and end apart: 8, of which 7 were waited for; matrix products, arithmetic and copies ran while one was open for 2% of the time, Pallas kernels for 6%

profile of v7, /device:TPU:40, one launch (start us, length us, event | category | flops | bytes accessed | tf_op | source)
XLA Modules:
  0.0 127.6 jit_solution(14165649700676085121)
XLA Ops:
  0.0 1.7 %first_tile.1 = f32[8,128,128]{2,1,0:T(8,128)} custom-call(f32[1,128,8,128]{3,2,1,0:T(8,128)} %matrix_ref.1), custom_call_target="tpu_custom_call" | custom-call | tf_op jit(solution)/shard_map/first_tile/pallas_call | solution.py:59
  1.7 4.3 %all-to-all-start = ((f32[8,128,128]{2,1,0:T(8,128)}), f32[8,128,128]{2,1,0:T(8,128)S(1)}, u32[]{:S(2)}, u32[]{:S(2)}) async-start(f32[8,128,128]{2,1,0:T(8,128)} %first_tile.1), calls=%async_computation | async-start | bytes 1048576 | tf_op jit(solution)/shard_map/all_to_all | solution.py:234
  6.0 10.3 %all-to-all-done = f32[8,128,128]{2,1,0:T(8,128)S(1)} async-done(((f32[8,128,128]{2,1,0:T(8,128)}), f32[8,128,128]{2,1,0:T(8,128)S(1)}, u32[]{:S(2)}, u32[]{:S(2)}) %all-to-all-start) | async-done | bytes 524320 | tf_op jit(solution)/shard_map/all_to_all | solution.py:234
  16.3 1.9 %collective-permute-start = (f32[128,128]{1,0:T(8,128)S(1)}, f32[128,128]{1,0:T(8,128)S(1)}, u32[]{:S(2)}, u32[]{:S(2)}) collective-permute-start(f32[128,128]{1,0:T(8,128)S(1)} %get-tuple-element.6), channel_id=1, source_target_pairs={{0,32},{1,24},{2,40},{3,16},{6,48},{7,8},{4,56},{5,0},{8,41},{9,33... | collective-permute-start | bytes 196616 | tf_op jit(solution)/shard_map/ppermute | solution.py:237
  18.3 8.8 %collective-permute-done = f32[128,128]{1,0:T(8,128)S(1)} collective-permute-done((f32[128,128]{1,0:T(8,128)S(1)}, f32[128,128]{1,0:T(8,128)S(1)}, u32[]{:S(2)}, u32[]{:S(2)}) %collective-permute-start) | collective-permute-done | bytes 65568 | tf_op jit(solution)/shard_map/ppermute | solution.py:237
  27.1 0.1 copy.12
  27.2 0.8 broadcast_in_dim.10
  28.0 10.4 %all-to-all-start.1 = ((f32[8,128,128]{1,2,0:T(8,128)}), f32[8,128,128]{1,2,0:T(8,128)S(1)}, u32[]{:S(2)}, u32[]{:S(2)}) async-start(f32[8,128,128]{1,2,0:T(8,128)} %broadcast_in_dim.10), calls=%async_computation.1 | async-start | bytes 1048576 | tf_op jit(solution)/shard_map/all_to_all | solution.py:27
  38.5 0.1 copy.28
  38.6 16.8 %all-to-all-done.1 = f32[8,128,128]{1,2,0:T(8,128)S(1)} async-done(((f32[8,128,128]{1,2,0:T(8,128)}), f32[8,128,128]{1,2,0:T(8,128)S(1)}, u32[]{:S(2)}, u32[]{:S(2)}) %all-to-all-start.1) | async-done | bytes 524320 | tf_op jit(solution)/shard_map/all_to_all | solution.py:27
  55.4 0.1 constant_dynamic-slice_fusion
  55.5 0.1 copy.15
  55.6 0.6 convolution_bitcast_fusion.1.gram_ref
  56.2 0.6 convolution_bitcast_fusion.2.part_ref
  56.8 0.1 shared.1
  56.8 1.0 broadcast_in_dim.11
  57.8 3.6 %all-to-all-start.2 = ((f32[8,240,128]{2,1,0:T(8,128)}), f32[8,240,128]{2,1,0:T(8,128)S(1)}, u32[]{:S(2)}, u32[]{:S(2)}) async-start(f32[8,240,128]{2,1,0:T(8,128)} %broadcast_in_dim.11), calls=%async_computation.2 | async-start | bytes 1966080 | tf_op jit(solution)/shard_map/all_to_all | solution.py:27
  61.4 4.6 %collective-permute-start.2 = (f32[128,128]{1,0:T(8,128)S(1)}, f32[128,128]{1,0:T(8,128)S(1)}, u32[]{:S(2)}, u32[]{:S(2)}) collective-permute-start(f32[128,128]{1,0:T(8,128)S(1)} %get-tuple-element.5), channel_id=1, source_target_pairs={{0,32},{1,24},{2,40},{3,16},{6,48},{7,8},{4,56},{5,0},{8,41},{9,33... | collective-permute-start | bytes 196616 | tf_op jit(solution)/shard_map/ppermute | solution.py:240
  66.0 11.9 %all-to-all-done.2 = f32[8,240,128]{2,1,0:T(8,128)S(1)} async-done(((f32[8,240,128]{2,1,0:T(8,128)}), f32[8,240,128]{2,1,0:T(8,128)S(1)}, u32[]{:S(2)}, u32[]{:S(2)}) %all-to-all-start.2) | async-done | bytes 983072 | tf_op jit(solution)/shard_map/all_to_all | solution.py:27
  78.0 1.9 %collective-permute-start.1 = (f32[128,128]{1,0:T(8,128)S(1)}, f32[128,128]{1,0:T(8,128)S(1)}, u32[]{:S(2)}, u32[]{:S(2)}) collective-permute-start(f32[128,128]{1,0:T(8,128)S(1)} %slice.87), channel_id=1, source_target_pairs={{0,32},{1,24},{2,40},{3,16},{6,48},{7,8},{4,56},{5,0},{8,41},{9,33... | collective-permute-start | bytes 196616 | tf_op jit(solution)/shard_map/ppermute | solution.py:251
  80.0 4.0 %shard_map.17 = f32[128,128]{1,0:T(8,128)S(1)} custom-call(f32[64,128]{1,0:T(8,128)S(1)} %slice.85.upper_ref, f32[32,128]{1,0:T(8,128)S(1)} %slice.86.corner_ref), custom_call_target="tpu_custom_call" | custom-call | bytes 30000000 | tf_op jit(solution)/shard_map/pallas_call | solution.py:210
  84.0 0.0 collective-permute-done.2
  84.0 4.1 %collective-permute-done.1 = f32[128,128]{1,0:T(8,128)S(1)} collective-permute-done((f32[128,128]{1,0:T(8,128)S(1)}, f32[128,128]{1,0:T(8,128)S(1)}, u32[]{:S(2)}, u32[]{:S(2)}) %collective-permute-start.1) | collective-permute-done | bytes 65568 | tf_op jit(solution)/shard_map/ppermute | solution.py:251
  88.1 0.3 convolution_add_fusion.4
  88.4 0.9 broadcast_in_dim.12
  89.2 3.5 %all-to-all-start.3 = ((f32[8,144,128]{2,1,0:T(8,128)}), f32[8,144,128]{2,1,0:T(8,128)S(1)}, u32[]{:S(2)}, u32[]{:S(2)}) async-start(f32[8,144,128]{2,1,0:T(8,128)} %broadcast_in_dim.12), calls=%async_computation.3 | async-start | bytes 1179648 | tf_op jit(solution)/shard_map/all_to_all | solution.py:27
  92.8 0.3 convolution_add_fusion.5
  93.1 0.3 convolution_add_fusion.2
  93.4 1.0 convolution_add_fusion
  94.4 16.6 %all-to-all-done.3 = f32[8,144,128]{2,1,0:T(8,128)S(1)} async-done(((f32[8,144,128]{2,1,0:T(8,128)}), f32[8,144,128]{2,1,0:T(8,128)S(1)}, u32[]{:S(2)}, u32[]{:S(2)}) %all-to-all-start.3) | async-done | bytes 589856 | tf_op jit(solution)/shard_map/all_to_all | solution.py:27
  111.0 0.6 convolution_bitcast_fusion
  111.6 0.1 fusion.17
  111.7 0.1 maximum_maximum_fusion
  111.8 0.8 broadcast_in_dim.13
  112.5 3.6 %all-to-all-start.4 = ((f32[8,96,128]{2,1,0:T(8,128)}), f32[8,96,128]{2,1,0:T(8,128)S(1)}, u32[]{:S(2)}, u32[]{:S(2)}) async-start(f32[8,96,128]{2,1,0:T(8,128)} %broadcast_in_dim.13), calls=%async_computation.4 | async-start | bytes 786432 | tf_op jit(solution)/shard_map/all_to_all | solution.py:27
  116.2 0.3 convolution_add_fusion.3.matrix_ref
  116.5 4.1 %shard_map.18 = f32[128,128]{1,0:T(8,128)S(1)} custom-call(f32[128,128]{1,0:T(8,128)S(1)} %convolution_add_fusion.3.matrix_ref), custom_call_target="tpu_custom_call" | custom-call | bytes 30000000 | tf_op jit(solution)/shard_map/pallas_call | solution.py:210
  120.5 0.3 fusion.18
  120.8 0.4 convolution_subtract_fusion.1
  121.2 0.2 fusion.19
  121.4 3.4 %all-to-all-done.4 = f32[8,96,128]{2,1,0:T(8,128)S(1)} async-done(((f32[8,96,128]{2,1,0:T(8,128)}), f32[8,96,128]{2,1,0:T(8,128)S(1)}, u32[]{:S(2)}, u32[]{:S(2)}) %all-to-all-start.4) | async-done | bytes 393248 | tf_op jit(solution)/shard_map/all_to_all | solution.py:27
  124.8 0.3 fusion.9
  125.2 0.1 fusion.16
  125.3 0.3 fusion.12
  125.6 0.3 convolution_add_fusion.1
  125.9 0.2 fusion.1
  126.1 0.4 fusion
  126.5 1.1 copy.19
  (17 shorter events, 0.2 us)
Async XLA Ops:
  1.7 14.6 %all-to-all-start = ((f32[8,128,128]{2,1,0:T(8,128)}), f32[8,128,128]{2,1,0:T(8,128)S(1)}, u32[]{:S(2)}, u32[]{:S(2)}) async-start(f32[8,128,128]{2,1,0:T(8,128)} %first_tile.1), calls=%async_computation | async-start | bytes 1048576 | tf_op jit(solution)/shard_map/all_to_all | solution.py:234
  16.3 10.7 %collective-permute-start = (f32[128,128]{1,0:T(8,128)S(1)}, f32[128,128]{1,0:T(8,128)S(1)}, u32[]{:S(2)}, u32[]{:S(2)}) collective-permute-start(f32[128,128]{1,0:T(8,128)S(1)} %get-tuple-element.6), channel_id=1, source_target_pairs={{0,32},{1,24},{2,40},{3,16},{6,48},{7,8},{4,56},{5,0},{8,41},{9,33... | collective-permute-start | bytes 196616 | tf_op jit(solution)/shard_map/ppermute | solution.py:237
  28.0 10.5 %copy-start = (f32[1,128,8,128]{3,2,1,0:T(8,128)S(1)}, f32[1,128,8,128]{3,2,1,0:T(8,128)}, u32[]{:S(2)}) copy-start(f32[1,128,8,128]{3,2,1,0:T(8,128)} %matrix_ref.1) | copy-start | bytes 1572868
  28.0 27.4 %all-to-all-start.1 = ((f32[8,128,128]{1,2,0:T(8,128)}), f32[8,128,128]{1,2,0:T(8,128)S(1)}, u32[]{:S(2)}, u32[]{:S(2)}) async-start(f32[8,128,128]{1,2,0:T(8,128)} %broadcast_in_dim.10), calls=%async_computation.1 | async-start | bytes 1048576 | tf_op jit(solution)/shard_map/all_to_all | solution.py:27
  57.8 20.1 %all-to-all-start.2 = ((f32[8,240,128]{2,1,0:T(8,128)}), f32[8,240,128]{2,1,0:T(8,128)S(1)}, u32[]{:S(2)}, u32[]{:S(2)}) async-start(f32[8,240,128]{2,1,0:T(8,128)} %broadcast_in_dim.11), calls=%async_computation.2 | async-start | bytes 1966080 | tf_op jit(solution)/shard_map/all_to_all | solution.py:27
  61.4 22.6 %collective-permute-start.2 = (f32[128,128]{1,0:T(8,128)S(1)}, f32[128,128]{1,0:T(8,128)S(1)}, u32[]{:S(2)}, u32[]{:S(2)}) collective-permute-start(f32[128,128]{1,0:T(8,128)S(1)} %get-tuple-element.5), channel_id=1, source_target_pairs={{0,32},{1,24},{2,40},{3,16},{6,48},{7,8},{4,56},{5,0},{8,41},{9,33... | collective-permute-start | bytes 196616 | tf_op jit(solution)/shard_map/ppermute | solution.py:240
  78.0 10.1 %collective-permute-start.1 = (f32[128,128]{1,0:T(8,128)S(1)}, f32[128,128]{1,0:T(8,128)S(1)}, u32[]{:S(2)}, u32[]{:S(2)}) collective-permute-start(f32[128,128]{1,0:T(8,128)S(1)} %slice.87), channel_id=1, source_target_pairs={{0,32},{1,24},{2,40},{3,16},{6,48},{7,8},{4,56},{5,0},{8,41},{9,33... | collective-permute-start | bytes 196616 | tf_op jit(solution)/shard_map/ppermute | solution.py:251
  89.2 21.8 %all-to-all-start.3 = ((f32[8,144,128]{2,1,0:T(8,128)}), f32[8,144,128]{2,1,0:T(8,128)S(1)}, u32[]{:S(2)}, u32[]{:S(2)}) async-start(f32[8,144,128]{2,1,0:T(8,128)} %broadcast_in_dim.12), calls=%async_computation.3 | async-start | bytes 1179648 | tf_op jit(solution)/shard_map/all_to_all | solution.py:27
  112.5 12.3 %all-to-all-start.4 = ((f32[8,96,128]{2,1,0:T(8,128)}), f32[8,96,128]{2,1,0:T(8,128)S(1)}, u32[]{:S(2)}, u32[]{:S(2)}) async-start(f32[8,96,128]{2,1,0:T(8,128)} %broadcast_in_dim.13), calls=%async_computation.4 | async-start | bytes 786432 | tf_op jit(solution)/shard_map/all_to_all | solution.py:27

commit v8 on v7

--- a/solution.py
+++ b/solution.py
@@ -71,7 +71,7 @@
     )(pltpu.with_memory_space_constraint(matrix, pltpu.HBM))
 
 
-def shared_kernel(part_ref, gram_ref, head_ref, out_ref):
+def shared_kernel(part_ref, gram_ref, out_ref):
     width = part_ref.shape[1]
     half, quarter = width // 2, width // 4
     gram = gram_ref[...]
@@ -79,19 +79,18 @@
     out_ref[width : width + half, :] = gram[:half]
     corner = [gram[half : half + quarter, half:], gram[half + quarter :, half:]]
     low = width + half
-    out_ref[low : low + quarter, :] = jnp.concatenate(corner, axis=1)
-    out_ref[low + quarter :, :] = head_ref[...]
-
-
-def shared_call(part, gram, head):
+    out_ref[low:, :] = jnp.concatenate(corner, axis=1)
+
+
+def shared_call(part, gram):
     width = part.shape[1]
-    tall = width + width // 2 + width // 4 + head.shape[0]
+    tall = width + width // 2 + width // 4
     return pl.pallas_call(
         shared_kernel,
         out_shape=jax.ShapeDtypeStruct((tall, width), jnp.float32),
         compiler_params=pltpu.CompilerParams(vmem_limit_bytes=2 << 20),
         name="shared",
-    )(part, gram, head)
+    )(part, gram)
 
 
 def columns_of(rows, low, width):
@@ -221,14 +220,16 @@
 def per_device(matrix):
     _, width, count, _ = matrix.shape
     side = lax.axis_size("y")
-    depth = lax.axis_index("z")
-    row = depth * side + lax.axis_index("y")
+    row = lax.axis_index("z") * side + lax.axis_index("y")
     col = lax.axis_index(COL)
     swap = transposition(side)
-    piece, half = width // side, width // 2
+    half = width // 2
     local = matrix[0]
 
     on_row = lax.optimization_barrier(unit(width) * (row == 1))
+    on_col = lax.optimization_barrier((col == 1).astype(jnp.float32))
+    at_col = (jnp.arange(count) == 0).astype(jnp.float32) * on_col
+    at_col = lax.optimization_barrier(at_col)
     identity = unit(width)
 
     first = lax.all_to_all(first_call(matrix, side), COL, 0, 0, tiled=True)
@@ -241,12 +242,8 @@
 
     part = product(near, panel, ((0, 2), (0, 1)))
     gram_part = product(panel, panel, ((0, 1), (0, 1)))
-    head_slice = lax.dynamic_slice_in_dim(panel[0], depth * piece, piece, 0)
-    shared = shared_call(part, gram_part, head_slice)
-    came = spread(shared, COL, side)
-    tall = shared.shape[0] - piece
-    total = jnp.sum(came[:, :tall], axis=0)
-    head_slice = came[1, tall:]
+    shared = shared_call(part, gram_part)
+    total = jnp.sum(spread(shared, COL, side), axis=0)
     mixed_row = total[:width]
     mixed_own = lax.ppermute(mixed_row, PLANE, swap)
     inverse = factor_call(
@@ -254,11 +251,14 @@
     )
 
     image_own = product(mixed_own, inverse, ((1,), (1,))) + next_own
-    came = spread(jnp.concatenate([image_own, head_slice], axis=0), "z", count)
-    image = came[:, :width]
-    head = came[:, width:].reshape(width, width)
-
-    at_col = ((jnp.arange(count) == 0) & (col == 1)).astype(jnp.float32)
+    image = spread(image_own, "z", count)
+
+    head = lax.optimization_barrier(panel[0] * on_col)
+    head = head + lax.ppermute(head, "k", [(1, 0)])
+    head = head + lax.ppermute(head, "x", [(0, 2)])
+    came = lax.ppermute(head, "x", [(0, 1), (2, 3)])
+    head = lax.optimization_barrier(head + came)
+
     refl_row = product(panel_row, inverse, ((1,), (1,))) + on_row
     image_row = product(mixed_row, inverse, ((1,), (1,))) + next_row
     refl = product(panel, inverse, ((2,), (1,))) + identity[None] * at_col[:, None, None]

time: 128 us -> 134 us (1.047)
  the two profiles are of different devices: /device:TPU:40 before, /device:TPU:1 now
where the time goes in v8:
time: 134 us; the launch traced here: 132 us
  starting transfers between devices  59.2 us (44%)
  waiting for transfers between devices  51.2 us (38%)
  Pallas kernels  9.82 us (7%)
  matrix products  6.11 us (5%)
  local copies, waits for them, and re-layouts  4.91 us (4%)
    all_to_all x4, waiting for transfers between devices, spread(): return lax.all_to_all(whole, axis, 0, 0, tiled=True)  31.7 us
    all_to_all x4, starting transfers between devices, spread(): return lax.all_to_all(whole, axis, 0, 0, tiled=True)  30.3 us
    all_to_all x1, starting transfers between devices, per_device(): first = lax.all_to_all(first_call(matrix, side), COL, 0, 0, tiled=True)  10.2 us
    all_to_all x1, waiting for transfers between devices, per_device(): first = lax.all_to_all(first_call(matrix, side), COL, 0, 0, tiled=True)  9.38 us
    pallas_call x2, Pallas kernels, factor_call(): pl.pallas_call(kernel, out_shape=jax.ShapeDtypeStruct((width, width), jnp...  8.05 us
    ppermute x1, starting transfers between devices, per_device(): next_own = lax.ppermute(next_row, PLANE, swap)  6.42 us
    dot_general x16, matrix products, product(): lax.dot_general(left, right, (contract, ((), ())), precision=precision, p...  6.11 us
    ppermute x1, waiting for transfers between devices, per_device(): panel_own = lax.ppermute(panel_row, PLANE, swap)  5.64 us
  transfers between devices with their start and end apart: 11, of which 7 were waited for; matrix products, arithmetic and copies ran while one was open for 2% of the time, Pallas kernels for 6%

profile of v8, /device:TPU:1, one launch (start us, length us, event | category | flops | bytes accessed | tf_op | source)
XLA Modules:
  0.0 131.9 jit_solution(4207926003895006221)
XLA Ops:
  0.0 1.7 %first_tile.1 = f32[8,128,128]{2,1,0:T(8,128)} custom-call(f32[1,128,8,128]{3,2,1,0:T(8,128)} %matrix_ref.1), custom_call_target="tpu_custom_call" | custom-call | tf_op jit(solution)/shard_map/first_tile/pallas_call | solution.py:59
  1.7 10.2 %all-to-all-start = ((f32[8,128,128]{2,1,0:T(8,128)}), f32[8,128,128]{2,1,0:T(8,128)S(1)}, u32[]{:S(2)}, u32[]{:S(2)}) async-start(f32[8,128,128]{2,1,0:T(8,128)} %first_tile.1), calls=%async_computation | async-start | bytes 1048576 | tf_op jit(solution)/shard_map/all_to_all | solution.py:235
  11.9 9.4 %all-to-all-done = f32[8,128,128]{2,1,0:T(8,128)S(1)} async-done(((f32[8,128,128]{2,1,0:T(8,128)}), f32[8,128,128]{2,1,0:T(8,128)S(1)}, u32[]{:S(2)}, u32[]{:S(2)}) %all-to-all-start) | async-done | bytes 524320 | tf_op jit(solution)/shard_map/all_to_all | solution.py:235
  21.3 1.9 %collective-permute-start = (f32[128,128]{1,0:T(8,128)S(1)}, f32[128,128]{1,0:T(8,128)S(1)}, u32[]{:S(2)}, u32[]{:S(2)}) collective-permute-start(f32[128,128]{1,0:T(8,128)S(1)} %get-tuple-element.5), channel_id=1, source_target_pairs={{0,32},{1,24},{2,40},{3,16},{6,48},{7,8},{4,56},{5,0},{8,41},{9,33... | collective-permute-start | bytes 196616 | tf_op jit(solution)/shard_map/ppermute | solution.py:238
  23.3 5.6 %collective-permute-done = f32[128,128]{1,0:T(8,128)S(1)} collective-permute-done((f32[128,128]{1,0:T(8,128)S(1)}, f32[128,128]{1,0:T(8,128)S(1)}, u32[]{:S(2)}, u32[]{:S(2)}) %collective-permute-start) | collective-permute-done | bytes 65568 | tf_op jit(solution)/shard_map/ppermute | solution.py:238
  28.9 0.1 copy.11
  29.0 0.8 broadcast_in_dim.10
  29.8 5.9 %all-to-all-start.1 = ((f32[8,128,128]{1,2,0:T(8,128)}), f32[8,128,128]{1,2,0:T(8,128)S(1)}, u32[]{:S(2)}, u32[]{:S(2)}) async-start(f32[8,128,128]{1,2,0:T(8,128)} %broadcast_in_dim.10), calls=%async_computation.1 | async-start | bytes 1048576 | tf_op jit(solution)/shard_map/all_to_all | solution.py:27
  35.8 0.1 copy.26
  35.9 14.3 %all-to-all-done.1 = f32[8,128,128]{1,2,0:T(8,128)S(1)} async-done(((f32[8,128,128]{1,2,0:T(8,128)}), f32[8,128,128]{1,2,0:T(8,128)S(1)}, u32[]{:S(2)}, u32[]{:S(2)}) %all-to-all-start.1) | async-done | bytes 524320 | tf_op jit(solution)/shard_map/all_to_all | solution.py:27
  50.2 0.6 convolution_bitcast_fusion.1.gram_ref
  50.8 0.6 convolution_bitcast_fusion.2.part_ref
  51.4 0.1 shared.1
  51.5 1.0 broadcast_in_dim.11
  52.5 7.4 %all-to-all-start.2 = ((f32[8,224,128]{2,1,0:T(8,128)}), f32[8,224,128]{2,1,0:T(8,128)S(1)}, u32[]{:S(2)}, u32[]{:S(2)}) async-start(f32[8,224,128]{2,1,0:T(8,128)} %broadcast_in_dim.11), calls=%async_computation.2 | async-start | bytes 1835008 | tf_op jit(solution)/shard_map/all_to_all | solution.py:27
  59.9 2.0 %collective-permute-start.1 = (f32[128,128]{0,1:T(8,128)S(1)}, f32[128,128]{0,1:T(8,128)S(1)}, u32[]{:S(2)}, u32[]{:S(2)}) collective-permute-start(f32[128,128]{0,1:T(8,128)S(1)} %fusion.2), channel_id=1, source_target_pairs={{1,0},{3,2},{5,4},{7,6},{9,8},{11,10},{13,12},{15,14},{17,16},{19,... | collective-permute-start | bytes 196616 | tf_op jit(solution)/shard_map/ppermute | solution.py:257
  62.0 0.9 collective-permute-done.1
  62.9 5.0 %collective-permute-start.2 = (f32[128,128]{0,1:T(8,128)S(1)}, f32[128,128]{0,1:T(8,128)S(1)}, u32[]{:S(2)}, u32[]{:S(2)}) collective-permute-start(f32[128,128]{0,1:T(8,128)S(1)} %add.36), channel_id=1, source_target_pairs={{0,4},{1,5},{8,12},{9,13},{16,20},{17,21},{24,28},{25,29},{32,36},... | collective-permute-start | bytes 196616 | tf_op jit(solution)/shard_map/ppermute | solution.py:258
  67.9 3.7 %collective-permute-done.2 = f32[128,128]{0,1:T(8,128)S(1)} collective-permute-done((f32[128,128]{0,1:T(8,128)S(1)}, f32[128,128]{0,1:T(8,128)S(1)}, u32[]{:S(2)}, u32[]{:S(2)}) %collective-permute-start.2) | collective-permute-done | bytes 65568 | tf_op jit(solution)/shard_map/ppermute | solution.py:258
  71.6 1.3 collective-permute-start.3
  73.0 6.4 %collective-permute-start.5 = (f32[128,128]{1,0:T(8,128)S(1)}, f32[128,128]{1,0:T(8,128)S(1)}, u32[]{:S(2)}, u32[]{:S(2)}) collective-permute-start(f32[128,128]{1,0:T(8,128)S(1)} %get-tuple-element.6), channel_id=1, source_target_pairs={{0,32},{1,24},{2,40},{3,16},{6,48},{7,8},{4,56},{5,0},{8,41},{9,33... | collective-permute-start | bytes 196616 | tf_op jit(solution)/shard_map/ppermute | solution.py:241
  79.5 1.9 %collective-permute-start.4 = (f32[128,128]{1,0:T(8,128)S(1)}, f32[128,128]{1,0:T(8,128)S(1)}, u32[]{:S(2)}, u32[]{:S(2)}) collective-permute-start(f32[128,128]{1,0:T(8,128)S(1)} %slice.70), channel_id=1, source_target_pairs={{0,32},{1,24},{2,40},{3,16},{6,48},{7,8},{4,56},{5,0},{8,41},{9,33... | collective-permute-start | bytes 196616 | tf_op jit(solution)/shard_map/ppermute | solution.py:248
  81.4 4.0 %shard_map.17 = f32[128,128]{1,0:T(8,128)S(1)} custom-call(f32[64,128]{1,0:T(8,128)S(1)} %slice.67.upper_ref, f32[32,128]{1,0:T(8,128)S(1)} %slice.68.corner_ref), custom_call_target="tpu_custom_call" | custom-call | bytes 30000000 | tf_op jit(solution)/shard_map/pallas_call | solution.py:209
  85.4 0.2 convolution_add_fusion.4.matrix_ref
  85.7 4.1 %shard_map.18 = f32[128,128]{1,0:T(8,128)S(1)} custom-call(f32[128,128]{1,0:T(8,128)S(1)} %convolution_add_fusion.4.matrix_ref), custom_call_target="tpu_custom_call" | custom-call | bytes 30000000 | tf_op jit(solution)/shard_map/pallas_call | solution.py:209
  89.8 0.3 convolution_add_fusion.3
  90.0 0.8 broadcast_in_dim.12
  90.9 3.5 %all-to-all-start.3 = ((f32[8,128,128]{2,1,0:T(8,128)}), f32[8,128,128]{2,1,0:T(8,128)S(1)}, u32[]{:S(2)}, u32[]{:S(2)}) async-start(f32[8,128,128]{2,1,0:T(8,128)} %broadcast_in_dim.12), calls=%async_computation.3 | async-start | bytes 1048576 | tf_op jit(solution)/shard_map/all_to_all | solution.py:27
  94.4 0.3 convolution_add_fusion.5
  94.6 0.3 fusion.17
  94.9 0.3 convolution_add_fusion.2
  95.2 1.0 convolution_add_fusion
  96.2 10.2 %all-to-all-done.3 = f32[8,128,128]{2,1,0:T(8,128)S(1)} async-done(((f32[8,128,128]{2,1,0:T(8,128)}), f32[8,128,128]{2,1,0:T(8,128)S(1)}, u32[]{:S(2)}, u32[]{:S(2)}) %all-to-all-start.3) | async-done | bytes 524320 | tf_op jit(solution)/shard_map/all_to_all | solution.py:27
  106.4 0.6 convolution_bitcast_fusion
  107.0 0.1 fusion.16
  107.1 0.1 maximum_maximum_fusion
  107.2 0.8 broadcast_in_dim.13
  107.9 13.5 %all-to-all-start.4 = ((f32[8,96,128]{2,1,0:T(8,128)}), f32[8,96,128]{2,1,0:T(8,128)S(1)}, u32[]{:S(2)}, u32[]{:S(2)}) async-start(f32[8,96,128]{2,1,0:T(8,128)} %broadcast_in_dim.13), calls=%async_computation.4 | async-start | bytes 786432 | tf_op jit(solution)/shard_map/all_to_all | solution.py:27
  121.4 0.2 fusion.18
  121.6 0.4 convolution_subtract_fusion.1
  122.0 7.1 %all-to-all-done.4 = f32[8,96,128]{2,1,0:T(8,128)S(1)} async-done(((f32[8,96,128]{2,1,0:T(8,128)}), f32[8,96,128]{2,1,0:T(8,128)S(1)}, u32[]{:S(2)}, u32[]{:S(2)}) %all-to-all-start.4) | async-done | bytes 393248 | tf_op jit(solution)/shard_map/all_to_all | solution.py:27
  129.1 0.1 fusion.15
  129.2 0.3 fusion.11
  129.5 0.3 fusion.8
  129.9 0.3 convolution_add_fusion.1
  130.2 0.2 fusion.1
  130.4 0.4 fusion
  130.8 1.1 copy.17
  (21 shorter events, 0.2 us)
Async XLA Ops:
  1.7 19.6 %all-to-all-start = ((f32[8,128,128]{2,1,0:T(8,128)}), f32[8,128,128]{2,1,0:T(8,128)S(1)}, u32[]{:S(2)}, u32[]{:S(2)}) async-start(f32[8,128,128]{2,1,0:T(8,128)} %first_tile.1), calls=%async_computation | async-start | bytes 1048576 | tf_op jit(solution)/shard_map/all_to_all | solution.py:235
  21.3 7.6 %collective-permute-start = (f32[128,128]{1,0:T(8,128)S(1)}, f32[128,128]{1,0:T(8,128)S(1)}, u32[]{:S(2)}, u32[]{:S(2)}) collective-permute-start(f32[128,128]{1,0:T(8,128)S(1)} %get-tuple-element.5), channel_id=1, source_target_pairs={{0,32},{1,24},{2,40},{3,16},{6,48},{7,8},{4,56},{5,0},{8,41},{9,33... | collective-permute-start | bytes 196616 | tf_op jit(solution)/shard_map/ppermute | solution.py:238
  29.8 5.9 %copy-start = (f32[1,128,8,128]{3,2,1,0:T(8,128)S(1)}, f32[1,128,8,128]{3,2,1,0:T(8,128)}, u32[]{:S(2)}) copy-start(f32[1,128,8,128]{3,2,1,0:T(8,128)} %matrix_ref.1) | copy-start | bytes 1572868
  29.8 20.4 %all-to-all-start.1 = ((f32[8,128,128]{1,2,0:T(8,128)}), f32[8,128,128]{1,2,0:T(8,128)S(1)}, u32[]{:S(2)}, u32[]{:S(2)}) async-start(f32[8,128,128]{1,2,0:T(8,128)} %broadcast_in_dim.10), calls=%async_computation.1 | async-start | bytes 1048576 | tf_op jit(solution)/shard_map/all_to_all | solution.py:27
  52.5 26.9 %all-to-all-start.2 = ((f32[8,224,128]{2,1,0:T(8,128)}), f32[8,224,128]{2,1,0:T(8,128)S(1)}, u32[]{:S(2)}, u32[]{:S(2)}) async-start(f32[8,224,128]{2,1,0:T(8,128)} %broadcast_in_dim.11), calls=%async_computation.2 | async-start | bytes 1835008 | tf_op jit(solution)/shard_map/all_to_all | solution.py:27
  59.9 2.9 %collective-permute-start.1 = (f32[128,128]{0,1:T(8,128)S(1)}, f32[128,128]{0,1:T(8,128)S(1)}, u32[]{:S(2)}, u32[]{:S(2)}) collective-permute-start(f32[128,128]{0,1:T(8,128)S(1)} %fusion.2), channel_id=1, source_target_pairs={{1,0},{3,2},{5,4},{7,6},{9,8},{11,10},{13,12},{15,14},{17,16},{19,... | collective-permute-start | bytes 196616 | tf_op jit(solution)/shard_map/ppermute | solution.py:257
  62.9 8.8 %collective-permute-start.2 = (f32[128,128]{0,1:T(8,128)S(1)}, f32[128,128]{0,1:T(8,128)S(1)}, u32[]{:S(2)}, u32[]{:S(2)}) collective-permute-start(f32[128,128]{0,1:T(8,128)S(1)} %add.36), channel_id=1, source_target_pairs={{0,4},{1,5},{8,12},{9,13},{16,20},{17,21},{24,28},{25,29},{32,36},... | collective-permute-start | bytes 196616 | tf_op jit(solution)/shard_map/ppermute | solution.py:258
  71.6 7.7 %collective-permute-start.3 = (f32[128,128]{0,1:T(8,128)S(1)}, f32[128,128]{0,1:T(8,128)S(1)}, u32[]{:S(2)}, u32[]{:S(2)}) collective-permute-start(f32[128,128]{0,1:T(8,128)S(1)} %add.37), channel_id=1, source_target_pairs={{0,2},{4,6},{1,3},{5,7},{8,10},{12,14},{9,11},{13,15},{16,18},{20,... | collective-permute-start | bytes 196616 | tf_op jit(solution)/shard_map/ppermute | solution.py:259
  73.0 16.8 %collective-permute-start.5 = (f32[128,128]{1,0:T(8,128)S(1)}, f32[128,128]{1,0:T(8,128)S(1)}, u32[]{:S(2)}, u32[]{:S(2)}) collective-permute-start(f32[128,128]{1,0:T(8,128)S(1)} %get-tuple-element.6), channel_id=1, source_target_pairs={{0,32},{1,24},{2,40},{3,16},{6,48},{7,8},{4,56},{5,0},{8,41},{9,33... | collective-permute-start | bytes 196616 | tf_op jit(solution)/shard_map/ppermute | solution.py:241
  79.5 10.2 %collective-permute-start.4 = (f32[128,128]{1,0:T(8,128)S(1)}, f32[128,128]{1,0:T(8,128)S(1)}, u32[]{:S(2)}, u32[]{:S(2)}) collective-permute-start(f32[128,128]{1,0:T(8,128)S(1)} %slice.70), channel_id=1, source_target_pairs={{0,32},{1,24},{2,40},{3,16},{6,48},{7,8},{4,56},{5,0},{8,41},{9,33... | collective-permute-start | bytes 196616 | tf_op jit(solution)/shard_map/ppermute | solution.py:248
  90.9 15.6 %all-to-all-start.3 = ((f32[8,128,128]{2,1,0:T(8,128)}), f32[8,128,128]{2,1,0:T(8,128)S(1)}, u32[]{:S(2)}, u32[]{:S(2)}) async-start(f32[8,128,128]{2,1,0:T(8,128)} %broadcast_in_dim.12), calls=%async_computation.3 | async-start | bytes 1048576 | tf_op jit(solution)/shard_map/all_to_all | solution.py:27
  107.9 21.2 %all-to-all-start.4 = ((f32[8,96,128]{2,1,0:T(8,128)}), f32[8,96,128]{2,1,0:T(8,128)S(1)}, u32[]{:S(2)}, u32[]{:S(2)}) async-start(f32[8,96,128]{2,1,0:T(8,128)} %broadcast_in_dim.13), calls=%async_computation.4 | async-start | bytes 786432 | tf_op jit(solution)/shard_map/all_to_all | solution.py:27

commit v9 on v8

--- a/solution.py
+++ b/solution.py
@@ -44,6 +44,9 @@
     take = pltpu.make_async_copy(matrix_ref.at[0, :, 0, :], tile, sem)
     take.start()
     take.wait()
+    spots = lax.axis_index("z") + lax.axis_index("y") + lax.axis_index("x")
+    corner = spots + lax.axis_index("k") == 0
+    tile[...] = jnp.where(corner, 0.0, tile[...])
     copies = [
         pltpu.make_async_copy(tile, out_ref.at[i], sems.at[i])
         for i in range(out_ref.shape[0])
@@ -233,7 +236,7 @@
     identity = unit(width)
 
     first = lax.all_to_all(first_call(matrix, side), COL, 0, 0, tiled=True)
-    panel_row = first[0] * (row != 0).astype(jnp.float32)
+    panel_row = first[0]
     next_row = first[1]
     panel_own = lax.ppermute(panel_row, PLANE, swap)
     near = lax.optimization_barrier(jnp.transpose(local, (1, 0, 2)))

time: 134 us -> 134 us (level)
  blocking collectives: 0 us -> 18.6 us
  starting transfers between devices: 59.2 us -> 50 us
  waiting for transfers between devices: 51.2 us -> 42 us
    all_to_all x0 -> x1, blocking collectives: none -> 18.6 us  [per_device(): first = lax.all_to_all(first_call(matrix, side), COL, 0, 0, tiled=True)]
    all_to_all x1 -> x0, starting transfers between devices: 10.2 us -> none  [per_device(): first = lax.all_to_all(first_call(matrix, side), COL, 0, 0, tiled=True)]
    all_to_all x1 -> x0, waiting for transfers between devices: 9.38 us -> none  [per_device(): first = lax.all_to_all(first_call(matrix, side), COL, 0, 0, tiled=True)]
  transfers between devices with their start and end apart: 11 -> 10, of which waited for: 7 -> 6; matrix products, arithmetic and copies ran while one was open for 2% -> 2% of each run, Pallas kernels for 6% -> 6%
where the time goes in v9:
time: 134 us; the launch traced here: 132 us
  starting transfers between devices  50 us (37%)
  waiting for transfers between devices  42 us (31%)
  blocking collectives  18.6 us (14%)
  Pallas kernels  9.72 us (7%)
  matrix products  6.06 us (5%)
  local copies, waits for them, and re-layouts  4.92 us (4%)
    all_to_all x4, waiting for transfers between devices, spread(): return lax.all_to_all(whole, axis, 0, 0, tiled=True)  32 us
    all_to_all x4, starting transfers between devices, spread(): return lax.all_to_all(whole, axis, 0, 0, tiled=True)  30.8 us
    all_to_all x1, blocking collectives, per_device(): first = lax.all_to_all(first_call(matrix, side), COL, 0, 0, tiled=True)  18.6 us
    pallas_call x2, Pallas kernels, factor_call(): pl.pallas_call(kernel, out_shape=jax.ShapeDtypeStruct((width, width), jnp...  8.05 us
    ppermute x1, starting transfers between devices, per_device(): next_own = lax.ppermute(next_row, PLANE, swap)  6.42 us
    dot_general x16, matrix products, product(): lax.dot_general(left, right, (contract, ((), ())), precision=precision, p...  6.06 us
    ppermute x1, waiting for transfers between devices, per_device(): panel_own = lax.ppermute(panel_row, PLANE, swap)  5.43 us
    ppermute x1, starting transfers between devices, per_device(): head = head + lax.ppermute(head, 'x', [(0, 2)])  5.05 us
  transfers between devices with their start and end apart: 10, of which 6 were waited for; matrix products, arithmetic and copies ran while one was open for 2% of the time, Pallas kernels for 6%

profile of v9, /device:TPU:1, one launch (start us, length us, event | category | flops | bytes accessed | tf_op | source)
XLA Modules:
  0.0 131.8 jit_solution(10292376917958625514)
XLA Ops:
  0.0 1.6 %first_tile.1 = f32[8,128,128]{2,1,0:T(8,128)S(1)} custom-call(f32[1,128,8,128]{3,2,1,0:T(8,128)} %matrix_ref.1), custom_call_target="tpu_custom_call" | custom-call | tf_op jit(solution)/shard_map/first_tile/pallas_call | solution.py:62
  1.6 18.6 %all_to_all.25 = f32[8,128,128]{2,1,0:T(8,128)S(1)} all-to-all(f32[8,128,128]{2,1,0:T(8,128)S(1)} %first_tile.1), channel_id=1, replica_groups=mesh['z'=8,'y'=8,'x'=4,'k'=2] {'x','k'}, dimensions={0} | all-to-all | bytes 1048576 | tf_op jit(solution)/shard_map/all_to_all | solution.py:238
  20.2 2.5 %collective-permute-start = (f32[128,128]{1,0:T(8,128)S(1)}, f32[128,128]{1,0:T(8,128)S(1)}, u32[]{:S(2)}, u32[]{:S(2)}) collective-permute-start(f32[128,128]{1,0:T(8,128)S(1)} %get-tuple-element.5), channel_id=1, source_target_pairs={{0,32},{1,24},{2,40},{3,16},{6,48},{7,8},{4,56},{5,0},{8,41},{9,33... | collective-permute-start | bytes 196616 | tf_op jit(solution)/shard_map/ppermute | solution.py:241
  22.7 5.4 %collective-permute-done = f32[128,128]{1,0:T(8,128)S(1)} collective-permute-done((f32[128,128]{1,0:T(8,128)S(1)}, f32[128,128]{1,0:T(8,128)S(1)}, u32[]{:S(2)}, u32[]{:S(2)}) %collective-permute-start) | collective-permute-done | bytes 65568 | tf_op jit(solution)/shard_map/ppermute | solution.py:241
  28.1 0.8 broadcast_in_dim.10
  28.9 6.4 %all-to-all-start.1 = ((f32[8,128,128]{2,1,0:T(8,128)}), f32[8,128,128]{2,1,0:T(8,128)S(1)}, u32[]{:S(2)}, u32[]{:S(2)}) async-start(f32[8,128,128]{2,1,0:T(8,128)} %broadcast_in_dim.10), calls=%async_computation.1 | async-start | bytes 1048576 | tf_op jit(solution)/shard_map/all_to_all | solution.py:27
  35.3 0.1 copy.19
  35.4 14.3 %all-to-all-done.1 = f32[8,128,128]{2,1,0:T(8,128)S(1)} async-done(((f32[8,128,128]{2,1,0:T(8,128)}), f32[8,128,128]{2,1,0:T(8,128)S(1)}, u32[]{:S(2)}, u32[]{:S(2)}) %all-to-all-start.1) | async-done | bytes 524320 | tf_op jit(solution)/shard_map/all_to_all | solution.py:27
  49.7 1.0 convolution_bitcast_fusion.3.gram_ref
  50.7 0.6 convolution_bitcast_fusion.4.part_ref
  51.4 0.1 shared.1
  51.5 1.0 broadcast_in_dim.11
  52.5 7.5 %all-to-all-start.2 = ((f32[8,224,128]{2,1,0:T(8,128)}), f32[8,224,128]{2,1,0:T(8,128)S(1)}, u32[]{:S(2)}, u32[]{:S(2)}) async-start(f32[8,224,128]{2,1,0:T(8,128)} %broadcast_in_dim.11), calls=%async_computation.2 | async-start | bytes 1835008 | tf_op jit(solution)/shard_map/all_to_all | solution.py:27
  60.0 2.0 %collective-permute-start.1 = (f32[128,128]{1,0:T(8,128)S(1)}, f32[128,128]{1,0:T(8,128)S(1)}, u32[]{:S(2)}, u32[]{:S(2)}) collective-permute-start(f32[128,128]{1,0:T(8,128)S(1)} %fusion.4), channel_id=1, source_target_pairs={{1,0},{3,2},{5,4},{7,6},{9,8},{11,10},{13,12},{15,14},{17,16},{19,... | collective-permute-start | bytes 196616 | tf_op jit(solution)/shard_map/ppermute | solution.py:260
  62.0 0.9 collective-permute-done.1
  62.9 5.1 %collective-permute-start.2 = (f32[128,128]{1,0:T(8,128)S(1)}, f32[128,128]{1,0:T(8,128)S(1)}, u32[]{:S(2)}, u32[]{:S(2)}) collective-permute-start(f32[128,128]{1,0:T(8,128)S(1)} %add.36), channel_id=1, source_target_pairs={{0,4},{1,5},{8,12},{9,13},{16,20},{17,21},{24,28},{25,29},{32,36},... | collective-permute-start | bytes 196616 | tf_op jit(solution)/shard_map/ppermute | solution.py:261
  68.0 3.7 %collective-permute-done.2 = f32[128,128]{1,0:T(8,128)S(1)} collective-permute-done((f32[128,128]{1,0:T(8,128)S(1)}, f32[128,128]{1,0:T(8,128)S(1)}, u32[]{:S(2)}, u32[]{:S(2)}) %collective-permute-start.2) | collective-permute-done | bytes 65568 | tf_op jit(solution)/shard_map/ppermute | solution.py:261
  71.7 1.3 collective-permute-start.3
  73.0 0.1 copy.11
  73.1 6.4 %collective-permute-start.5 = (f32[128,128]{1,0:T(8,128)S(1)}, f32[128,128]{1,0:T(8,128)S(1)}, u32[]{:S(2)}, u32[]{:S(2)}) collective-permute-start(f32[128,128]{1,0:T(8,128)S(1)} %get-tuple-element.6), channel_id=1, source_target_pairs={{0,32},{1,24},{2,40},{3,16},{6,48},{7,8},{4,56},{5,0},{8,41},{9,33... | collective-permute-start | bytes 196616 | tf_op jit(solution)/shard_map/ppermute | solution.py:244
  79.5 0.0 collective-permute-done.3
  79.7 1.9 %collective-permute-start.4 = (f32[128,128]{1,0:T(8,128)S(1)}, f32[128,128]{1,0:T(8,128)S(1)}, u32[]{:S(2)}, u32[]{:S(2)}) collective-permute-start(f32[128,128]{1,0:T(8,128)S(1)} %slice.70), channel_id=1, source_target_pairs={{0,32},{1,24},{2,40},{3,16},{6,48},{7,8},{4,56},{5,0},{8,41},{9,33... | collective-permute-start | bytes 196616 | tf_op jit(solution)/shard_map/ppermute | solution.py:251
  81.6 4.0 %shard_map.17 = f32[128,128]{1,0:T(8,128)S(1)} custom-call(f32[64,128]{1,0:T(8,128)S(1)} %slice.67.upper_ref, f32[32,128]{1,0:T(8,128)S(1)} %slice.68.corner_ref), custom_call_target="tpu_custom_call" | custom-call | bytes 30000000 | tf_op jit(solution)/shard_map/pallas_call | solution.py:212
  85.6 0.3 convolution_add_fusion.3.matrix_ref
  85.8 4.1 %shard_map.18 = f32[128,128]{1,0:T(8,128)S(1)} custom-call(f32[128,128]{1,0:T(8,128)S(1)} %convolution_add_fusion.3.matrix_ref), custom_call_target="tpu_custom_call" | custom-call | bytes 30000000 | tf_op jit(solution)/shard_map/pallas_call | solution.py:212
  89.9 0.3 convolution_add_fusion.2
  90.2 0.8 broadcast_in_dim.12
  91.0 3.5 %all-to-all-start.3 = ((f32[8,128,128]{2,1,0:T(8,128)}), f32[8,128,128]{2,1,0:T(8,128)S(1)}, u32[]{:S(2)}, u32[]{:S(2)}) async-start(f32[8,128,128]{2,1,0:T(8,128)} %broadcast_in_dim.12), calls=%async_computation.3 | async-start | bytes 1048576 | tf_op jit(solution)/shard_map/all_to_all | solution.py:27
  94.6 0.3 fusion.3
  94.8 0.3 fusion.18
  95.1 0.3 convolution_add_fusion.1
  95.4 0.6 fusion
  96.0 10.6 %all-to-all-done.3 = f32[8,128,128]{2,1,0:T(8,128)S(1)} async-done(((f32[8,128,128]{2,1,0:T(8,128)}), f32[8,128,128]{2,1,0:T(8,128)S(1)}, u32[]{:S(2)}, u32[]{:S(2)}) %all-to-all-start.3) | async-done | bytes 524320 | tf_op jit(solution)/shard_map/all_to_all | solution.py:27
  106.6 0.4 convolution_bitcast_fusion.1
  107.0 0.1 fusion.17
  107.1 0.1 maximum_maximum_fusion
  107.1 0.8 broadcast_in_dim.13
  107.9 13.4 %all-to-all-start.4 = ((f32[8,96,128]{2,1,0:T(8,128)}), f32[8,96,128]{2,1,0:T(8,128)S(1)}, u32[]{:S(2)}, u32[]{:S(2)}) async-start(f32[8,96,128]{2,1,0:T(8,128)} %broadcast_in_dim.13), calls=%async_computation.4 | async-start | bytes 786432 | tf_op jit(solution)/shard_map/all_to_all | solution.py:27
  121.3 0.2 fusion.19
  121.5 0.4 convolution_subtract_fusion.1
  121.9 7.1 %all-to-all-done.4 = f32[8,96,128]{2,1,0:T(8,128)S(1)} async-done(((f32[8,96,128]{2,1,0:T(8,128)}), f32[8,96,128]{2,1,0:T(8,128)S(1)}, u32[]{:S(2)}, u32[]{:S(2)}) %all-to-all-start.4) | async-done | bytes 393248 | tf_op jit(solution)/shard_map/all_to_all | solution.py:27
  129.0 0.1 fusion.16
  129.1 0.3 fusion.12
  129.5 0.3 fusion.9
  129.8 0.3 convolution_add_fusion
  130.1 0.2 fusion.2
  130.3 0.4 fusion.1
  130.7 1.1 copy.13
  (20 shorter events, 0.2 us)
Async XLA Ops:
  20.2 7.9 %collective-permute-start = (f32[128,128]{1,0:T(8,128)S(1)}, f32[128,128]{1,0:T(8,128)S(1)}, u32[]{:S(2)}, u32[]{:S(2)}) collective-permute-start(f32[128,128]{1,0:T(8,128)S(1)} %get-tuple-element.5), channel_id=1, source_target_pairs={{0,32},{1,24},{2,40},{3,16},{6,48},{7,8},{4,56},{5,0},{8,41},{9,33... | collective-permute-start | bytes 196616 | tf_op jit(solution)/shard_map/ppermute | solution.py:241
  28.9 6.4 %copy-start = (f32[1,128,8,128]{3,2,1,0:T(8,128)S(1)}, f32[1,128,8,128]{3,2,1,0:T(8,128)}, u32[]{:S(2)}) copy-start(f32[1,128,8,128]{3,2,1,0:T(8,128)} %matrix_ref.1) | copy-start | bytes 1572868
  28.9 20.8 %all-to-all-start.1 = ((f32[8,128,128]{2,1,0:T(8,128)}), f32[8,128,128]{2,1,0:T(8,128)S(1)}, u32[]{:S(2)}, u32[]{:S(2)}) async-start(f32[8,128,128]{2,1,0:T(8,128)} %broadcast_in_dim.10), calls=%async_computation.1 | async-start | bytes 1048576 | tf_op jit(solution)/shard_map/all_to_all | solution.py:27
  52.5 27.1 %all-to-all-start.2 = ((f32[8,224,128]{2,1,0:T(8,128)}), f32[8,224,128]{2,1,0:T(8,128)S(1)}, u32[]{:S(2)}, u32[]{:S(2)}) async-start(f32[8,224,128]{2,1,0:T(8,128)} %broadcast_in_dim.11), calls=%async_computation.2 | async-start | bytes 1835008 | tf_op jit(solution)/shard_map/all_to_all | solution.py:27
  60.0 2.9 %collective-permute-start.1 = (f32[128,128]{1,0:T(8,128)S(1)}, f32[128,128]{1,0:T(8,128)S(1)}, u32[]{:S(2)}, u32[]{:S(2)}) collective-permute-start(f32[128,128]{1,0:T(8,128)S(1)} %fusion.4), channel_id=1, source_target_pairs={{1,0},{3,2},{5,4},{7,6},{9,8},{11,10},{13,12},{15,14},{17,16},{19,... | collective-permute-start | bytes 196616 | tf_op jit(solution)/shard_map/ppermute | solution.py:260
  62.9 8.8 %collective-permute-start.2 = (f32[128,128]{1,0:T(8,128)S(1)}, f32[128,128]{1,0:T(8,128)S(1)}, u32[]{:S(2)}, u32[]{:S(2)}) collective-permute-start(f32[128,128]{1,0:T(8,128)S(1)} %add.36), channel_id=1, source_target_pairs={{0,4},{1,5},{8,12},{9,13},{16,20},{17,21},{24,28},{25,29},{32,36},... | collective-permute-start | bytes 196616 | tf_op jit(solution)/shard_map/ppermute | solution.py:261
  71.7 7.8 %collective-permute-start.3 = (f32[128,128]{1,0:T(8,128)S(1)}, f32[128,128]{1,0:T(8,128)S(1)}, u32[]{:S(2)}, u32[]{:S(2)}) collective-permute-start(f32[128,128]{1,0:T(8,128)S(1)} %add.37), channel_id=1, source_target_pairs={{0,2},{4,6},{1,3},{5,7},{8,10},{12,14},{9,11},{13,15},{16,18},{20,... | collective-permute-start | bytes 196616 | tf_op jit(solution)/shard_map/ppermute | solution.py:262
  73.1 16.8 %collective-permute-start.5 = (f32[128,128]{1,0:T(8,128)S(1)}, f32[128,128]{1,0:T(8,128)S(1)}, u32[]{:S(2)}, u32[]{:S(2)}) collective-permute-start(f32[128,128]{1,0:T(8,128)S(1)} %get-tuple-element.6), channel_id=1, source_target_pairs={{0,32},{1,24},{2,40},{3,16},{6,48},{7,8},{4,56},{5,0},{8,41},{9,33... | collective-permute-start | bytes 196616 | tf_op jit(solution)/shard_map/ppermute | solution.py:244
  79.7 10.3 %collective-permute-start.4 = (f32[128,128]{1,0:T(8,128)S(1)}, f32[128,128]{1,0:T(8,128)S(1)}, u32[]{:S(2)}, u32[]{:S(2)}) collective-permute-start(f32[128,128]{1,0:T(8,128)S(1)} %slice.70), channel_id=1, source_target_pairs={{0,32},{1,24},{2,40},{3,16},{6,48},{7,8},{4,56},{5,0},{8,41},{9,33... | collective-permute-start | bytes 196616 | tf_op jit(solution)/shard_map/ppermute | solution.py:251
  91.0 15.6 %all-to-all-start.3 = ((f32[8,128,128]{2,1,0:T(8,128)}), f32[8,128,128]{2,1,0:T(8,128)S(1)}, u32[]{:S(2)}, u32[]{:S(2)}) async-start(f32[8,128,128]{2,1,0:T(8,128)} %broadcast_in_dim.12), calls=%async_computation.3 | async-start | bytes 1048576 | tf_op jit(solution)/shard_map/all_to_all | solution.py:27
  107.9 21.1 %all-to-all-start.4 = ((f32[8,96,128]{2,1,0:T(8,128)}), f32[8,96,128]{2,1,0:T(8,128)S(1)}, u32[]{:S(2)}, u32[]{:S(2)}) async-start(f32[8,96,128]{2,1,0:T(8,128)} %broadcast_in_dim.13), calls=%async_computation.4 | async-start | bytes 786432 | tf_op jit(solution)/shard_map/all_to_all | solution.py:27

commit v10 on v9

--- a/solution.py
+++ b/solution.py
@@ -281,15 +281,15 @@
     corner = jnp.concatenate([corner[:, :, :half], corner[:, :, half:]], axis=1)
     corner = jnp.sum(corner, axis=0)
     far = turned_row[:, half:]
-    sandwich_row = product(turned_row[:, :half], upper, ((1,), (0,)))
+    sandwich_row = product(turned_row[:, :half], upper, ((1,), (0,)), FAST)
     sandwich_row += jnp.concatenate(
         [
-            product(far, upper[:, half:], ((1,), (1,))),
-            product(far, corner, ((1,), (0,))),
+            product(far, upper[:, half:], ((1,), (1,)), FAST),
+            product(far, corner, ((1,), (0,)), FAST),
         ],
         axis=1,
     )
-    sandwich_row = product(sandwich_row, coupling, ((1,), (0,)))
+    sandwich_row = product(sandwich_row, coupling, ((1,), (0,)), FAST)
     result = partial - product(half_row - sandwich_row, refl, ((1,), (2,)), FAST)
     return result[None]
 

time: 134 us -> 133 us (level)
  no operation moved by 1% of the time
where the time goes in v10:
time: 133 us; the launch traced here: 132 us
  starting transfers between devices  50 us (38%)
  waiting for transfers between devices  42 us (32%)
  blocking collectives  18.6 us (14%)
  Pallas kernels  9.72 us (7%)
  matrix products  5.92 us (4%)
  local copies, waits for them, and re-layouts  4.92 us (4%)
    all_to_all x4, waiting for transfers between devices, spread(): return lax.all_to_all(whole, axis, 0, 0, tiled=True)  32 us
    all_to_all x4, starting transfers between devices, spread(): return lax.all_to_all(whole, axis, 0, 0, tiled=True)  30.8 us
    all_to_all x1, blocking collectives, per_device(): first = lax.all_to_all(first_call(matrix, side), COL, 0, 0, tiled=True)  18.6 us
    pallas_call x2, Pallas kernels, factor_call(): pl.pallas_call(kernel, out_shape=jax.ShapeDtypeStruct((width, width), jnp...  8.05 us
    ppermute x1, starting transfers between devices, per_device(): next_own = lax.ppermute(next_row, PLANE, swap)  6.42 us
    dot_general x16, matrix products, product(): lax.dot_general(left, right, (contract, ((), ())), precision=precision, p...  5.92 us
    ppermute x1, waiting for transfers between devices, per_device(): panel_own = lax.ppermute(panel_row, PLANE, swap)  5.43 us
    ppermute x1, starting transfers between devices, per_device(): head = head + lax.ppermute(head, 'x', [(0, 2)])  5.05 us
  transfers between devices with their start and end apart: 10, of which 6 were waited for; matrix products, arithmetic and copies ran while one was open for 2% of the time, Pallas kernels for 6%

profile of v10, /device:TPU:1, one launch (start us, length us, event | category | flops | bytes accessed | tf_op | source)
XLA Modules:
  0.0 131.6 jit_solution(3402003826928729548)
XLA Ops:
  0.0 1.6 %first_tile.1 = f32[8,128,128]{2,1,0:T(8,128)S(1)} custom-call(f32[1,128,8,128]{3,2,1,0:T(8,128)} %matrix_ref.1), custom_call_target="tpu_custom_call" | custom-call | tf_op jit(solution)/shard_map/first_tile/pallas_call | solution.py:62
  1.6 18.6 %all_to_all.25 = f32[8,128,128]{2,1,0:T(8,128)S(1)} all-to-all(f32[8,128,128]{2,1,0:T(8,128)S(1)} %first_tile.1), channel_id=1, replica_groups=mesh['z'=8,'y'=8,'x'=4,'k'=2] {'x','k'}, dimensions={0} | all-to-all | bytes 1048576 | tf_op jit(solution)/shard_map/all_to_all | solution.py:238
  20.2 2.5 %collective-permute-start = (f32[128,128]{1,0:T(8,128)S(1)}, f32[128,128]{1,0:T(8,128)S(1)}, u32[]{:S(2)}, u32[]{:S(2)}) collective-permute-start(f32[128,128]{1,0:T(8,128)S(1)} %get-tuple-element.5), channel_id=1, source_target_pairs={{0,32},{1,24},{2,40},{3,16},{6,48},{7,8},{4,56},{5,0},{8,41},{9,33... | collective-permute-start | bytes 196616 | tf_op jit(solution)/shard_map/ppermute | solution.py:241
  22.7 5.4 %collective-permute-done = f32[128,128]{1,0:T(8,128)S(1)} collective-permute-done((f32[128,128]{1,0:T(8,128)S(1)}, f32[128,128]{1,0:T(8,128)S(1)}, u32[]{:S(2)}, u32[]{:S(2)}) %collective-permute-start) | collective-permute-done | bytes 65568 | tf_op jit(solution)/shard_map/ppermute | solution.py:241
  28.1 0.8 broadcast_in_dim.10
  28.9 6.4 %all-to-all-start.1 = ((f32[8,128,128]{2,1,0:T(8,128)}), f32[8,128,128]{2,1,0:T(8,128)S(1)}, u32[]{:S(2)}, u32[]{:S(2)}) async-start(f32[8,128,128]{2,1,0:T(8,128)} %broadcast_in_dim.10), calls=%async_computation.1 | async-start | bytes 1048576 | tf_op jit(solution)/shard_map/all_to_all | solution.py:27
  35.3 0.1 copy.19
  35.4 14.3 %all-to-all-done.1 = f32[8,128,128]{2,1,0:T(8,128)S(1)} async-done(((f32[8,128,128]{2,1,0:T(8,128)}), f32[8,128,128]{2,1,0:T(8,128)S(1)}, u32[]{:S(2)}, u32[]{:S(2)}) %all-to-all-start.1) | async-done | bytes 524320 | tf_op jit(solution)/shard_map/all_to_all | solution.py:27
  49.7 1.0 convolution_bitcast_fusion.3.gram_ref
  50.7 0.6 convolution_bitcast_fusion.4.part_ref
  51.4 0.1 shared.1
  51.5 1.0 broadcast_in_dim.11
  52.5 7.5 %all-to-all-start.2 = ((f32[8,224,128]{2,1,0:T(8,128)}), f32[8,224,128]{2,1,0:T(8,128)S(1)}, u32[]{:S(2)}, u32[]{:S(2)}) async-start(f32[8,224,128]{2,1,0:T(8,128)} %broadcast_in_dim.11), calls=%async_computation.2 | async-start | bytes 1835008 | tf_op jit(solution)/shard_map/all_to_all | solution.py:27
  60.0 2.0 %collective-permute-start.1 = (f32[128,128]{1,0:T(8,128)S(1)}, f32[128,128]{1,0:T(8,128)S(1)}, u32[]{:S(2)}, u32[]{:S(2)}) collective-permute-start(f32[128,128]{1,0:T(8,128)S(1)} %fusion.4), channel_id=1, source_target_pairs={{1,0},{3,2},{5,4},{7,6},{9,8},{11,10},{13,12},{15,14},{17,16},{19,... | collective-permute-start | bytes 196616 | tf_op jit(solution)/shard_map/ppermute | solution.py:260
  62.0 0.9 collective-permute-done.1
  62.9 5.1 %collective-permute-start.2 = (f32[128,128]{1,0:T(8,128)S(1)}, f32[128,128]{1,0:T(8,128)S(1)}, u32[]{:S(2)}, u32[]{:S(2)}) collective-permute-start(f32[128,128]{1,0:T(8,128)S(1)} %add.36), channel_id=1, source_target_pairs={{0,4},{1,5},{8,12},{9,13},{16,20},{17,21},{24,28},{25,29},{32,36},... | collective-permute-start | bytes 196616 | tf_op jit(solution)/shard_map/ppermute | solution.py:261
  68.0 3.7 %collective-permute-done.2 = f32[128,128]{1,0:T(8,128)S(1)} collective-permute-done((f32[128,128]{1,0:T(8,128)S(1)}, f32[128,128]{1,0:T(8,128)S(1)}, u32[]{:S(2)}, u32[]{:S(2)}) %collective-permute-start.2) | collective-permute-done | bytes 65568 | tf_op jit(solution)/shard_map/ppermute | solution.py:261
  71.7 1.3 collective-permute-start.3
  73.0 0.1 copy.11
  73.1 6.4 %collective-permute-start.5 = (f32[128,128]{1,0:T(8,128)S(1)}, f32[128,128]{1,0:T(8,128)S(1)}, u32[]{:S(2)}, u32[]{:S(2)}) collective-permute-start(f32[128,128]{1,0:T(8,128)S(1)} %get-tuple-element.6), channel_id=1, source_target_pairs={{0,32},{1,24},{2,40},{3,16},{6,48},{7,8},{4,56},{5,0},{8,41},{9,33... | collective-permute-start | bytes 196616 | tf_op jit(solution)/shard_map/ppermute | solution.py:244
  79.5 0.0 collective-permute-done.3
  79.7 1.9 %collective-permute-start.4 = (f32[128,128]{1,0:T(8,128)S(1)}, f32[128,128]{1,0:T(8,128)S(1)}, u32[]{:S(2)}, u32[]{:S(2)}) collective-permute-start(f32[128,128]{1,0:T(8,128)S(1)} %slice.70), channel_id=1, source_target_pairs={{0,32},{1,24},{2,40},{3,16},{6,48},{7,8},{4,56},{5,0},{8,41},{9,33... | collective-permute-start | bytes 196616 | tf_op jit(solution)/shard_map/ppermute | solution.py:251
  81.6 4.0 %shard_map.17 = f32[128,128]{1,0:T(8,128)S(1)} custom-call(f32[64,128]{1,0:T(8,128)S(1)} %slice.67.upper_ref, f32[32,128]{1,0:T(8,128)S(1)} %slice.68.corner_ref), custom_call_target="tpu_custom_call" | custom-call | bytes 30000000 | tf_op jit(solution)/shard_map/pallas_call | solution.py:212
  85.6 0.3 convolution_add_fusion.3.matrix_ref
  85.8 4.1 %shard_map.18 = f32[128,128]{1,0:T(8,128)S(1)} custom-call(f32[128,128]{1,0:T(8,128)S(1)} %convolution_add_fusion.3.matrix_ref), custom_call_target="tpu_custom_call" | custom-call | bytes 30000000 | tf_op jit(solution)/shard_map/pallas_call | solution.py:212
  89.9 0.3 convolution_add_fusion.2
  90.2 0.8 broadcast_in_dim.12
  91.0 3.5 %all-to-all-start.3 = ((f32[8,128,128]{2,1,0:T(8,128)}), f32[8,128,128]{2,1,0:T(8,128)S(1)}, u32[]{:S(2)}, u32[]{:S(2)}) async-start(f32[8,128,128]{2,1,0:T(8,128)} %broadcast_in_dim.12), calls=%async_computation.3 | async-start | bytes 1048576 | tf_op jit(solution)/shard_map/all_to_all | solution.py:27
  94.6 0.3 fusion.3
  94.8 0.3 fusion.18
  95.1 0.3 convolution_add_fusion.1
  95.4 0.6 fusion
  96.0 10.6 %all-to-all-done.3 = f32[8,128,128]{2,1,0:T(8,128)S(1)} async-done(((f32[8,128,128]{2,1,0:T(8,128)}), f32[8,128,128]{2,1,0:T(8,128)S(1)}, u32[]{:S(2)}, u32[]{:S(2)}) %all-to-all-start.3) | async-done | bytes 524320 | tf_op jit(solution)/shard_map/all_to_all | solution.py:27
  106.6 0.4 convolution_bitcast_fusion.1
  107.0 0.1 fusion.17
  107.1 0.1 maximum_maximum_fusion
  107.1 0.8 broadcast_in_dim.13
  107.9 13.4 %all-to-all-start.4 = ((f32[8,96,128]{2,1,0:T(8,128)}), f32[8,96,128]{2,1,0:T(8,128)S(1)}, u32[]{:S(2)}, u32[]{:S(2)}) async-start(f32[8,96,128]{2,1,0:T(8,128)} %broadcast_in_dim.13), calls=%async_computation.4 | async-start | bytes 786432 | tf_op jit(solution)/shard_map/all_to_all | solution.py:27
  121.3 0.2 fusion.19
  121.5 0.4 convolution_subtract_fusion.1
  121.9 7.1 %all-to-all-done.4 = f32[8,96,128]{2,1,0:T(8,128)S(1)} async-done(((f32[8,96,128]{2,1,0:T(8,128)}), f32[8,96,128]{2,1,0:T(8,128)S(1)}, u32[]{:S(2)}, u32[]{:S(2)}) %all-to-all-start.4) | async-done | bytes 393248 | tf_op jit(solution)/shard_map/all_to_all | solution.py:27
  129.0 0.1 fusion.16
  129.1 0.2 fusion.12
  129.4 0.3 fusion.9
  129.7 0.3 convolution_add_fusion
  130.0 0.2 fusion.2
  130.1 0.4 fusion.1
  130.5 1.1 copy.13
  (20 shorter events, 0.2 us)
Async XLA Ops:
  20.2 7.9 %collective-permute-start = (f32[128,128]{1,0:T(8,128)S(1)}, f32[128,128]{1,0:T(8,128)S(1)}, u32[]{:S(2)}, u32[]{:S(2)}) collective-permute-start(f32[128,128]{1,0:T(8,128)S(1)} %get-tuple-element.5), channel_id=1, source_target_pairs={{0,32},{1,24},{2,40},{3,16},{6,48},{7,8},{4,56},{5,0},{8,41},{9,33... | collective-permute-start | bytes 196616 | tf_op jit(solution)/shard_map/ppermute | solution.py:241
  28.9 6.4 %copy-start = (f32[1,128,8,128]{3,2,1,0:T(8,128)S(1)}, f32[1,128,8,128]{3,2,1,0:T(8,128)}, u32[]{:S(2)}) copy-start(f32[1,128,8,128]{3,2,1,0:T(8,128)} %matrix_ref.1) | copy-start | bytes 1572868
  28.9 20.8 %all-to-all-start.1 = ((f32[8,128,128]{2,1,0:T(8,128)}), f32[8,128,128]{2,1,0:T(8,128)S(1)}, u32[]{:S(2)}, u32[]{:S(2)}) async-start(f32[8,128,128]{2,1,0:T(8,128)} %broadcast_in_dim.10), calls=%async_computation.1 | async-start | bytes 1048576 | tf_op jit(solution)/shard_map/all_to_all | solution.py:27
  52.5 27.1 %all-to-all-start.2 = ((f32[8,224,128]{2,1,0:T(8,128)}), f32[8,224,128]{2,1,0:T(8,128)S(1)}, u32[]{:S(2)}, u32[]{:S(2)}) async-start(f32[8,224,128]{2,1,0:T(8,128)} %broadcast_in_dim.11), calls=%async_computation.2 | async-start | bytes 1835008 | tf_op jit(solution)/shard_map/all_to_all | solution.py:27
  60.0 2.9 %collective-permute-start.1 = (f32[128,128]{1,0:T(8,128)S(1)}, f32[128,128]{1,0:T(8,128)S(1)}, u32[]{:S(2)}, u32[]{:S(2)}) collective-permute-start(f32[128,128]{1,0:T(8,128)S(1)} %fusion.4), channel_id=1, source_target_pairs={{1,0},{3,2},{5,4},{7,6},{9,8},{11,10},{13,12},{15,14},{17,16},{19,... | collective-permute-start | bytes 196616 | tf_op jit(solution)/shard_map/ppermute | solution.py:260
  62.9 8.8 %collective-permute-start.2 = (f32[128,128]{1,0:T(8,128)S(1)}, f32[128,128]{1,0:T(8,128)S(1)}, u32[]{:S(2)}, u32[]{:S(2)}) collective-permute-start(f32[128,128]{1,0:T(8,128)S(1)} %add.36), channel_id=1, source_target_pairs={{0,4},{1,5},{8,12},{9,13},{16,20},{17,21},{24,28},{25,29},{32,36},... | collective-permute-start | bytes 196616 | tf_op jit(solution)/shard_map/ppermute | solution.py:261
  71.7 7.8 %collective-permute-start.3 = (f32[128,128]{1,0:T(8,128)S(1)}, f32[128,128]{1,0:T(8,128)S(1)}, u32[]{:S(2)}, u32[]{:S(2)}) collective-permute-start(f32[128,128]{1,0:T(8,128)S(1)} %add.37), channel_id=1, source_target_pairs={{0,2},{4,6},{1,3},{5,7},{8,10},{12,14},{9,11},{13,15},{16,18},{20,... | collective-permute-start | bytes 196616 | tf_op jit(solution)/shard_map/ppermute | solution.py:262
  73.1 16.8 %collective-permute-start.5 = (f32[128,128]{1,0:T(8,128)S(1)}, f32[128,128]{1,0:T(8,128)S(1)}, u32[]{:S(2)}, u32[]{:S(2)}) collective-permute-start(f32[128,128]{1,0:T(8,128)S(1)} %get-tuple-element.6), channel_id=1, source_target_pairs={{0,32},{1,24},{2,40},{3,16},{6,48},{7,8},{4,56},{5,0},{8,41},{9,33... | collective-permute-start | bytes 196616 | tf_op jit(solution)/shard_map/ppermute | solution.py:244
  79.7 10.3 %collective-permute-start.4 = (f32[128,128]{1,0:T(8,128)S(1)}, f32[128,128]{1,0:T(8,128)S(1)}, u32[]{:S(2)}, u32[]{:S(2)}) collective-permute-start(f32[128,128]{1,0:T(8,128)S(1)} %slice.70), channel_id=1, source_target_pairs={{0,32},{1,24},{2,40},{3,16},{6,48},{7,8},{4,56},{5,0},{8,41},{9,33... | collective-permute-start | bytes 196616 | tf_op jit(solution)/shard_map/ppermute | solution.py:251
  91.0 15.6 %all-to-all-start.3 = ((f32[8,128,128]{2,1,0:T(8,128)}), f32[8,128,128]{2,1,0:T(8,128)S(1)}, u32[]{:S(2)}, u32[]{:S(2)}) async-start(f32[8,128,128]{2,1,0:T(8,128)} %broadcast_in_dim.12), calls=%async_computation.3 | async-start | bytes 1048576 | tf_op jit(solution)/shard_map/all_to_all | solution.py:27
  107.9 21.1 %all-to-all-start.4 = ((f32[8,96,128]{2,1,0:T(8,128)}), f32[8,96,128]{2,1,0:T(8,128)S(1)}, u32[]{:S(2)}, u32[]{:S(2)}) async-start(f32[8,96,128]{2,1,0:T(8,128)} %broadcast_in_dim.13), calls=%async_computation.4 | async-start | bytes 786432 | tf_op jit(solution)/shard_map/all_to_all | solution.py:27
